TPU v7x, 32 devices: a whole 2x2x4 slice. The times are simulated.
32 devices in a mesh: groups: 2 (over x), cx: 16 (over z, y, core).
Axes of the slice: x: 2, y: 2, z: 4, core: 2. Of those that a mesh axis runs over, the one named last changes fastest.
Arguments:
- displacements: bfloat16 [512, 3, 5120], P(('groups', 'cx')), parts along dimension 0, may hold values from -6 to 6
- forces: bfloat16 [512, 3, 5120], P(('groups', 'cx')), parts along dimension 0, may hold values from -6 to 6
- phi: bfloat16 [160, 14, 192, 192], P(('groups', 'cx')), parts along dimension 0, may hold values from -0.125 to 0.125
- neighbours: int32 [80, 14], P('cx'), may hold values from 0 to 79, as said below
- cluster_atoms: int32 [80, 64], P('cx'), may hold values from 0 to 5119, as said below
- config_order: int32 [512], P('groups'), parts along dimension 0, may hold values from 0 to 255, each once
- weights: float32 [512], P('groups'), parts along dimension 0, may hold values from 0.02 to 0.3
Outputs:
- residual: bfloat16 [160, 192, 256], P(('groups', 'cx')), parts along dimension 0
- gradient: bfloat16 [160, 14, 192, 192], P(('groups', 'cx')), parts along dimension 0
There are 2 independent parts, one for each index of `groups`. A program takes and returns all parts, laid end to end along the dimension named above; an argument that names none is the same for every part. Nothing has to cross between parts.
Inputs may be any that keep to these rules, and one draw needn't show every extreme that they name: `neighbours`: cluster c lies in layer c // 5 of 16 periodic layers; its 14 blocks name distinct clusters of its own layer and the two layers beside it, wrapping at the ends. `cluster_atoms`: the clusters of layer j hold the atoms 5 * 64 * j to 5 * 64 * (j + 1) - 1, each once. `config_order`: each ensemble index once.
All inputs are finite; a program needn't handle non-finite values.
Results may differ from a plain program's by a relative error of at most 0.0085.
Values may be sent and summed in bfloat16 or wider, within the bound.
No kernel may reach another device: no remote copies, remote signals or barrier semaphores. Data moves between devices by JAX's collectives and lax.ppermute only.
A program may use at most 128 MiB of HBM per device.

v0:
```python
import jax
import jax.numpy as jnp
from jax import lax
from jax.sharding import PartitionSpec as P

ATOMS = 64
LAYER = 5


def with_halo(block, sides, width):
    for axis, dim in sides:
        count = lax.axis_size(axis)
        forward = [(i, i + 1) for i in range(count - 1)]
        forward.append((count - 1, 0))
        backward = [(target, source) for source, target in forward]
        low = lax.ppermute(
            lax.slice_in_dim(block, block.shape[dim] - width, None, axis=dim), axis, forward
        )
        high = lax.ppermute(lax.slice_in_dim(block, 0, width, axis=dim), axis, backward)
        block = jnp.concatenate([low, block, high], axis=dim)
    return block


def arrange(field, atom_map):
    picked = jnp.take(field, atom_map.reshape(-1), axis=2)
    picked = picked.reshape(field.shape[0], 3, atom_map.shape[0], atom_map.shape[1])
    return jnp.transpose(picked, (2, 1, 3, 0)).reshape(
        atom_map.shape[0], 3 * atom_map.shape[1], field.shape[0]
    )


def shards(displacements, forces, phi, neighbours, cluster_atoms, config_order, weights):
    axis_width = lax.axis_size("cx")
    position = lax.axis_index("cx")
    atom_local = cluster_atoms - position * (LAYER * ATOMS)
    layer_of = neighbours // LAYER
    offset = (layer_of - position + 1 + axis_width) % axis_width
    near_index = offset * LAYER + neighbours % LAYER
    moved_disp, moved_force = (
        lax.all_to_all(displacements, "cx", split_axis=2, concat_axis=0, tiled=True),
        lax.all_to_all(forces, "cx", split_axis=2, concat_axis=0, tiled=True),
    )
    cluster_force = arrange(moved_force, atom_local)
    cluster_disp = arrange(moved_disp, atom_local)
    framed_disp = with_halo(cluster_disp, (("cx", 0),), LAYER)
    beside_disp = jnp.take(framed_disp, near_index, axis=0)
    harmonic = jnp.einsum("ckij,ckjs->cis", phi, beside_disp, preferred_element_type=jnp.float32)
    residual = (cluster_force.astype(jnp.float32) + harmonic).astype(jnp.bfloat16)
    framed_resid = with_halo(residual, (("cx", 0),), LAYER)
    beside_resid = jnp.take(framed_resid, near_index, axis=0)
    match = config_order[:, None] == jnp.arange(config_order.shape[0], dtype=jnp.int32)[None, :]
    weight_row = jnp.sum(
        jnp.where(match, weights[None, :], jnp.zeros_like(weights)[None, :]), axis=1
    )
    wres = (residual.astype(jnp.float32) * weight_row[None, None, :]).astype(jnp.bfloat16)
    wdisp = (cluster_disp.astype(jnp.float32) * weight_row[None, None, :]).astype(jnp.bfloat16)
    first = jnp.einsum("cis,ckjs->ckij", wres, beside_disp, preferred_element_type=jnp.float32)
    second = jnp.einsum("cis,ckjs->ckij", wdisp, beside_resid, preferred_element_type=jnp.float32)
    summed = first + second
    gradient = (0.5 * summed).astype(jnp.bfloat16)
    return (residual, gradient)


def solution(mesh):
    in_specs = (
        P(("groups", "cx"), None, None),
        P(("groups", "cx"), None, None),
        P(("groups", "cx"), None, None, None),
        P("cx", None),
        P("cx", None),
        P("groups"),
        P("groups"),
    )
    out_specs = (P(("groups", "cx"), None, None), P(("groups", "cx"), None, None, None))
    return jax.shard_map(shards, mesh=mesh, in_specs=in_specs, out_specs=out_specs, check_vma=False)
```

profile of v0, /device:TPU:0, one launch (start us, length us, event | category | flops | bytes accessed | tf_op | source)
XLA Modules:
  0.0 138.1 jit_solution(12460175650179497296)
XLA Ops:
  0.6 0.0 copy-start.3
  0.6 0.0 copy-start.2
  0.6 6.5 %copy.46 = bf16[16,3,5120]{0,1,2:T(4,128)(2,1)} copy(bf16[16,3,5120]{2,0,1:T(8,128)(2,1)} %param.11) | data formatting | bytes 983040 | tf_op args[0]
  7.1 8.1 %reshape.93 = bf16[16,2,7680]{2,1,0:T(2,128)(2,1)} reshape(bf16[5120,3,16]{2,1,0:T(4,128)(2,1)} %bitcast.54) | data formatting | bytes 983040
  15.2 7.6 %all-to-all-start.1 = ((bf16[16,2,7680]{2,1,0:T(2,128)(2,1)}), bf16[16,2,7680]{2,1,0:T(2,128)(2,1)S(1)}, u32[]{:S(2)}, u32[]{:S(2)}) async-start(bf16[16,2,7680]{2,1,0:T(2,128)(2,1)} %reshape.93), calls=%async_computation.1 | async-start | bytes 983040 | tf_op jit(solution)/shard_map/all_to_all | solution.py:40
  22.8 0.0 copy-done.3
  22.8 0.1 reshape.33
  22.9 0.0 copy-done.2
  22.9 4.9 %copy.41 = bf16[16,3,5120]{0,1,2:T(4,128)(2,1)} copy(bf16[16,3,5120]{2,0,1:T(8,128)(2,1)S(1)} %copy-done.2) | data formatting | bytes 983040 | tf_op args[1]
  27.8 8.1 %reshape.91 = bf16[16,2,7680]{2,1,0:T(2,128)(2,1)} reshape(bf16[5120,3,16]{2,1,0:T(4,128)(2,1)} %bitcast.55) | data formatting | bytes 983040
  35.9 0.0 copy-done.4
  36.0 0.6 all-to-all-done.1
  36.5 5.5 %all-to-all-start = ((bf16[16,2,7680]{2,1,0:T(2,128)(2,1)}), bf16[16,2,7680]{2,1,0:T(2,128)(2,1)S(1)}, u32[]{:S(2)}, u32[]{:S(2)}) async-start(bf16[16,2,7680]{2,1,0:T(2,128)(2,1)} %reshape.91), calls=%async_computation | async-start | bytes 983040 | tf_op jit(solution)/shard_map/all_to_all | solution.py:41
  42.0 0.1 reshape.80
  42.1 0.0 copy-done.5
  42.1 0.0 copy-done.6
  42.1 0.2 select_reduce_fusion
  42.3 6.4 %reshape.94 = bf16[5120,3,16]{2,1,0:T(4,128)(2,1)} reshape(bf16[16,2,7680]{2,1,0:T(2,128)(2,1)S(1)} %all-to-all-done.1) | data formatting | bytes 983040
  48.7 5.9 %copy.47 = bf16[16,3,16,320]{3,0,2,1:T(8,128)(2,1)S(1)} copy(bf16[16,3,16,320]{0,1,3,2:T(4,128)(2,1)} %bitcast.52) | data formatting | bytes 983040 | tf_op jit(solution)/shard_map/all_to_all | solution.py:40
  54.6 0.7 copy.48
  55.3 2.3 %gather_fusion.1 = bf16[320,256,3]{1,2,0:T(4,128)(2,1)S(1)} fusion(bf16[256,3,320]{0,1,2:T(4,128)(2,1)S(1)} %copy.48, s32[1024]{0:T(1024)S(1)} %pad_clamp_fusion.1), kind=kCustom, calls=%fused_computation.2.clone | custom fusion | bytes 984320 | tf_op jit(solution)/shard_map/jit(_take)/gather | solution.py:25
  57.6 1.1 select_bitcast_fusion
  58.8 0.1 copy.49
  58.9 4.4 %collective-permute-start.1 = (bf16[5,192,256]{2,1,0:T(8,128)(2,1)S(1)}, bf16[5,192,256]{2,1,0:T(8,128)(2,1)}, u32[]{:S(2)}, u32[]{:S(2)}) collective-permute-start(bf16[5,192,256]{2,1,0:T(8,128)(2,1)S(1)} %bitcast.56), channel_id=1, source_target_pairs={{1,0},{2,1},{3,2},{4,3},{5,4},{6,5},{7,6},{8,7},{9,8},{10,9},{11,1... | collective-permute-start | bytes 1474568 | tf_op jit(solution)/shard_map/ppermute | solution.py:19
  63.3 0.0 collective-permute-start
  63.3 0.0 all-to-all-done
  63.3 6.4 %reshape.92 = bf16[5120,3,16]{2,1,0:T(4,128)(2,1)} reshape(bf16[16,2,7680]{2,1,0:T(2,128)(2,1)S(1)} %all-to-all-done) | data formatting | bytes 983040
  69.7 5.9 %copy.42 = bf16[16,3,16,320]{3,0,2,1:T(8,128)(2,1)S(1)} copy(bf16[16,3,16,320]{0,1,3,2:T(4,128)(2,1)} %bitcast.53) | data formatting | bytes 983040 | tf_op jit(solution)/shard_map/all_to_all | solution.py:41
  75.6 0.7 copy.43
  76.3 2.3 %gather_fusion = bf16[320,256,3]{1,2,0:T(4,128)(2,1)S(1)} fusion(bf16[256,3,320]{0,1,2:T(4,128)(2,1)S(1)} %copy.43, s32[1024]{0:T(1024)S(1)} %pad_clamp_fusion.1), kind=kCustom, calls=%fused_computation.clone | custom fusion | bytes 984320 | tf_op jit(solution)/shard_map/jit(_take)/gather | solution.py:25
  78.6 0.1 copy_select_fusion
  78.7 0.1 convert_bitcast_fusion
  78.8 0.1 copy.45
  78.9 0.0 collective-permute-done.1
  78.9 0.0 collective-permute-done
  78.9 1.3 pad_maximum_fusion
  80.3 6.7 %gather_fusion.2 = bf16[70,192,256]{2,1,0:T(8,128)(2,1)} fusion(bf16[15,192,256]{2,1,0:T(8,128)(2,1)S(1)} %pad_maximum_fusion, s32[1024]{0:T(1024)S(1)} %pad_clamp_fusion), kind=kCustom, calls=%fused_computation.1.clone | custom fusion | bytes 13762840 | tf_op jit(solution)/shard_map/jit(_take)/gather | solution.py:46
  87.0 7.2 %fusion.12 = bf16[5,192,256]{2,1,0:T(8,128)(2,1)S(1)} fusion(f32[5,192,256]{2,1,0:T(8,128)S(1)} %bitcast.64, bf16[5,14,192,192]{3,2,1,0:T(8,128)(2,1)} %param.13, bf16[5,14,192,256]{3,2,1,0:T(8,128)(2,1)} %bitcast.50, pred[5,14]{1,0:T(8,128)(4,1)S(1)} %get-tuple-element.14), kind=kOutput, calls=%fused_computation.18 | convolution fusion | flops 1325137920 | bytes 13516870 | tf_op jit(solution)/shard_map/ckij,ckjs->cis/dot_general | solution.py:47
  94.2 0.0 copy-start.1
  94.2 4.5 %collective-permute-start.3 = (bf16[5,192,256]{2,1,0:T(8,128)(2,1)S(1)}, bf16[5,192,256]{2,1,0:T(8,128)(2,1)S(1)}, u32[]{:S(2)}, u32[]{:S(2)}) collective-permute-start(bf16[5,192,256]{2,1,0:T(8,128)(2,1)S(1)} %fusion.12), channel_id=1, source_target_pairs={{1,0},{2,1},{3,2},{4,3},{5,4},{6,5},{7,6},{8,7},{9,8},{10,9},{11,1... | collective-permute-start | bytes 1474568 | tf_op jit(solution)/shard_map/ppermute | solution.py:19
  98.7 0.0 collective-permute-start.2
  98.7 7.0 %fusion.2 = f32[5,14,192,192]{3,2,1,0:T(8,128)} fusion(bf16[5,14,192,256]{3,2,1,0:T(8,128)(2,1)S(1)} %bitcast.51, pred[5,14]{1,0:T(8,128)(4,1)S(1)} %get-tuple-element.14, bf16[5,192,256]{2,1,0:T(8,128)(2,1)S(1)} %fusion.12, f32[256]{0:T(256)S(1)} %select_reduce_fusion), kind=kOutput, calls=%fused_computation.8 | convolution fusion | flops 1325383680 | bytes 17695814 | tf_op jit(solution)/shard_map/cis,ckjs->ckij/dot_general | solution.py:57
  105.7 0.0 collective-permute-done.3
  105.7 4.0 %collective-permute-done.2 = bf16[5,192,256]{2,1,0:T(8,128)(2,1)S(1)} collective-permute-done((bf16[5,192,256]{2,1,0:T(8,128)(2,1)S(1)}, bf16[5,192,256]{2,1,0:T(8,128)(2,1)S(1)}, u32[]{:S(2)}, u32[]{:S(2)}) %collective-permute-start.2) | collective-permute-done | bytes 491552 | tf_op jit(solution)/shard_map/ppermute | solution.py:16
  109.6 0.2 pad_maximum_fusion.1
  109.8 6.7 %gather_fusion.3 = bf16[70,192,256]{2,1,0:T(8,128)(2,1)} fusion(bf16[15,192,256]{2,1,0:T(8,128)(2,1)S(1)} %pad_maximum_fusion.1, s32[1024]{0:T(1024)S(1)} %pad_clamp_fusion), kind=kCustom, calls=%fused_computation.3.clone | custom fusion | bytes 13762840 | tf_op jit(solution)/shard_map/jit(_take)/gather | solution.py:50
  116.5 11.6 %fusion.4 = bf16[5,14,192,192]{2,3,1,0:T(8,128)(2,1)} fusion(f32[5,14,192,192]{3,2,1,0:T(8,128)} %fusion.2, bf16[5,14,192,256]{3,2,1,0:T(8,128)(2,1)} %bitcast.49, pred[5,14]{1,0:T(8,128)(4,1)S(1)} %get-tuple-element.14, bf16[5,192,256]{2,1,0:T(8,128)(2,1)S(1)} %bitcast.59, f32[256]{0:T(256)S(1)} %select_reduce_fusion), kind=kOutput, calls=%fused_computation.10 | convolution fusion | flops 1333125120 | bytes 22856774 | tf_op jit(solution)/shard_map/cis,ckjs->ckij/dot_general | solution.py:58
  128.2 10.0 %copy.51 = bf16[5,14,192,192]{3,2,1,0:T(8,128)(2,1)} copy(bf16[5,14,192,192]{2,3,1,0:T(8,128)(2,1)} %fusion.4) | data formatting | bytes 10321920
  (13 shorter events, 0.1 us)
Async XLA Ops:
  0.6 22.2 %copy-start.3 = (s32[5,64]{1,0:T(8,128)S(1)}, s32[5,64]{1,0:T(8,128)}, u32[]{:S(2)}) copy-start(s32[5,64]{1,0:T(8,128)} %param.15) | copy-start | bytes 3844
  0.6 22.3 %copy-start.2 = (bf16[16,3,5120]{2,0,1:T(8,128)(2,1)S(1)}, bf16[16,3,5120]{2,0,1:T(8,128)(2,1)}, u32[]{:S(2)}) copy-start(bf16[16,3,5120]{2,0,1:T(8,128)(2,1)} %param.12) | copy-start | bytes 1474564
  15.2 20.7 %copy-start.4 = (s32[5,14]{1,0:T(8,128)S(1)}, s32[5,14]{1,0:T(8,128)}, u32[]{:S(2)}) copy-start(s32[5,14]{1,0:T(8,128)} %param.14) | copy-start | bytes 844
  15.2 26.9 %copy-start.5 = (f32[256]{0:T(256)S(1)}, f32[256]{0:T(256)}, u32[]{:S(2)}) copy-start(f32[256]{0:T(256)} %param.17) | copy-start | bytes 3076
  15.2 26.9 %copy-start.6 = (s32[256]{0:T(256)S(1)}, s32[256]{0:T(256)}, u32[]{:S(2)}) copy-start(s32[256]{0:T(256)} %param.16) | copy-start | bytes 3076
  15.2 21.3 %all-to-all-start.1 = ((bf16[16,2,7680]{2,1,0:T(2,128)(2,1)}), bf16[16,2,7680]{2,1,0:T(2,128)(2,1)S(1)}, u32[]{:S(2)}, u32[]{:S(2)}) async-start(bf16[16,2,7680]{2,1,0:T(2,128)(2,1)} %reshape.93), calls=%async_computation.1 | async-start | bytes 983040 | tf_op jit(solution)/shard_map/all_to_all | solution.py:40
  36.5 26.8 %all-to-all-start = ((bf16[16,2,7680]{2,1,0:T(2,128)(2,1)}), bf16[16,2,7680]{2,1,0:T(2,128)(2,1)S(1)}, u32[]{:S(2)}, u32[]{:S(2)}) async-start(bf16[16,2,7680]{2,1,0:T(2,128)(2,1)} %reshape.91), calls=%async_computation | async-start | bytes 983040 | tf_op jit(solution)/shard_map/all_to_all | solution.py:41
  58.9 20.0 %collective-permute-start.1 = (bf16[5,192,256]{2,1,0:T(8,128)(2,1)S(1)}, bf16[5,192,256]{2,1,0:T(8,128)(2,1)}, u32[]{:S(2)}, u32[]{:S(2)}) collective-permute-start(bf16[5,192,256]{2,1,0:T(8,128)(2,1)S(1)} %bitcast.56), channel_id=1, source_target_pairs={{1,0},{2,1},{3,2},{4,3},{5,4},{6,5},{7,6},{8,7},{9,8},{10,9},{11,1... | collective-permute-start | bytes 1474568 | tf_op jit(solution)/shard_map/ppermute | solution.py:19
  63.3 15.6 %collective-permute-start = (bf16[5,192,256]{2,1,0:T(8,128)(2,1)S(1)}, bf16[5,192,256]{2,1,0:T(8,128)(2,1)}, u32[]{:S(2)}, u32[]{:S(2)}) collective-permute-start(bf16[5,192,256]{2,1,0:T(8,128)(2,1)S(1)} %bitcast.57), channel_id=1, source_target_pairs={{0,1},{1,2},{2,3},{3,4},{4,5},{5,6},{6,7},{7,8},{8,9},{9,10},{10,1... | collective-permute-start | bytes 1474568 | tf_op jit(solution)/shard_map/ppermute | solution.py:16
  87.0 11.7 %copy-start = (bf16[70,192,256]{2,1,0:T(8,128)(2,1)S(1)}, bf16[70,192,256]{2,1,0:T(8,128)(2,1)}, u32[]{:S(2)}) copy-start(bf16[70,192,256]{2,1,0:T(8,128)(2,1)} %gather_fusion.2) | copy-start | bytes 20643844
  94.2 15.4 %copy-start.1 = (bf16[5,192,256]{2,1,0:T(8,128)(2,1)}, bf16[5,192,256]{2,1,0:T(8,128)(2,1)S(1)}, u32[]{:S(2)}) copy-start(bf16[5,192,256]{2,1,0:T(8,128)(2,1)S(1)} %fusion.12) | copy-start | bytes 1474564
  94.2 11.5 %collective-permute-start.3 = (bf16[5,192,256]{2,1,0:T(8,128)(2,1)S(1)}, bf16[5,192,256]{2,1,0:T(8,128)(2,1)S(1)}, u32[]{:S(2)}, u32[]{:S(2)}) collective-permute-start(bf16[5,192,256]{2,1,0:T(8,128)(2,1)S(1)} %fusion.12), channel_id=1, source_target_pairs={{1,0},{2,1},{3,2},{4,3},{5,4},{6,5},{7,6},{8,7},{9,8},{10,9},{11,1... | collective-permute-start | bytes 1474568 | tf_op jit(solution)/shard_map/ppermute | solution.py:19
  98.7 11.0 %collective-permute-start.2 = (bf16[5,192,256]{2,1,0:T(8,128)(2,1)S(1)}, bf16[5,192,256]{2,1,0:T(8,128)(2,1)S(1)}, u32[]{:S(2)}, u32[]{:S(2)}) collective-permute-start(bf16[5,192,256]{2,1,0:T(8,128)(2,1)S(1)} %fusion.12), channel_id=1, source_target_pairs={{0,1},{1,2},{2,3},{3,4},{4,5},{5,6},{6,7},{7,8},{8,9},{9,10},{10,1... | collective-permute-start | bytes 1474568 | tf_op jit(solution)/shard_map/ppermute | solution.py:16
where the time goes:
time: 140 us; the launch traced here: 138 us
  local copies, waits for them, and re-layouts  82 us (59%)
  matrix products  25.8 us (18%)
  starting transfers between devices  21.9 us (16%)
  waiting for transfers between devices  4.56 us (3%)
  other arithmetic  3.08 us (2%)
    unnamed x21, local copies, waits for them, and re-layouts  50.4 us
    dot_general x1, matrix products, shards(): jnp.einsum('cis,ckjs->ckij', wdisp, beside_resid, preferred_element_type=...  11.6 us
    ppermute x2, starting transfers between devices, with_halo(): lax.ppermute(lax.slice_in_dim(block, 0, width, axis=dim), axis, backward)  8.87 us
    all_to_all x1, starting transfers between devices, shards(): lax.all_to_all(displacements, 'cx', split_axis=2, concat_axis=0, tiled=True)  7.55 us
    dot_general x1, matrix products, shards(): jnp.einsum('ckij,ckjs->cis', phi, beside_disp, preferred_element_type=jnp...  7.16 us
    dot_general x1, matrix products, shards(): jnp.einsum('cis,ckjs->ckij', wres, beside_disp, preferred_element_type=jn...  6.97 us
    gather x1, local copies, waits for them, and re-layouts, shards(): beside_disp = jnp.take(framed_disp, near_index, axis=0)  6.73 us
    gather x1, local copies, waits for them, and re-layouts, shards(): beside_resid = jnp.take(framed_resid, near_index, axis=0)  6.73 us
  transfers between devices with their start and end apart: 6, of which 2 were waited for; matrix products, arithmetic and copies ran while one was open for 38% of the time, Pallas kernels for 0%

commit v1 on v0

v1 whole, which is shorter than its diff:
```python
import jax
import jax.numpy as jnp
from jax import lax
from jax.experimental import pallas as pl
from jax.experimental.pallas import tpu as pltpu
from jax.sharding import PartitionSpec as P

BF16 = jnp.bfloat16
F32 = jnp.float32
VMEM = pltpu.VMEM
NT = (((1,), (1,)), ((), ()))


def whole(*arrays):
    return [pl.BlockSpec(memory_space=VMEM) for _ in arrays]


def params(**kw):
    return pltpu.CompilerParams(vmem_limit_bytes=48 * 1024 * 1024, **kw)


def cost(flops, nbytes):
    return pl.CostEstimate(flops=flops, bytes_accessed=nbytes, transcendentals=0)


def pack_kernel(disp_ref, force_ref, out1_ref, out2_ref, scratch):
    configs, parts, lanes = disp_ref.shape
    tiles = lanes // 128
    full = tiles // 2
    low = lax.broadcasted_iota(jnp.int32, (configs, 128), 1) < 64
    pieces = []
    for field, ref in enumerate((disp_ref, force_ref)):
        for s in range(configs):
            row = ref[s].astype(F32)
            for t in range(tiles):
                scratch[field, t, pl.ds(8 * s, parts), :] = row[:, 128 * t : 128 * (t + 1)]
    for field in range(2):
        pieces.append(
            [
                [scratch[field, t, pl.ds(a, configs, stride=8), :] for t in range(tiles)]
                for a in range(parts)
            ]
        )
    disp, force = pieces
    for e in range(2):
        first = e * (full + 1)

        def paired(lower, upper, e=e):
            if e == 0:
                return jnp.where(low, lower, pltpu.roll(upper, 64, 1))
            return jnp.where(low, pltpu.roll(lower, 64, 1), upper)

        for a in range(parts):
            for t in range(full):
                out1_ref[e, a * full + t] = disp[a][first + t].astype(BF16)
                out2_ref[e, a * full + t] = force[a][first + t].astype(BF16)
        base = parts * full
        out1_ref[e, base] = paired(disp[0][full], disp[1][full]).astype(BF16)
        out1_ref[e, base + 1] = paired(disp[2][full], force[2][full]).astype(BF16)
        out2_ref[e, base] = paired(force[0][full], force[1][full]).astype(BF16)


def pack(displacements, forces, width):
    configs, parts, atoms = displacements.shape
    per = atoms // width
    full = per // 128
    spec = pl.BlockSpec((configs, parts, 2 * per), lambda i: (0, 0, i))
    sizes = (parts * full + 2, parts * full + 1)
    return pl.pallas_call(
        pack_kernel,
        grid=(width // 2,),
        in_specs=[spec, spec],
        out_specs=[pl.BlockSpec((2, n, configs, 128), lambda i: (i, 0, 0, 0)) for n in sizes],
        out_shape=[jax.ShapeDtypeStruct((width, n, configs, 128), BF16) for n in sizes],
        scratch_shapes=[VMEM((2, 2 * full + 1, 8 * configs, 128), F32)],
        compiler_params=params(),
        cost_estimate=cost(0, 8 * displacements.size),
    )(displacements, forces)


def one_hots(index_ref, full):
    index = index_ref[...]
    rows = index.shape[0]
    lane = lax.broadcasted_iota(jnp.int32, (rows, 128), 1)

    def hot(cond):
        return jnp.where(cond, 1.0, 0.0).astype(BF16)

    wholes = [hot(index - 128 * t == lane) for t in range(full)]
    rest = index - 128 * full
    lower = hot(rest == lane)
    upper = hot((rest >= 0) & (rest + 64 == lane))
    return wholes, lower, upper


def picked(wholes, half_hot, tiles, half):
    total = lax.dot_general(half_hot, half, NT, preferred_element_type=F32)
    for hot, tile in zip(wholes, tiles):
        total = total + lax.dot_general(hot, tile, NT, preferred_element_type=F32)
    return total


def flat(ref, t):
    block = ref[:, t]
    return block.reshape(block.shape[0] * block.shape[1], 128)


def gather_kernel(index_ref, recv_ref, disp_ref, wt_ref, wdisp_ref):
    clusters, dof, _ = disp_ref.shape
    atoms = dof // 3
    full = (recv_ref.shape[1] - 2) // 3
    wholes, lower, upper = one_hots(index_ref, full)
    for a in range(3):
        half_hot = upper if a == 1 else lower
        half = flat(recv_ref, 3 * full + a // 2)
        tiles = [flat(recv_ref, a * full + t) for t in range(full)]
        got = picked(wholes, half_hot, tiles, half)
        for c in range(clusters):
            disp_ref[c, a * atoms : (a + 1) * atoms] = got[c * atoms : (c + 1) * atoms].astype(BF16)


def gather(index, recv, clusters, atoms):
    configs = recv.shape[0] * recv.shape[2]
    return pl.pallas_call(
        lambda i, r, o: gather_kernel(i, r, o, None, None),
        in_specs=whole(index, recv),
        out_specs=pl.BlockSpec(memory_space=VMEM),
        out_shape=jax.ShapeDtypeStruct((clusters, 3 * atoms, configs), BF16),
        compiler_params=params(),
        cost_estimate=cost(2 * recv.size * index.size, 4 * recv.size),
    )(index, recv)


def residual_kernel(index_ref, recv1_ref, recv2_ref, harm_ref, out_ref):
    clusters, dof, _ = out_ref.shape
    atoms = dof // 3
    full = (recv2_ref.shape[1] - 1) // 3
    wholes, lower, upper = one_hots(index_ref, full)
    for a in range(3):
        half_hot = lower if a == 0 else upper
        half = flat(recv1_ref, 3 * full + 1) if a == 2 else flat(recv2_ref, 3 * full)
        tiles = [flat(recv2_ref, a * full + t) for t in range(full)]
        got = picked(wholes, half_hot, tiles, half)
        for c in range(clusters):
            rows = pl.ds(a * atoms, atoms)
            out_ref[c, rows] = (got[c * atoms : (c + 1) * atoms] + harm_ref[c, rows]).astype(BF16)


def residual_of(index, recv1, recv2, harmonic):
    return pl.pallas_call(
        residual_kernel,
        in_specs=whole(index, recv1, recv2, harmonic),
        out_specs=pl.BlockSpec(memory_space=VMEM),
        out_shape=jax.ShapeDtypeStruct(harmonic.shape, BF16),
        compiler_params=params(),
        cost_estimate=cost(2 * recv2.size * index.size, 8 * recv2.size),
    )(index, recv1, recv2, harmonic)


def load_frame(refs, frame, sem):
    layer = refs[0].shape[0]
    copies = [
        pltpu.make_async_copy(ref, frame.at[pl.ds(i * layer, layer)], sem.at[i])
        for i, ref in enumerate(refs)
    ]
    for copy in copies:
        copy.start()
    for copy in copies:
        copy.wait()


def harmonic_kernel(near_ref, phi_ref, low_ref, own_ref, high_ref, out_ref, frame, sem):
    c = pl.program_id(0)

    @pl.when(c == 0)
    def _():
        load_frame((low_ref, own_ref, high_ref), frame, sem)

    total = jnp.zeros(out_ref.shape[1:], F32)
    for k in range(phi_ref.shape[1]):
        total = total + jnp.dot(phi_ref[0, k], frame[near_ref[c, k]], preferred_element_type=F32)
    out_ref[0] = total


def harmonic_of(near, phi, low, own, high):
    clusters, blocks, dof, _ = phi.shape
    configs = own.shape[2]
    raw = pl.BlockSpec(memory_space=pl.ANY)
    return pl.pallas_call(
        harmonic_kernel,
        grid_spec=pltpu.PrefetchScalarGridSpec(
            num_scalar_prefetch=1,
            grid=(clusters,),
            in_specs=[
                pl.BlockSpec((1, blocks, dof, dof), lambda c, near: (c, 0, 0, 0)),
                raw,
                raw,
                raw,
            ],
            out_specs=pl.BlockSpec((1, dof, configs), lambda c, near: (c, 0, 0)),
            scratch_shapes=[
                VMEM((3 * own.shape[0], dof, configs), BF16),
                pltpu.SemaphoreType.DMA((3,)),
            ],
        ),
        out_shape=jax.ShapeDtypeStruct((clusters, dof, configs), F32),
        compiler_params=params(),
        cost_estimate=cost(2 * phi.size * configs, 2 * phi.size + 8 * own.size),
    )(near, phi, low, own, high)


def gradient_kernel(
    near_ref, wt_ref, dlow, down, dhigh, rlow, rown, rhigh, out_ref, disp, resid, sem
):
    c = pl.program_id(0)
    layer = pl.num_programs(0)

    @pl.when(c == 0)
    def _():
        load_frame((dlow, down, dhigh), disp, sem)
        load_frame((rlow, rown, rhigh), resid, sem)

    wt = wt_ref[...]
    wres = (resid[layer + c].astype(F32) * wt).astype(BF16)
    wdisp = (disp[layer + c].astype(F32) * wt).astype(BF16)
    for k in range(out_ref.shape[1]):
        n = near_ref[c, k]
        total = lax.dot_general(wres, disp[n], NT, preferred_element_type=F32)
        total = total + lax.dot_general(wdisp, resid[n], NT, preferred_element_type=F32)
        out_ref[0, k] = (0.5 * total).astype(BF16)


def gradient_of(near, wt, disp, resid):
    clusters, blocks = near.shape
    layer, dof, configs = disp[1].shape
    raw = pl.BlockSpec(memory_space=pl.ANY)
    return pl.pallas_call(
        gradient_kernel,
        grid_spec=pltpu.PrefetchScalarGridSpec(
            num_scalar_prefetch=1,
            grid=(clusters,),
            in_specs=[pl.BlockSpec((1, configs), lambda c, near: (0, 0))] + [raw] * 6,
            out_specs=pl.BlockSpec((1, blocks, dof, dof), lambda c, near: (c, 0, 0, 0)),
            scratch_shapes=[
                VMEM((3 * layer, dof, configs), BF16),
                VMEM((3 * layer, dof, configs), BF16),
                pltpu.SemaphoreType.DMA((3,)),
            ],
        ),
        out_shape=jax.ShapeDtypeStruct((clusters, blocks, dof, dof), BF16),
        compiler_params=params(),
        cost_estimate=cost(
            4 * clusters * blocks * dof * dof * configs, 2 * clusters * blocks * dof * dof
        ),
    )(near, wt, *disp, *resid)


def halo(block):
    count = lax.axis_size("cx")
    forward = [(i, (i + 1) % count) for i in range(count)]
    backward = [(b, a) for a, b in forward]
    return lax.ppermute(block, "cx", forward), lax.ppermute(block, "cx", backward)


def arrange(field, atom_map):
    picked_ = jnp.take(field, atom_map.reshape(-1), axis=2)
    picked_ = picked_.reshape(field.shape[0], 3, atom_map.shape[0], atom_map.shape[1])
    return jnp.transpose(picked_, (2, 1, 3, 0)).reshape(
        atom_map.shape[0], 3 * atom_map.shape[1], field.shape[0]
    )


def shards(displacements, forces, phi, neighbours, cluster_atoms, config_order, weights):
    width = lax.axis_size("cx")
    position = lax.axis_index("cx")
    layer, atoms = cluster_atoms.shape
    per = displacements.shape[2] // width
    offset = (neighbours // layer - position + 1 + width) % width
    near = offset * layer + neighbours % layer
    match = config_order[:, None] == jnp.arange(config_order.shape[0], dtype=jnp.int32)[None, :]
    wt = jnp.sum(jnp.where(match, weights[None, :], 0.0), axis=1)[None, :]
    atom_local = cluster_atoms - position * per
    dense = displacements.shape[0] % 16 == 0 and per % 128 == 64 and width % 2 == 0
    if dense:
        send1, send2 = pack(displacements, forces, width)
        recv1 = lax.all_to_all(send1, "cx", split_axis=0, concat_axis=0, tiled=True)
        recv2 = lax.all_to_all(send2, "cx", split_axis=0, concat_axis=0, tiled=True)
        index = ((atom_local - 64 * (position % 2) + per) % per).reshape(-1, 1)
        disp = gather(index, recv1, layer, atoms)
    else:
        disp, force = (
            arrange(
                lax.all_to_all(x, "cx", split_axis=2, concat_axis=0, tiled=True), atom_local
            )
            for x in (displacements, forces)
        )
    disp_low, disp_high = halo(disp)
    harmonic = harmonic_of(near, phi, disp_low, disp, disp_high)
    if dense:
        residual = residual_of(index, recv1, recv2, harmonic)
    else:
        residual = (force.astype(F32) + harmonic).astype(BF16)
    res_low, res_high = halo(residual)
    gradient = gradient_of(
        near, wt, (disp_low, disp, disp_high), (res_low, residual, res_high)
    )
    return residual, gradient


def solution(mesh):
    both = ("groups", "cx")
    in_specs = (
        P(both, None, None),
        P(both, None, None),
        P(both, None, None, None),
        P("cx", None),
        P("cx", None),
        P("groups"),
        P("groups"),
    )
    out_specs = (P(both, None, None), P(both, None, None, None))
    return jax.shard_map(shards, mesh=mesh, in_specs=in_specs, out_specs=out_specs, check_vma=False)
```

time: 140 us -> 83.9 us (0.60)
  the two profiles are of different devices: /device:TPU:0 before, /device:TPU:1 now
where the time goes in v1:
time: 83.9 us; the launch traced here: 83.4 us
  waiting for transfers between devices  25.9 us (31%)
  blocking collectives  21.1 us (25%)
  Pallas kernels  21 us (25%)
  starting transfers between devices  8.72 us (10%)
  local copies, waits for them, and re-layouts  5.03 us (6%)
  other arithmetic  0.91 us (1%)
    all_to_all x1, blocking collectives, shards(): recv1 = lax.all_to_all(send1, 'cx', split_axis=0, concat_axis=0, tiled=True)  21.1 us
    ppermute x2, waiting for transfers between devices, halo(): lax.ppermute(block, 'cx', backward)  21.1 us
    pallas_call x1, Pallas kernels, gradient_of(): pl.pallas_call(gradient_kernel, grid_spec=pltpu.PrefetchScalarGridSpec(nu...  8.55 us
    pallas_call x1, Pallas kernels, harmonic_of(): pl.pallas_call(harmonic_kernel, grid_spec=pltpu.PrefetchScalarGridSpec(nu...  7.19 us
    unnamed x14, local copies, waits for them, and re-layouts  4.88 us
    ppermute x2, waiting for transfers between devices, halo(): lax.ppermute(block, 'cx', forward)  4.8 us
    all_to_all x1, starting transfers between devices, shards(): recv2 = lax.all_to_all(send2, 'cx', split_axis=0, concat_axis=0, tiled=True)  4.44 us
    pallas_call x1, Pallas kernels, pack(): pl.pallas_call(pack_kernel, grid=(width // 2,), in_specs=[spec, spec], ou...  3.31 us
  transfers between devices with their start and end apart: 5, of which 3 were waited for; matrix products, arithmetic and copies ran while one was open for 1% of the time, Pallas kernels for 9%

profile of v1, /device:TPU:1, one launch (start us, length us, event | category | flops | bytes accessed | tf_op | source)
XLA Modules:
  0.0 83.4 jit_solution(3438912067788518234)
XLA Ops:
  0.6 0.0 copy-start.3
  0.6 1.5 %copy.15.disp_ref = bf16[16,3,5120]{2,1,0:T(4,128)(2,1)S(1)} copy(bf16[16,3,5120]{2,0,1:T(8,128)(2,1)} %param.7) | data formatting | bytes 983040 | tf_op args[0]
  2.1 1.5 %copy.16.force_ref = bf16[16,3,5120]{2,1,0:T(4,128)(2,1)S(1)} copy(bf16[16,3,5120]{2,0,1:T(8,128)(2,1)} %param.8) | data formatting | bytes 983040 | tf_op args[1]
  3.6 3.3 %shard_map.86 = (bf16[16,8,16,128]{3,2,1,0:T(8,128)(2,1)S(1)}, bf16[16,7,16,128]{3,2,1,0:T(8,128)(2,1)}) custom-call(bf16[16,3,5120]{2,1,0:T(4,128)(2,1)S(1)} %copy.15.disp_ref, bf16[16,3,5120]{2,1,0:T(4,128)(2,1)S(1)} %copy.16.force_ref), custom_call_target="tpu_custom_call" | custom-call | bytes 1966080 | tf_op jit(solution)/shard_map/pallas_call | solution.py:69
  6.9 21.1 %all_to_all.10.r.recv1_ref = bf16[16,8,16,128]{3,2,1,0:T(8,128)(2,1)S(1)} all-to-all(bf16[16,8,16,128]{3,2,1,0:T(8,128)(2,1)S(1)} %get-tuple-element.4), channel_id=1, replica_groups=mesh['groups'=2,'cx'=16] {'cx'}, dimensions={0} | all-to-all | bytes 1048576 | tf_op jit(solution)/shard_map/all_to_all | solution.py:286
  28.0 4.4 %all-to-all-start.1 = ((bf16[16,7,16,128]{3,2,1,0:T(8,128)(2,1)}), bf16[16,7,16,128]{3,2,1,0:T(8,128)(2,1)S(1)}, u32[]{:S(2)}, u32[]{:S(2)}) async-start(bf16[16,7,16,128]{3,2,1,0:T(8,128)(2,1)} %get-tuple-element.5), calls=%async_computation.1 | async-start | bytes 917504 | tf_op jit(solution)/shard_map/all_to_all | solution.py:287
  32.4 0.0 copy-start.4
  32.4 0.0 copy-start.5
  32.5 0.7 add_select_fusion.3
  33.2 0.1 reshape.10.i.index_ref
  33.3 0.0 copy-start.1
  33.3 0.6 shard_map.87.own_ref.down
  33.9 0.1 collective-permute-start.1
  34.1 1.7 %collective-permute-start = (bf16[5,192,256]{2,1,0:T(8,128)(2,1)S(1)}, bf16[5,192,256]{2,1,0:T(8,128)(2,1)S(1)}, u32[]{:S(2)}, u32[]{:S(2)}) collective-permute-start(bf16[5,192,256]{2,1,0:T(8,128)(2,1)S(1)} %shard_map.87.own_ref.down), channel_id=1, source_target_pairs={{0,1},{1,2},{2,3},{3,4},{4,5},{5,6},{6,7},{7,8},{8,9},{9,10},{10,1... | collective-permute-start | bytes 1474568 | tf_op jit(solution)/shard_map/ppermute | solution.py:262
  35.7 0.0 copy-done.3
  35.8 9.3 %collective-permute-done.1.high_ref.dhigh = bf16[5,192,256]{2,1,0:T(8,128)(2,1)S(1)} collective-permute-done((bf16[5,192,256]{2,1,0:T(8,128)(2,1)S(1)}, bf16[5,192,256]{2,1,0:T(8,128)(2,1)S(1)}, u32[]{:S(2)}, u32[]{:S(2)}) %collective-permute-start.1) | collective-permute-done | bytes 491552 | tf_op jit(solution)/shard_map/ppermute | solution.py:262
  45.1 0.0 copy-done.1
  45.1 4.8 %collective-permute-done.low_ref.dlow = bf16[5,192,256]{2,1,0:T(8,128)(2,1)S(1)} collective-permute-done((bf16[5,192,256]{2,1,0:T(8,128)(2,1)S(1)}, bf16[5,192,256]{2,1,0:T(8,128)(2,1)S(1)}, u32[]{:S(2)}, u32[]{:S(2)}) %collective-permute-start) | collective-permute-done | bytes 491552 | tf_op jit(solution)/shard_map/ppermute | solution.py:262
  49.9 7.2 %shard_map.88.harm_ref = f32[5,192,256]{2,1,0:T(8,128)S(1)} custom-call(s32[5,14]{1,0:T(8,128)S(1)} %fusion.4.near_ref, bf16[5,14,192,192]{3,2,1,0:T(8,128)(2,1)} %phi_ref.1, bf16[5,192,256]{2,1,0:T(8,128)(2,1)S(1)} %collective-permute-done.low_ref.dlow, bf16[5,192,256]{2,1,0:T(8,128)(2,1)S(1)} %shard_map.87.own_ref.down, ...), custom_call_target="tpu_custom_call" | custom-call | flops 1321205760 | bytes 7127040 | tf_op jit(solution)/shard_map/pallas_call | solution.py:189
  57.1 0.0 all-to-all-done.1.recv2_ref
  57.1 0.0 copy-start.2
  57.1 0.9 %copy-done.2 = s32[320,1]{1,0:T(8,128)S(1)} copy-done((s32[320,1]{1,0:T(8,128)S(1)}, s32[320,1]{1,0:T(8,128)}, u32[]{:S(2)}) %copy-start.2) | copy-done | bytes 1304
  58.0 1.4 %shard_map.89.rown = bf16[5,192,256]{2,1,0:T(8,128)(2,1)} custom-call(s32[320,1]{1,0:T(8,128)S(1)} %copy-done.2, bf16[16,8,16,128]{3,2,1,0:T(8,128)(2,1)S(1)} %all_to_all.10.r.recv1_ref, bf16[16,7,16,128]{3,2,1,0:T(8,128)(2,1)S(1)} %all-to-all-done.1.recv2_ref, f32[5,192,256]{2,1,0:T(8,128)S(1)} %shard_map.88.harm_ref), custom_call_target="tpu_custom_call" | custom-call | flops 146800640 | bytes 1835008 | tf_op jit(solution)/shard_map/pallas_call | solution.py:150
  59.4 1.2 %collective-permute-start.3 = (bf16[5,192,256]{2,1,0:T(8,128)(2,1)}, bf16[5,192,256]{2,1,0:T(8,128)(2,1)S(1)}, u32[]{:S(2)}, u32[]{:S(2)}) collective-permute-start(bf16[5,192,256]{2,1,0:T(8,128)(2,1)} %shard_map.89.rown), channel_id=1, source_target_pairs={{1,0},{2,1},{3,2},{4,3},{5,4},{6,5},{7,6},{8,7},{9,8},{10,9},{11,1... | collective-permute-start | bytes 1474568 | tf_op jit(solution)/shard_map/ppermute | solution.py:262
  60.5 1.3 %collective-permute-start.2 = (bf16[5,192,256]{2,1,0:T(8,128)(2,1)}, bf16[5,192,256]{2,1,0:T(8,128)(2,1)S(1)}, u32[]{:S(2)}, u32[]{:S(2)}) collective-permute-start(bf16[5,192,256]{2,1,0:T(8,128)(2,1)} %shard_map.89.rown), channel_id=1, source_target_pairs={{0,1},{1,2},{2,3},{3,4},{4,5},{5,6},{6,7},{7,8},{8,9},{9,10},{10,1... | collective-permute-start | bytes 1474568 | tf_op jit(solution)/shard_map/ppermute | solution.py:262
  61.8 0.0 copy-done.4
  61.8 0.0 copy-done.5
  61.8 0.2 select_reduce_fusion
  62.0 11.8 %collective-permute-done.3.rhigh = bf16[5,192,256]{2,1,0:T(8,128)(2,1)S(1)} collective-permute-done((bf16[5,192,256]{2,1,0:T(8,128)(2,1)}, bf16[5,192,256]{2,1,0:T(8,128)(2,1)S(1)}, u32[]{:S(2)}, u32[]{:S(2)}) %collective-permute-start.3) | collective-permute-done | bytes 491552 | tf_op jit(solution)/shard_map/ppermute | solution.py:262
  73.8 0.0 collective-permute-done.2.rlow
  73.8 0.0 copy-start
  73.8 1.0 %copy-done = bf16[5,192,256]{2,1,0:T(8,128)(2,1)S(1)} copy-done((bf16[5,192,256]{2,1,0:T(8,128)(2,1)S(1)}, bf16[5,192,256]{2,1,0:T(8,128)(2,1)}, u32[]{:S(2)}) %copy-start) | copy-done | bytes 491544
  74.9 8.5 %shard_map.90 = bf16[5,14,192,192]{3,2,1,0:T(8,128)(2,1)} custom-call(s32[5,14]{1,0:T(8,128)S(1)} %fusion.4.near_ref, f32[1,256]{1,0:T(1,128)S(1)} %bitcast.1, bf16[5,192,256]{2,1,0:T(8,128)(2,1)S(1)} %collective-permute-done.low_ref.dlow, bf16[5,192,256]{2,1,0:T(8,128)(2,1)S(1)} %shard_map.87.own_ref.down, ...), custom_call_target="tpu_custom_call" | custom-call | flops 2642411520 | bytes 5160960 | tf_op jit(solution)/shard_map/pallas_call | solution.py:237
  (1 shorter events, 0.0 us)
Async XLA Ops:
  0.6 35.1 %copy-start.3 = (s32[5,14]{1,0:T(8,128)S(1)}, s32[5,14]{1,0:T(8,128)}, u32[]{:S(2)}) copy-start(s32[5,14]{1,0:T(8,128)} %param.10) | copy-start | bytes 844
  28.0 29.1 %all-to-all-start.1 = ((bf16[16,7,16,128]{3,2,1,0:T(8,128)(2,1)}), bf16[16,7,16,128]{3,2,1,0:T(8,128)(2,1)S(1)}, u32[]{:S(2)}, u32[]{:S(2)}) async-start(bf16[16,7,16,128]{3,2,1,0:T(8,128)(2,1)} %get-tuple-element.5), calls=%async_computation.1 | async-start | bytes 917504 | tf_op jit(solution)/shard_map/all_to_all | solution.py:287
  32.4 29.4 %copy-start.4 = (f32[256]{0:T(256)S(1)}, f32[256]{0:T(256)}, u32[]{:S(2)}) copy-start(f32[256]{0:T(256)} %param.13) | copy-start | bytes 3076
  32.4 29.4 %copy-start.5 = (s32[256]{0:T(256)S(1)}, s32[256]{0:T(256)}, u32[]{:S(2)}) copy-start(s32[256]{0:T(256)} %param.12) | copy-start | bytes 3076
  33.3 11.7 %copy-start.1 = (s32[320,1]{1,0:T(8,128)}, s32[320,1]{1,0:T(8,128)S(1)}, u32[]{:S(2)}) copy-start(s32[320,1]{1,0:T(8,128)S(1)} %reshape.10.i.index_ref) | copy-start | bytes 3844
  33.9 11.1 %collective-permute-start.1 = (bf16[5,192,256]{2,1,0:T(8,128)(2,1)S(1)}, bf16[5,192,256]{2,1,0:T(8,128)(2,1)S(1)}, u32[]{:S(2)}, u32[]{:S(2)}) collective-permute-start(bf16[5,192,256]{2,1,0:T(8,128)(2,1)S(1)} %shard_map.87.own_ref.down), channel_id=1, source_target_pairs={{1,0},{2,1},{3,2},{4,3},{5,4},{6,5},{7,6},{8,7},{9,8},{10,9},{11,1... | collective-permute-start | bytes 1474568 | tf_op jit(solution)/shard_map/ppermute | solution.py:262
  34.1 15.8 %collective-permute-start = (bf16[5,192,256]{2,1,0:T(8,128)(2,1)S(1)}, bf16[5,192,256]{2,1,0:T(8,128)(2,1)S(1)}, u32[]{:S(2)}, u32[]{:S(2)}) collective-permute-start(bf16[5,192,256]{2,1,0:T(8,128)(2,1)S(1)} %shard_map.87.own_ref.down), channel_id=1, source_target_pairs={{0,1},{1,2},{2,3},{3,4},{4,5},{5,6},{6,7},{7,8},{8,9},{9,10},{10,1... | collective-permute-start | bytes 1474568 | tf_op jit(solution)/shard_map/ppermute | solution.py:262
  57.1 0.9 %copy-start.2 = (s32[320,1]{1,0:T(8,128)S(1)}, s32[320,1]{1,0:T(8,128)}, u32[]{:S(2)}) copy-start(s32[320,1]{1,0:T(8,128)} %copy-done.1) | copy-start | bytes 3844
  59.4 14.5 %collective-permute-start.3 = (bf16[5,192,256]{2,1,0:T(8,128)(2,1)}, bf16[5,192,256]{2,1,0:T(8,128)(2,1)S(1)}, u32[]{:S(2)}, u32[]{:S(2)}) collective-permute-start(bf16[5,192,256]{2,1,0:T(8,128)(2,1)} %shard_map.89.rown), channel_id=1, source_target_pairs={{1,0},{2,1},{3,2},{4,3},{5,4},{6,5},{7,6},{8,7},{9,8},{10,9},{11,1... | collective-permute-start | bytes 1474568 | tf_op jit(solution)/shard_map/ppermute | solution.py:262
  60.5 13.3 %collective-permute-start.2 = (bf16[5,192,256]{2,1,0:T(8,128)(2,1)}, bf16[5,192,256]{2,1,0:T(8,128)(2,1)S(1)}, u32[]{:S(2)}, u32[]{:S(2)}) collective-permute-start(bf16[5,192,256]{2,1,0:T(8,128)(2,1)} %shard_map.89.rown), channel_id=1, source_target_pairs={{0,1},{1,2},{2,3},{3,4},{4,5},{5,6},{6,7},{7,8},{8,9},{9,10},{10,1... | collective-permute-start | bytes 1474568 | tf_op jit(solution)/shard_map/ppermute | solution.py:262
  73.8 1.0 %copy-start = (bf16[5,192,256]{2,1,0:T(8,128)(2,1)S(1)}, bf16[5,192,256]{2,1,0:T(8,128)(2,1)}, u32[]{:S(2)}) copy-start(bf16[5,192,256]{2,1,0:T(8,128)(2,1)} %shard_map.89.rown) | copy-start | bytes 1474564

commit v2 on v0

v2 whole, which is shorter than its diff:
```python
import jax
import jax.numpy as jnp
from jax import lax
from jax.experimental import pallas as pl
from jax.experimental.pallas import tpu as pltpu
from jax.sharding import PartitionSpec as P

BF16 = jnp.bfloat16
F32 = jnp.float32
VMEM = pltpu.VMEM
SMEM = pltpu.SMEM
NT = (((1,), (1,)), ((), ()))
MIB = 1024 * 1024


def in_vmem(count):
    return [pl.BlockSpec(memory_space=VMEM)] * count


def in_smem():
    return pl.BlockSpec(memory_space=SMEM)


def in_place():
    return pl.BlockSpec(memory_space=pl.ANY)


def params(mib, **kw):
    return pltpu.CompilerParams(vmem_limit_bytes=mib * MIB, **kw)


def cost(flops, nbytes):
    return pl.CostEstimate(flops=flops, bytes_accessed=nbytes, transcendentals=0)


def shape(dims, dtype=BF16):
    return jax.ShapeDtypeStruct(dims, dtype)


def pack_kernel(disp_ref, force_ref, out1_ref, out2_ref):
    parts, configs, lanes = disp_ref.shape
    tiles = 2 * lanes // 128 // out1_ref.shape[0]
    full = tiles // 2
    low = lax.broadcasted_iota(jnp.int32, (configs, 128), 1) < 64
    for pair in range(out1_ref.shape[0] // 2):

        def tile(ref, a, t, pair=pair):
            return ref[a, :, pl.ds(128 * (pair * tiles + t), 128)]

        for e in range(2):
            first = e * (full + 1)

            def paired(ref0, a0, ref1, a1, e=e, tile=tile):
                x, y = tile(ref0, a0, full).astype(F32), tile(ref1, a1, full).astype(F32)
                if e == 0:
                    y = pltpu.roll(y, 64, 1)
                else:
                    x = pltpu.roll(x, 64, 1)
                return jnp.where(low, x, y).astype(BF16)

            dest = 2 * pair + e
            for a in range(parts):
                for t in range(full):
                    out1_ref[dest, a * full + t] = tile(disp_ref, a, first + t)
                    out2_ref[dest, a * full + t] = tile(force_ref, a, first + t)
            base = parts * full
            out1_ref[dest, base] = paired(disp_ref, 0, disp_ref, 1)
            out1_ref[dest, base + 1] = paired(disp_ref, 2, force_ref, 2)
            out2_ref[dest, base] = paired(force_ref, 0, force_ref, 1)


def pack(displacements, forces, width):
    parts, configs, atoms = displacements.shape
    per = atoms // width
    full = per // 128
    steps = 4 if width % 8 == 0 else width // 2
    group = width // steps
    spec = pl.BlockSpec((parts, configs, group * per), lambda i: (0, 0, i))
    sizes = (parts * full + 2, parts * full + 1)
    return pl.pallas_call(
        pack_kernel,
        grid=(steps,),
        in_specs=[spec, spec],
        out_specs=[pl.BlockSpec((group, n, configs, 128), lambda i: (i, 0, 0, 0)) for n in sizes],
        out_shape=[shape((width, n, configs, 128)) for n in sizes],
        compiler_params=params(8),
        cost_estimate=cost(0, 8 * displacements.size),
    )(displacements, forces)


def one_hots(index_ref, full):
    index = index_ref[...]
    rows = index.shape[0]
    lane = lax.broadcasted_iota(jnp.int32, (rows, 128), 1)

    def hot(cond):
        return jnp.where(cond, 1.0, 0.0).astype(BF16)

    wholes = [hot(index - 128 * t == lane) for t in range(full)]
    rest = index - 128 * full
    lower = hot(rest == lane)
    upper = hot((rest >= 0) & (rest + 64 == lane))
    return wholes, lower, upper


def picked(wholes, half_hot, tiles, half):
    total = lax.dot_general(half_hot, half, NT, preferred_element_type=F32)
    for hot, tile in zip(wholes, tiles):
        total = total + lax.dot_general(hot, tile, NT, preferred_element_type=F32)
    return total


def flat(ref, t):
    block = ref[:, t]
    return block.reshape(block.shape[0] * block.shape[1], 128)


def gather_kernel(index_ref, recv_ref, disp_ref):
    clusters, dof, _ = disp_ref.shape
    atoms = dof // 3
    full = (recv_ref.shape[1] - 2) // 3
    wholes, lower, upper = one_hots(index_ref, full)
    for a in range(3):
        half_hot = upper if a == 1 else lower
        half = flat(recv_ref, 3 * full + a // 2)
        tiles = [flat(recv_ref, a * full + t) for t in range(full)]
        got = picked(wholes, half_hot, tiles, half)
        for c in range(clusters):
            disp_ref[c, a * atoms : (a + 1) * atoms] = got[c * atoms : (c + 1) * atoms].astype(BF16)


def gather(index, recv, clusters, atoms):
    configs = recv.shape[0] * recv.shape[2]
    return pl.pallas_call(
        gather_kernel,
        in_specs=in_vmem(2),
        out_specs=in_vmem(1)[0],
        out_shape=shape((clusters, 3 * atoms, configs)),
        compiler_params=params(8),
        cost_estimate=cost(2 * recv.size * index.size, 4 * recv.size),
    )(index, recv)


def add_force_kernel(index_ref, recv1_ref, recv2_ref, harm_ref, out_ref):
    clusters, dof, _ = out_ref.shape
    atoms = dof // 3
    full = (recv2_ref.shape[1] - 1) // 3
    wholes, lower, upper = one_hots(index_ref, full)
    for a in range(3):
        half_hot = lower if a == 0 else upper
        half = flat(recv1_ref, 3 * full + 1) if a == 2 else flat(recv2_ref, 3 * full)
        tiles = [flat(recv2_ref, a * full + t) for t in range(full)]
        got = picked(wholes, half_hot, tiles, half)
        for c in range(clusters):
            rows = pl.ds(a * atoms, atoms)
            out_ref[c, rows] = got[c * atoms : (c + 1) * atoms] + harm_ref[c, rows]


def add_force(index, recv1, recv2, harmonic):
    return pl.pallas_call(
        add_force_kernel,
        in_specs=in_vmem(4),
        out_specs=in_vmem(1)[0],
        out_shape=shape(harmonic.shape, F32),
        compiler_params=params(8),
        cost_estimate=cost(2 * recv2.size * index.size, 8 * recv2.size),
    )(index, recv1, recv2, harmonic)


def blocks_for(block_ref, phi_ref, n):
    clusters, blocks = phi_ref.shape[:2]
    rows = []
    for c in range(clusters):
        k = block_ref[c, n]
        block = phi_ref[c, jnp.minimum(k, blocks - 1)]
        rows.append(jnp.where(k < blocks, block, jnp.zeros_like(block)))
    return jnp.concatenate(rows, axis=0)


def near_harmonic_kernel(block_ref, phi_ref, own_ref, partner_ref, out_ref):
    clusters, dof, configs = out_ref.shape
    layer = own_ref.shape[0]
    for n in range(2 * layer):
        disp = own_ref[n] if n < layer else partner_ref[n - layer]
        got = jnp.dot(blocks_for(block_ref, phi_ref, n), disp, preferred_element_type=F32)
        got = got.reshape(out_ref.shape)
        out_ref[...] = got if n == 0 else out_ref[...] + got


def near_harmonic(block_of, phi, own, partner):
    clusters, blocks, dof, _ = phi.shape
    configs = own.shape[2]
    return pl.pallas_call(
        near_harmonic_kernel,
        in_specs=[in_smem()] + in_vmem(3),
        out_specs=in_vmem(1)[0],
        out_shape=shape((clusters, dof, configs), F32),
        compiler_params=params(12),
        cost_estimate=cost(4 * phi.size * configs // 3, 4 * phi.size // 3),
    )(block_of, phi, own, partner)


def residual_kernel(
    block_ref, phi_ref, far_ref, base_ref, own_ref, wt_ref, out_ref, res_ref, left_ref, total
):
    clusters, dof, configs = out_ref.shape
    layer = far_ref.shape[0]
    for n in range(layer):
        left = blocks_for(block_ref, phi_ref, 2 * layer + n)
        got = jnp.dot(left, far_ref[n], preferred_element_type=F32).reshape(out_ref.shape)
        total[...] = (base_ref[...] if n == 0 else total[...]) + got
    wt = 0.5 * wt_ref[...]
    for c in range(clusters):
        res = total[c].astype(BF16)
        out_ref[c] = res
        res_ref[c] = res
        left_ref[c, :, :configs] = (res.astype(F32) * wt).astype(BF16)
        left_ref[c, :, configs:] = (own_ref[c].astype(F32) * wt).astype(BF16)


def residual_of(block_of, phi, far, base, own, wt):
    clusters, blocks, dof, _ = phi.shape
    configs = own.shape[2]
    return pl.pallas_call(
        residual_kernel,
        in_specs=[in_smem()] + in_vmem(5),
        out_specs=in_vmem(3),
        out_shape=[
            shape((clusters, dof, configs)),
            shape((clusters, dof, configs)),
            shape((clusters, dof, 2 * configs)),
        ],
        scratch_shapes=[VMEM((clusters, dof, configs), F32)],
        compiler_params=params(12),
        cost_estimate=cost(2 * phi.size * configs // 3, 2 * phi.size // 3),
    )(block_of, phi, far, base, own, wt)


def gradient_part(block_ref, left_ref, pairs, out_ref, held, sem, first):
    clusters, blocks, dof, _ = out_ref.shape
    width = left_ref.shape[2]
    left = left_ref[...].reshape(clusters * dof, width)

    def placed(i, c):
        k = block_ref[c, first + i]
        copy = pltpu.make_async_copy(
            held.at[i, c], out_ref.at[c, jnp.minimum(k, blocks - 1)], sem.at[i, c]
        )
        return k < blocks, copy

    for i, (disp_ref, res_ref, n) in enumerate(pairs):
        right = jnp.concatenate([disp_ref[n], res_ref[n]], axis=1)
        got = lax.dot_general(left, right, NT, preferred_element_type=F32)
        held[i] = got.astype(BF16).reshape(held.shape[1:])
        for c in range(clusters):
            there, copy = placed(i, c)
            pl.when(there)(copy.start)
    for i in range(len(pairs)):
        for c in range(clusters):
            there, copy = placed(i, c)
            pl.when(there)(copy.wait)


def near_gradient_kernel(block_ref, left_ref, down, dpart, rown, rpart, out_ref, held, sem):
    layer = down.shape[0]
    pairs = [(down, rown, n) for n in range(layer)] + [(dpart, rpart, n) for n in range(layer)]
    gradient_part(block_ref, left_ref, pairs, out_ref, held, sem, 0)


def far_gradient_kernel(block_ref, left_ref, dfar, rfar, prior_ref, out_ref, held, sem):
    layer = dfar.shape[0]
    pairs = [(dfar, rfar, n) for n in range(layer)]
    gradient_part(block_ref, left_ref, pairs, out_ref, held, sem, 2 * layer)


def gradient_call(kernel, layers, block_of, left, fields, out, prior):
    clusters, blocks, dof, _ = out.shape
    layer = fields[0].shape[0]
    count = layers * layer
    return pl.pallas_call(
        kernel,
        in_specs=[in_smem()] + in_vmem(1 + len(fields)) + [in_place()] * len(prior),
        out_specs=in_place(),
        out_shape=out,
        scratch_shapes=[
            VMEM((count, clusters, dof, dof), BF16),
            pltpu.SemaphoreType.DMA((count, clusters)),
        ],
        input_output_aliases={2 + len(fields): 0} if prior else {},
        compiler_params=params(8 * layers + 4),
        cost_estimate=cost(
            2 * count * dof * left.size, 2 * count * clusters * dof * dof
        ),
    )(block_of, left, *fields, *prior)


def swap_near(block):
    count = lax.axis_size("cx")
    return lax.ppermute(block, "cx", [(i, i ^ 1) for i in range(count)])


def swap_far(block):
    count = lax.axis_size("cx")
    pairs = [(i, (i + 1) % count if i % 2 else (i - 1) % count) for i in range(count)]
    return lax.ppermute(block, "cx", pairs)


def arrange(field, atom_map):
    taken = jnp.take(field, atom_map.reshape(-1), axis=2)
    taken = taken.reshape(field.shape[0], 3, atom_map.shape[0], atom_map.shape[1])
    return jnp.transpose(taken, (2, 1, 3, 0)).reshape(
        atom_map.shape[0], 3 * atom_map.shape[1], field.shape[0]
    )


def shards(displacements, forces, phi, neighbours, cluster_atoms, config_order, weights):
    width = lax.axis_size("cx")
    position = lax.axis_index("cx")
    layer, atoms = cluster_atoms.shape
    blocks = neighbours.shape[1]
    per = displacements.shape[2] // width
    offset = (neighbours // layer - position + 1 + width) % width
    partner = jnp.where(position % 2 == 0, 2, 0)
    group = jnp.where(offset == 1, 0, jnp.where(offset == partner, 1, 2))
    slot = group * layer + neighbours % layer
    named = slot[:, None, :] == jnp.arange(3 * layer, dtype=jnp.int32)[None, :, None]
    block_of = jnp.min(
        jnp.where(named, jnp.arange(blocks, dtype=jnp.int32)[None, None, :], blocks), axis=2
    )
    match = config_order[:, None] == jnp.arange(config_order.shape[0], dtype=jnp.int32)[None, :]
    wt = jnp.sum(jnp.where(match, weights[None, :], 0.0), axis=1)[None, :]
    atom_local = cluster_atoms - position * per
    dense = displacements.shape[0] % 16 == 0 and per % 128 == 64 and width % 2 == 0
    if dense:
        send1, send2 = pack(
            jnp.transpose(displacements, (1, 0, 2)), jnp.transpose(forces, (1, 0, 2)), width
        )
        recv1 = lax.all_to_all(send1, "cx", split_axis=0, concat_axis=0, tiled=True)
        recv2 = lax.all_to_all(send2, "cx", split_axis=0, concat_axis=0, tiled=True)
        index = ((atom_local - 64 * (position % 2) + per) % per).reshape(-1, 1)
        disp = gather(index, recv1, layer, atoms)
    else:
        disp, force = (
            arrange(lax.all_to_all(x, "cx", split_axis=2, concat_axis=0, tiled=True), atom_local)
            for x in (displacements, forces)
        )
    disp_near, disp_far = swap_near(disp), swap_far(disp)
    harmonic = near_harmonic(block_of, phi, disp, disp_near)
    if dense:
        base = add_force(index, recv1, recv2, harmonic)
    else:
        base = force.astype(F32) + harmonic
    residual, res, left = residual_of(block_of, phi, disp_far, base, disp, wt)
    res_near, res_far = swap_near(res), swap_far(res)
    out = shape(phi.shape)
    gradient = gradient_call(
        near_gradient_kernel, 2, block_of, left, (disp, disp_near, res, res_near), out, ()
    )
    gradient = gradient_call(
        far_gradient_kernel, 1, block_of, left, (disp_far, res_far), out, (gradient,)
    )
    return residual, gradient


def solution(mesh):
    both = ("groups", "cx")
    in_specs = (
        P(both, None, None),
        P(both, None, None),
        P(both, None, None, None),
        P("cx", None),
        P("cx", None),
        P("groups"),
        P("groups"),
    )
    out_specs = (P(both, None, None), P(both, None, None, None))
    return jax.shard_map(shards, mesh=mesh, in_specs=in_specs, out_specs=out_specs, check_vma=False)
```

time: 140 us -> 72.2 us (0.52)
  the two profiles are of different devices: /device:TPU:0 before, /device:TPU:1 now
where the time goes in v2:
time: 72.2 us; the launch traced here: 71.7 us
  blocking collectives  21.1 us (29%)
  Pallas kernels  15.4 us (21%)
  waiting for transfers between devices  15.4 us (21%)
  local copies, waits for them, and re-layouts  9.07 us (13%)
  starting transfers between devices  7.5 us (10%)
  other arithmetic  2.46 us (3%)
  between operations  0.74 us (1%)
    all_to_all x1, blocking collectives, shards(): recv1 = lax.all_to_all(send1, 'cx', split_axis=0, concat_axis=0, tiled=True)  21.1 us
    unnamed x12, local copies, waits for them, and re-layouts  8.92 us
    pallas_call x2, Pallas kernels, gradient_call(): pl.pallas_call(kernel, in_specs=[in_smem()] + in_vmem(1 + len(fields)) +...  8.14 us
    all_to_all x1, waiting for transfers between devices, shards(): recv2 = lax.all_to_all(send2, 'cx', split_axis=0, concat_axis=0, tiled=True)  8.02 us
    ppermute x2, waiting for transfers between devices, swap_far(): return lax.ppermute(block, 'cx', pairs)  6.75 us
    all_to_all x1, starting transfers between devices, shards(): recv2 = lax.all_to_all(send2, 'cx', split_axis=0, concat_axis=0, tiled=True)  4.44 us
    ppermute x2, starting transfers between devices, swap_far(): return lax.ppermute(block, 'cx', pairs)  2.87 us
    pallas_call x1, Pallas kernels, residual_of(): pl.pallas_call(residual_kernel, in_specs=[in_smem()] + in_vmem(5), out_sp...  2.36 us
  transfers between devices with their start and end apart: 5, of which 3 were waited for; matrix products, arithmetic and copies ran while one was open for 4% of the time, Pallas kernels for 11%

profile of v2, /device:TPU:1, one launch (start us, length us, event | category | flops | bytes accessed | tf_op | source)
XLA Modules:
  0.0 71.7 jit_solution(3714081922101852813)
XLA Ops:
  0.6 0.0 copy-start.4
  0.6 1.0 %copy-done.4 = bf16[16,3,5120]{2,0,1:T(8,128)(2,1)S(1)} copy-done((bf16[16,3,5120]{2,0,1:T(8,128)(2,1)S(1)}, bf16[16,3,5120]{2,0,1:T(8,128)(2,1)}, u32[]{:S(2)}) %copy-start.4) | copy-done | bytes 491544
  1.7 0.0 copy-start.5
  1.7 1.0 %copy-done.5 = bf16[16,3,5120]{2,0,1:T(8,128)(2,1)S(1)} copy-done((bf16[16,3,5120]{2,0,1:T(8,128)(2,1)S(1)}, bf16[16,3,5120]{2,0,1:T(8,128)(2,1)}, u32[]{:S(2)}) %copy-start.5) | copy-done | bytes 491544
  2.7 1.6 %shard_map.86 = (bf16[16,8,16,128]{3,2,1,0:T(8,128)(2,1)S(1)}, bf16[16,7,16,128]{3,2,1,0:T(8,128)(2,1)}) custom-call(bf16[3,16,5120]{2,1,0:T(8,128)(2,1)S(1)} %bitcast.3, bf16[3,16,5120]{2,1,0:T(8,128)(2,1)S(1)} %bitcast.4), custom_call_target="tpu_custom_call" | custom-call | bytes 1966080 | tf_op jit(solution)/shard_map/pallas_call | solution.py:80
  4.3 21.1 %all_to_all.10.recv_ref.recv1_ref = bf16[16,8,16,128]{3,2,1,0:T(8,128)(2,1)S(1)} all-to-all(bf16[16,8,16,128]{3,2,1,0:T(8,128)(2,1)S(1)} %get-tuple-element.7), channel_id=1, replica_groups=mesh['groups'=2,'cx'=16] {'cx'}, dimensions={0} | all-to-all | bytes 1048576 | tf_op jit(solution)/shard_map/all_to_all | solution.py:338
  25.4 4.4 %all-to-all-start.1 = ((bf16[16,7,16,128]{3,2,1,0:T(8,128)(2,1)}), bf16[16,7,16,128]{3,2,1,0:T(8,128)(2,1)S(1)}, u32[]{:S(2)}, u32[]{:S(2)}) async-start(bf16[16,7,16,128]{3,2,1,0:T(8,128)(2,1)} %get-tuple-element.8), calls=%async_computation.1 | async-start | bytes 917504 | tf_op jit(solution)/shard_map/all_to_all | solution.py:339
  29.9 0.7 add_select_fusion
  30.6 0.1 reshape.11.index_ref
  30.7 0.0 copy-start.2
  30.7 0.6 shard_map.87.own_ref.down
  31.3 0.2 collective-permute-start.1
  31.5 1.6 %collective-permute-start = (bf16[5,192,256]{2,1,0:T(8,128)(2,1)S(1)}, bf16[5,192,256]{2,1,0:T(8,128)(2,1)S(1)}, u32[]{:S(2)}, u32[]{:S(2)}) collective-permute-start(bf16[5,192,256]{2,1,0:T(8,128)(2,1)S(1)} %shard_map.87.own_ref.down), channel_id=1, source_target_pairs={{0,15},{1,2},{2,1},{3,4},{4,3},{5,6},{6,5},{7,8},{8,7},{9,10},{10,... | collective-permute-start | bytes 1474568 | tf_op jit(solution)/shard_map/ppermute | solution.py:305
  33.2 0.7 fusion.3
  33.9 0.2 select_reduce_fusion.1.block_ref
  34.0 0.9 %select_reduce_fusion = f32[256]{0:T(256)S(1)} fusion(f32[256]{0:T(256)} %param.13, s32[256]{0:T(256)} %param.12), kind=kLoop, calls=%fused_computation | loop fusion | flops 196352 | bytes 3072 | tf_op jit(solution)/shard_map/reduce_sum | solution.py:331
  34.9 0.0 copy-done.2
  34.9 0.0 collective-permute-done.1.partner_ref.dpart
  34.9 0.0 copy-start
  35.0 3.0 %copy-done = bf16[5,14,192,192]{3,2,1,0:T(8,128)(2,1)S(1)} copy-done((bf16[5,14,192,192]{3,2,1,0:T(8,128)(2,1)S(1)}, bf16[5,14,192,192]{3,2,1,0:T(8,128)(2,1)}, u32[]{:S(2)}) %copy-start) | copy-done | bytes 5160984
  37.9 2.1 %shard_map.88.harm_ref = f32[5,192,256]{2,1,0:T(8,128)S(1)} custom-call(s32[5,15]{1,0:T(8,128)S(1)} %select_reduce_fusion.1.block_ref, bf16[5,14,192,192]{3,2,1,0:T(8,128)(2,1)S(1)} %copy-done, bf16[5,192,256]{2,1,0:T(8,128)(2,1)S(1)} %shard_map.87.own_ref.down, bf16[5,192,256]{2,1,0:T(8,128)(2,1)S(1)} %collective-permute-done.1.partner_ref.dpart), custom_call_target="tpu_custom_call" | custom-call | flops 880803840 | bytes 3440640 | tf_op jit(solution)/shard_map/pallas_call | solution.py:193
  40.0 8.0 %all-to-all-done.1.recv2_ref = bf16[16,7,16,128]{3,2,1,0:T(8,128)(2,1)S(1)} async-done(((bf16[16,7,16,128]{3,2,1,0:T(8,128)(2,1)}), bf16[16,7,16,128]{3,2,1,0:T(8,128)(2,1)S(1)}, u32[]{:S(2)}, u32[]{:S(2)}) %all-to-all-start.1) | async-done | bytes 458784 | tf_op jit(solution)/shard_map/all_to_all | solution.py:339
  48.1 0.0 copy-start.3
  48.1 0.9 %copy-done.3 = s32[320,1]{1,0:T(8,128)S(1)} copy-done((s32[320,1]{1,0:T(8,128)S(1)}, s32[320,1]{1,0:T(8,128)}, u32[]{:S(2)}) %copy-start.3) | copy-done | bytes 1304
  49.0 0.6 shard_map.89.base_ref
  49.6 0.0 collective-permute-done.far_ref.dfar
  49.6 0.0 copy-start.1
  49.6 3.0 %copy-done.1 = bf16[5,14,192,192]{3,2,1,0:T(8,128)(2,1)S(1)} copy-done((bf16[5,14,192,192]{3,2,1,0:T(8,128)(2,1)S(1)}, bf16[5,14,192,192]{3,2,1,0:T(8,128)(2,1)}, u32[]{:S(2)}) %copy-start.1) | copy-done | bytes 5160984
  52.6 2.4 %shard_map.90 = (bf16[5,192,256]{2,1,0:T(8,128)(2,1)}, bf16[5,192,256]{2,1,0:T(8,128)(2,1)S(1)}, bf16[5,192,512]{2,1,0:T(8,128)(2,1)S(1)}) custom-call(s32[5,15]{1,0:T(8,128)S(1)} %select_reduce_fusion.1.block_ref, bf16[5,14,192,192]{3,2,1,0:T(8,128)(2,1)S(1)} %copy-done.1, bf16[5,192,256]{2,1,0:T(8,128)(2,1)S(1)} %collective-permute-done.far_ref.dfar, ...), custom_call_target="tpu_custom_call" | custom-call | flops 440401920 | bytes 1720320 | tf_op jit(solution)/shard_map/pallas_call | solution.py:224
  54.9 0.0 collective-permute-start.3
  54.9 1.2 %collective-permute-start.2 = (bf16[5,192,256]{2,1,0:T(8,128)(2,1)S(1)}, bf16[5,192,256]{2,1,0:T(8,128)(2,1)S(1)}, u32[]{:S(2)}, u32[]{:S(2)}) collective-permute-start(bf16[5,192,256]{2,1,0:T(8,128)(2,1)S(1)} %get-tuple-element.11.rown), channel_id=1, source_target_pairs={{0,15},{1,2},{2,1},{3,4},{4,3},{5,6},{6,5},{7,8},{8,7},{9,10},{10,... | collective-permute-start | bytes 1474568 | tf_op jit(solution)/shard_map/ppermute | solution.py:305
  56.2 0.6 collective-permute-done.3.rpart
  56.8 4.9 %shard_map.91.prior_ref = bf16[5,14,192,192]{3,2,1,0:T(8,128)(2,1)} custom-call(s32[5,15]{1,0:T(8,128)S(1)} %select_reduce_fusion.1.block_ref, bf16[5,192,512]{2,1,0:T(8,128)(2,1)S(1)} %get-tuple-element.10.left_ref, bf16[5,192,256]{2,1,0:T(8,128)(2,1)S(1)} %shard_map.87.own_ref.down, bf16[5,192,256]{2,1,0:T(8,128)(2,1)S(1)} %collective-permute-done.1.partner_ref.dpart, ...), custom_call_target="tpu_custom_call" | custom-call | flops 1887436800 | bytes 3686400 | tf_op jit(solution)/shard_map/pallas_call | solution.py:280
  61.7 6.7 %collective-permute-done.2.rfar = bf16[5,192,256]{2,1,0:T(8,128)(2,1)S(1)} collective-permute-done((bf16[5,192,256]{2,1,0:T(8,128)(2,1)S(1)}, bf16[5,192,256]{2,1,0:T(8,128)(2,1)S(1)}, u32[]{:S(2)}, u32[]{:S(2)}) %collective-permute-start.2) | collective-permute-done | bytes 491552 | tf_op jit(solution)/shard_map/ppermute | solution.py:305
  68.4 3.2 %shard_map.92 = bf16[5,14,192,192]{3,2,1,0:T(8,128)(2,1)} custom-call(s32[5,15]{1,0:T(8,128)S(1)} %select_reduce_fusion.1.block_ref, bf16[5,192,512]{2,1,0:T(8,128)(2,1)S(1)} %get-tuple-element.10.left_ref, bf16[5,192,256]{2,1,0:T(8,128)(2,1)S(1)} %collective-permute-done.far_ref.dfar, ...), custom_call_target="tpu_custom_call", output_to_operand_aliasing={{}: (4, {})} | custom-call | flops 943718400 | bytes 1843200 | tf_op jit(solution)/shard_map/pallas_call | solution.py:280
Async XLA Ops:
  0.6 1.0 %copy-start.4 = (bf16[16,3,5120]{2,0,1:T(8,128)(2,1)S(1)}, bf16[16,3,5120]{2,0,1:T(8,128)(2,1)}, u32[]{:S(2)}) copy-start(bf16[16,3,5120]{2,0,1:T(8,128)(2,1)} %param.7) | copy-start | bytes 1474564
  1.7 1.0 %copy-start.5 = (bf16[16,3,5120]{2,0,1:T(8,128)(2,1)S(1)}, bf16[16,3,5120]{2,0,1:T(8,128)(2,1)}, u32[]{:S(2)}) copy-start(bf16[16,3,5120]{2,0,1:T(8,128)(2,1)} %param.8) | copy-start | bytes 1474564
  25.4 22.6 %all-to-all-start.1 = ((bf16[16,7,16,128]{3,2,1,0:T(8,128)(2,1)}), bf16[16,7,16,128]{3,2,1,0:T(8,128)(2,1)S(1)}, u32[]{:S(2)}, u32[]{:S(2)}) async-start(bf16[16,7,16,128]{3,2,1,0:T(8,128)(2,1)} %get-tuple-element.8), calls=%async_computation.1 | async-start | bytes 917504 | tf_op jit(solution)/shard_map/all_to_all | solution.py:339
  30.7 4.2 %copy-start.2 = (s32[320,1]{1,0:T(8,128)}, s32[320,1]{1,0:T(8,128)S(1)}, u32[]{:S(2)}) copy-start(s32[320,1]{1,0:T(8,128)S(1)} %reshape.11.index_ref) | copy-start | bytes 3844
  31.3 3.6 %collective-permute-start.1 = (bf16[5,192,256]{2,1,0:T(8,128)(2,1)S(1)}, bf16[5,192,256]{2,1,0:T(8,128)(2,1)S(1)}, u32[]{:S(2)}, u32[]{:S(2)}) collective-permute-start(bf16[5,192,256]{2,1,0:T(8,128)(2,1)S(1)} %shard_map.87.own_ref.down), channel_id=1, source_target_pairs={{0,1},{1,0},{2,3},{3,2},{4,5},{5,4},{6,7},{7,6},{8,9},{9,8},{10,11... | collective-permute-start | bytes 1474568 | tf_op jit(solution)/shard_map/ppermute | solution.py:299
  31.5 18.0 %collective-permute-start = (bf16[5,192,256]{2,1,0:T(8,128)(2,1)S(1)}, bf16[5,192,256]{2,1,0:T(8,128)(2,1)S(1)}, u32[]{:S(2)}, u32[]{:S(2)}) collective-permute-start(bf16[5,192,256]{2,1,0:T(8,128)(2,1)S(1)} %shard_map.87.own_ref.down), channel_id=1, source_target_pairs={{0,15},{1,2},{2,1},{3,4},{4,3},{5,6},{6,5},{7,8},{8,7},{9,10},{10,... | collective-permute-start | bytes 1474568 | tf_op jit(solution)/shard_map/ppermute | solution.py:305
  34.9 3.0 %copy-start = (bf16[5,14,192,192]{3,2,1,0:T(8,128)(2,1)S(1)}, bf16[5,14,192,192]{3,2,1,0:T(8,128)(2,1)}, u32[]{:S(2)}) copy-start(bf16[5,14,192,192]{3,2,1,0:T(8,128)(2,1)} %phi_ref.3) | copy-start | bytes 15482884
  48.1 0.9 %copy-start.3 = (s32[320,1]{1,0:T(8,128)S(1)}, s32[320,1]{1,0:T(8,128)}, u32[]{:S(2)}) copy-start(s32[320,1]{1,0:T(8,128)} %copy-done.2) | copy-start | bytes 3844
  49.6 3.0 %copy-start.1 = (bf16[5,14,192,192]{3,2,1,0:T(8,128)(2,1)S(1)}, bf16[5,14,192,192]{3,2,1,0:T(8,128)(2,1)}, u32[]{:S(2)}) copy-start(bf16[5,14,192,192]{3,2,1,0:T(8,128)(2,1)} %phi_ref.3) | copy-start | bytes 15482884
  54.9 1.9 %collective-permute-start.3 = (bf16[5,192,256]{2,1,0:T(8,128)(2,1)S(1)}, bf16[5,192,256]{2,1,0:T(8,128)(2,1)S(1)}, u32[]{:S(2)}, u32[]{:S(2)}) collective-permute-start(bf16[5,192,256]{2,1,0:T(8,128)(2,1)S(1)} %get-tuple-element.11.rown), channel_id=1, source_target_pairs={{0,1},{1,0},{2,3},{3,2},{4,5},{5,4},{6,7},{7,6},{8,9},{9,8},{10,11... | collective-permute-start | bytes 1474568 | tf_op jit(solution)/shard_map/ppermute | solution.py:299
  54.9 13.5 %collective-permute-start.2 = (bf16[5,192,256]{2,1,0:T(8,128)(2,1)S(1)}, bf16[5,192,256]{2,1,0:T(8,128)(2,1)S(1)}, u32[]{:S(2)}, u32[]{:S(2)}) collective-permute-start(bf16[5,192,256]{2,1,0:T(8,128)(2,1)S(1)} %get-tuple-element.11.rown), channel_id=1, source_target_pairs={{0,15},{1,2},{2,1},{3,4},{4,3},{5,6},{6,5},{7,8},{8,7},{9,10},{10,... | collective-permute-start | bytes 1474568 | tf_op jit(solution)/shard_map/ppermute | solution.py:305

commit v3 on v2

v3 whole, which is shorter than its diff:
```python
import functools

import jax
import jax.numpy as jnp
from jax import lax
from jax.experimental import pallas as pl
from jax.experimental.pallas import tpu as pltpu
from jax.sharding import PartitionSpec as P


BF16 = jnp.bfloat16
F32 = jnp.float32
VMEM = pltpu.VMEM
SMEM = pltpu.SMEM
NT = (((1,), (1,)), ((), ()))
MIB = 1024 * 1024


def in_vmem(count):
    return [pl.BlockSpec(memory_space=VMEM)] * count


def in_smem():
    return pl.BlockSpec(memory_space=SMEM)


def params(mib, **kw):
    return pltpu.CompilerParams(vmem_limit_bytes=mib * MIB, **kw)


def cost(flops, nbytes):
    return pl.CostEstimate(flops=flops, bytes_accessed=nbytes, transcendentals=0)


def shape(dims, dtype=BF16):
    return jax.ShapeDtypeStruct(dims, dtype)


def pack_kernel(disp_ref, force_ref, out_ref):
    parts, configs, lanes = disp_ref.shape
    tiles = 2 * lanes // 128 // out_ref.shape[0]
    full = tiles // 2
    low = lax.broadcasted_iota(jnp.int32, (configs, 128), 1) < 64
    for pair in range(out_ref.shape[0] // 2):

        def tile(ref, a, t, pair=pair):
            return ref[a, :, pl.ds(128 * (pair * tiles + t), 128)]

        for e in range(2):
            first = e * (full + 1)

            def paired(ref0, a0, ref1, a1, e=e, tile=tile):
                x, y = tile(ref0, a0, full).astype(F32), tile(ref1, a1, full).astype(F32)
                if e == 0:
                    y = pltpu.roll(y, 64, 1)
                else:
                    x = pltpu.roll(x, 64, 1)
                return jnp.where(low, x, y).astype(BF16)

            dest = 2 * pair + e
            base = parts * full
            for a in range(parts):
                for t in range(full):
                    out_ref[dest, a * full + t] = tile(disp_ref, a, first + t)
                    out_ref[dest, base + 3 + a * full + t] = tile(force_ref, a, first + t)
            out_ref[dest, base] = paired(disp_ref, 0, disp_ref, 1)
            out_ref[dest, base + 1] = paired(disp_ref, 2, force_ref, 2)
            out_ref[dest, base + 2] = paired(force_ref, 0, force_ref, 1)


def pack(displacements, forces, width):
    parts, configs, atoms = displacements.shape
    per = atoms // width
    steps = 4 if width % 8 == 0 else width // 2
    group = width // steps
    spec = pl.BlockSpec((parts, configs, group * per), lambda i: (0, 0, i))
    tiles = 2 * parts * (per // 128) + 3
    return pl.pallas_call(
        pack_kernel,
        grid=(steps,),
        in_specs=[spec, spec],
        out_specs=pl.BlockSpec((group, tiles, configs, 128), lambda i: (i, 0, 0, 0)),
        out_shape=shape((width, tiles, configs, 128)),
        compiler_params=params(60),
        cost_estimate=cost(0, 8 * displacements.size),
    )(displacements, forces)


def one_hots(index_ref, full):
    index = index_ref[...]
    rows = index.shape[0]
    lane = lax.broadcasted_iota(jnp.int32, (rows, 128), 1)

    def hot(cond):
        return jnp.where(cond, 1.0, 0.0).astype(BF16)

    wholes = [hot(index - 128 * t == lane) for t in range(full)]
    rest = index - 128 * full
    lower = hot(rest == lane)
    upper = hot((rest >= 0) & (rest + 64 == lane))
    return wholes, lower, upper


def picked(wholes, half_hot, tiles, half):
    total = lax.dot_general(half_hot, half, NT, preferred_element_type=F32)
    for hot, tile in zip(wholes, tiles):
        total = total + lax.dot_general(hot, tile, NT, preferred_element_type=F32)
    return total


def flat(ref, t):
    block = ref[:, t]
    return block.reshape(block.shape[0] * block.shape[1], 128)


def component(recv_ref, hots, field, a):
    wholes, lower, upper = hots
    full = len(wholes)
    base = 3 * full
    half = base + 1 if a == 2 else base + 2 * field
    first = a * full + field * (base + 3)
    half_hot = upper if (a == 1 if field == 0 else a > 0) else lower
    tiles = [flat(recv_ref, first + t) for t in range(full)]
    return picked(wholes, half_hot, tiles, flat(recv_ref, half))


def gather_kernel(field, index_ref, recv_ref, out_ref):
    clusters, dof, _ = out_ref.shape
    atoms = dof // 3
    hots = one_hots(index_ref, (recv_ref.shape[1] - 3) // 6)
    for a in range(3):
        got = component(recv_ref, hots, field, a).astype(BF16)
        for c in range(clusters):
            out_ref[c, a * atoms : (a + 1) * atoms] = got[c * atoms : (c + 1) * atoms]


def gather(index, recv, field, clusters, atoms):
    configs = recv.shape[0] * recv.shape[2]
    return pl.pallas_call(
        functools.partial(gather_kernel, field),
        in_specs=in_vmem(2),
        out_specs=in_vmem(1)[0],
        out_shape=shape((clusters, 3 * atoms, configs)),
        compiler_params=params(8),
        cost_estimate=cost(recv.size * index.size, 3 * recv.size),
    )(index, recv)


def masked(block_ref, held, n, c, blocks):
    block = held[c]
    return jnp.where(block_ref[c, n] < blocks, block, jnp.zeros_like(block))


def near_harmonic_kernel(
    block_ref, phi_ref, own_ref, partner_ref, force_ref, out_ref, far_ref, held, sem
):
    clusters, blocks = phi_ref.shape[:2]
    layer = own_ref.shape[0]

    def fetch(n, c):
        k = jnp.minimum(block_ref[c, n], blocks - 1)
        return pltpu.make_async_copy(phi_ref.at[c, k], held.at[n, c], sem.at[n, c])

    for n in range(3 * layer):
        for c in range(clusters):
            fetch(n, c).start()
    for n in range(2 * layer):
        for c in range(clusters):
            fetch(n, c).wait()
        disp = own_ref[n] if n < layer else partner_ref[n - layer]
        left = jnp.concatenate(
            [masked(block_ref, held.at[n], n, c, blocks) for c in range(clusters)], axis=0
        )
        got = jnp.dot(left, disp, preferred_element_type=F32).reshape(out_ref.shape)
        out_ref[...] = (force_ref[...].astype(F32) if n == 0 else out_ref[...]) + got
    for n in range(2 * layer, 3 * layer):
        for c in range(clusters):
            fetch(n, c).wait()
    for c in range(clusters):
        row = [
            masked(block_ref, held.at[n], n, c, blocks) for n in range(2 * layer, 3 * layer)
        ]
        far_ref[c] = jnp.concatenate(row, axis=1)


def near_harmonic(block_of, phi, own, partner, force):
    clusters, _, dof, _ = phi.shape
    layer, _, configs = own.shape
    return pl.pallas_call(
        near_harmonic_kernel,
        in_specs=[in_smem(), pl.BlockSpec(memory_space=pltpu.HBM)] + in_vmem(3),
        out_specs=in_vmem(2),
        out_shape=[
            shape((clusters, dof, configs), F32),
            shape((clusters, dof, layer * dof)),
        ],
        scratch_shapes=[
            VMEM((3 * layer, clusters, dof, dof), BF16),
            pltpu.SemaphoreType.DMA((3 * layer, clusters)),
        ],
        compiler_params=params(16),
        cost_estimate=cost(4 * phi.size * configs // 3, 2 * phi.size),
    )(block_of, pltpu.with_memory_space_constraint(phi, pltpu.HBM), own, partner, force)


def residual_kernel(phi_ref, far_ref, base_ref, own_ref, wt_ref, out_ref, res_ref, left_ref):
    clusters, _, configs = out_ref.shape
    far = far_ref[...].reshape(phi_ref.shape[2], configs)
    wt = 0.5 * wt_ref[...]
    for c in range(clusters):
        total = base_ref[c] + jnp.dot(phi_ref[c], far, preferred_element_type=F32)
        res = total.astype(BF16)
        out_ref[c] = res
        res_ref[c] = res
        left_ref[c, :, :configs] = (res.astype(F32) * wt).astype(BF16)
        left_ref[c, :, configs:] = (own_ref[c].astype(F32) * wt).astype(BF16)


def residual_of(phi_far, far, base, own, wt):
    clusters, dof, configs = own.shape
    return pl.pallas_call(
        residual_kernel,
        in_specs=in_vmem(5),
        out_specs=in_vmem(3),
        out_shape=[
            shape((clusters, dof, configs)),
            shape((clusters, dof, configs)),
            shape((clusters, dof, 2 * configs)),
        ],
        compiler_params=params(8),
        cost_estimate=cost(2 * phi_far.size * configs, 2 * phi_far.size),
    )(phi_far, far, base, own, wt)


def put_blocks(block_ref, held, out_ref, sem, first):
    clusters, blocks = out_ref.shape[:2]

    def placed(i, c, act):
        k = block_ref[c, first + i]
        copy = pltpu.make_async_copy(
            held.at[i, c], out_ref.at[c, jnp.minimum(k, blocks - 1)], sem.at[i, c]
        )
        pl.when(k < blocks)(getattr(copy, act))

    def start(i):
        for c in range(clusters):
            placed(i, c, "start")

    def finish():
        for i in range(held.shape[0]):
            for c in range(clusters):
                placed(i, c, "wait")

    return start, finish


def near_gradient_kernel(
    block_ref, left_ref, down, dnear, dfar, rown, rnear, out_ref, far_ref, held, sem
):
    clusters, dof, width = left_ref.shape
    layer, _, configs = down.shape
    start, finish = put_blocks(block_ref, held, out_ref, sem, 0)
    left = left_ref[...].reshape(clusters * dof, width)
    for i in range(2 * layer):
        disp, res = (down, rown) if i < layer else (dnear, rnear)
        right = jnp.concatenate([disp[i % layer], res[i % layer]], axis=1)
        got = lax.dot_general(left, right, NT, preferred_element_type=F32)
        held[i] = got.astype(BF16).reshape(held.shape[1:])
        start(i)
    for i in range(layer):
        got = lax.dot_general(left[:, :configs], dfar[i], NT, preferred_element_type=F32)
        far_ref[i] = got.reshape(far_ref.shape[1:])
    finish()


def near_gradient(block_of, left, fields, out):
    clusters, _, dof, _ = out.shape
    layer = fields[0].shape[0]
    return pl.pallas_call(
        near_gradient_kernel,
        in_specs=[in_smem()] + in_vmem(6),
        out_specs=[pl.BlockSpec(memory_space=pltpu.HBM)] + in_vmem(1),
        out_shape=[out, shape((layer, clusters, dof, dof), F32)],
        scratch_shapes=[
            VMEM((2 * layer, clusters, dof, dof), BF16),
            pltpu.SemaphoreType.DMA((2 * layer, clusters)),
        ],
        compiler_params=params(16),
        cost_estimate=cost(5 * layer * dof * left.size, 4 * layer * clusters * dof * dof),
    )(block_of, left, *fields)


def far_gradient_kernel(block_ref, left_ref, rfar, far_ref, prior_ref, out_ref, held, sem):
    clusters, dof, width = left_ref.shape
    layer, _, configs = rfar.shape
    start, finish = put_blocks(block_ref, held, out_ref, sem, 2 * layer)
    left = left_ref[:, :, configs:].reshape(clusters * dof, width - configs)
    for i in range(layer):
        got = lax.dot_general(left, rfar[i], NT, preferred_element_type=F32)
        held[i] = (far_ref[i] + got.reshape(far_ref.shape[1:])).astype(BF16)
        start(i)
    finish()


def far_gradient(block_of, left, rfar, far, prior):
    clusters, _, dof, _ = prior.shape
    layer = rfar.shape[0]
    return pl.pallas_call(
        far_gradient_kernel,
        in_specs=[in_smem()] + in_vmem(3) + [pl.BlockSpec(memory_space=pltpu.HBM)],
        out_specs=pl.BlockSpec(memory_space=pltpu.HBM),
        out_shape=shape(prior.shape),
        scratch_shapes=[
            VMEM((layer, clusters, dof, dof), BF16),
            pltpu.SemaphoreType.DMA((layer, clusters)),
        ],
        input_output_aliases={4: 0},
        compiler_params=params(8),
        cost_estimate=cost(layer * dof * left.size, 6 * layer * clusters * dof * dof),
    )(block_of, left, rfar, far, prior)


def swap_near(block):
    count = lax.axis_size("cx")
    return lax.ppermute(block, "cx", [(i, i ^ 1) for i in range(count)])


def swap_far(block):
    count = lax.axis_size("cx")
    pairs = [(i, (i + 1) % count if i % 2 else (i - 1) % count) for i in range(count)]
    return lax.ppermute(block, "cx", pairs)


def arrange(field, atom_map):
    taken = jnp.take(field, atom_map.reshape(-1), axis=2)
    taken = taken.reshape(field.shape[0], 3, atom_map.shape[0], atom_map.shape[1])
    return jnp.transpose(taken, (2, 1, 3, 0)).reshape(
        atom_map.shape[0], 3 * atom_map.shape[1], field.shape[0]
    )


def tables(neighbours, config_order, weights, layer, position, width):
    blocks = neighbours.shape[1]
    offset = (neighbours // layer - position + 1 + width) % width
    partner = jnp.where(position % 2 == 0, 2, 0)
    group = jnp.where(offset == 1, 0, jnp.where(offset == partner, 1, 2))
    slot = group * layer + neighbours % layer
    named = slot[:, None, :] == jnp.arange(3 * layer, dtype=jnp.int32)[None, :, None]
    block_of = jnp.min(
        jnp.where(named, jnp.arange(blocks, dtype=jnp.int32)[None, None, :], blocks), axis=2
    )
    match = config_order[:, None] == jnp.arange(config_order.shape[0], dtype=jnp.int32)[None, :]
    wt = jnp.sum(jnp.where(match, weights[None, :], 0.0), axis=1)[None, :]
    return block_of, wt


def shards(displacements, forces, phi, neighbours, cluster_atoms, config_order, weights):
    width = lax.axis_size("cx")
    position = lax.axis_index("cx")
    layer, atoms = cluster_atoms.shape
    per = displacements.shape[2] // width
    block_of, wt = tables(neighbours, config_order, weights, layer, position, width)
    atom_local = cluster_atoms - position * per
    if displacements.shape[0] % 16 == 0 and per % 128 == 64 and width % 2 == 0:
        send = pack(
            jnp.transpose(displacements, (1, 0, 2)), jnp.transpose(forces, (1, 0, 2)), width
        )
        recv = lax.all_to_all(send, "cx", split_axis=0, concat_axis=0, tiled=True)
        index = ((atom_local - 64 * (position % 2) + per) % per).reshape(-1, 1)
        disp = gather(index, recv, 0, layer, atoms)
        force = gather(index, recv, 1, layer, atoms)
    else:
        disp, force = (
            arrange(lax.all_to_all(x, "cx", split_axis=2, concat_axis=0, tiled=True), atom_local)
            for x in (displacements, forces)
        )
    disp_near, disp_far = swap_near(disp), swap_far(disp)
    base, phi_far = near_harmonic(block_of, phi, disp, disp_near, force)
    residual, res, left = residual_of(phi_far, disp_far, base, disp, wt)
    res_near, res_far = swap_near(res), swap_far(res)
    gradient, far = near_gradient(
        block_of, left, (disp, disp_near, disp_far, res, res_near), shape(phi.shape)
    )
    return residual, far_gradient(block_of, left, res_far, far, gradient)


def solution(mesh):
    both = ("groups", "cx")
    in_specs = (
        P(both, None, None),
        P(both, None, None),
        P(both, None, None, None),
        P("cx", None),
        P("cx", None),
        P("groups"),
        P("groups"),
    )
    out_specs = (P(both, None, None), P(both, None, None, None))
    return jax.shard_map(shards, mesh=mesh, in_specs=in_specs, out_specs=out_specs, check_vma=False)
```

time: 72.2 us -> 67 us (0.928)
  the two profiles are of different devices: /device:TPU:1 before, /device:TPU:17 now
where the time goes in v3:
time: 67 us; the launch traced here: 66.6 us
  waiting for transfers between devices  36.3 us (54%)
  Pallas kernels  19.6 us (29%)
  starting transfers between devices  7.51 us (11%)
  other arithmetic  2.46 us (4%)
  between operations  0.69 us (1%)
    all_to_all x1, waiting for transfers between devices, shards(): recv = lax.all_to_all(send, 'cx', split_axis=0, concat_axis=0, tiled=True)  22.3 us
    ppermute x2, waiting for transfers between devices, swap_far(): return lax.ppermute(block, 'cx', pairs)  12.1 us
    all_to_all x1, starting transfers between devices, shards(): recv = lax.all_to_all(send, 'cx', split_axis=0, concat_axis=0, tiled=True)  6.47 us
    pallas_call x1, Pallas kernels, near_harmonic(): pl.pallas_call(near_harmonic_kernel, in_specs=[in_smem(), pl.BlockSpec(me...  5.99 us
    pallas_call x1, Pallas kernels, near_gradient(): pl.pallas_call(near_gradient_kernel, in_specs=[in_smem()] + in_vmem(6), o...  4.68 us
    pallas_call x1, Pallas kernels, pack(): pl.pallas_call(pack_kernel, grid=(steps,), in_specs=[spec, spec], out_spe...  3.51 us
    pallas_call x1, Pallas kernels, far_gradient(): pl.pallas_call(far_gradient_kernel, in_specs=[in_smem()] + in_vmem(3) + [...  2.66 us
    ppermute x2, waiting for transfers between devices, swap_near(): return lax.ppermute(block, 'cx', [(i, i ^ 1) for i in range(count)])  1.86 us
  transfers between devices with their start and end apart: 5, of which 4 were waited for; matrix products, arithmetic and copies ran while one was open for 4% of the time, Pallas kernels for 17%

profile of v3, /device:TPU:17, one launch (start us, length us, event | category | flops | bytes accessed | tf_op | source)
XLA Modules:
  0.0 66.6 jit_solution(13779910554597953583)
XLA Ops:
  0.6 3.5 %shard_map.86 = bf16[16,15,16,128]{3,2,1,0:T(8,128)(2,1)} custom-call(bf16[3,16,5120]{2,1,0:T(8,128)(2,1)} %bitcast.4, bf16[3,16,5120]{2,1,0:T(8,128)(2,1)} %bitcast.5), custom_call_target="tpu_custom_call" | custom-call | bytes 1966080 | tf_op jit(solution)/shard_map/pallas_call | solution.py:78
  4.1 6.5 %all-to-all-start = ((bf16[16,15,16,128]{3,2,1,0:T(8,128)(2,1)}), bf16[16,15,16,128]{3,2,1,0:T(8,128)(2,1)S(1)}, u32[]{:S(2)}, u32[]{:S(2)}) async-start(bf16[16,15,16,128]{3,2,1,0:T(8,128)(2,1)} %shard_map.86), calls=%async_computation | async-start | bytes 1966080 | tf_op jit(solution)/shard_map/all_to_all | solution.py:368
  10.6 0.7 %add_select_fusion = s32[5,64]{1,0:T(8,128)S(1)} fusion(s32[5,64]{1,0:T(8,128)} %param.11, s32[]{:T(128)S(6)} %mul_shard_map.3, s32[]{:T(128)S(6)} %mul.8), kind=kLoop, calls=%fused_computation.4 | loop fusion | flops 2880 | bytes 2568 | tf_op jit(solution)/shard_map/jit(remainder)/select_n | solution.py:369
  11.3 0.1 reshape.11.index_ref
  11.5 22.3 %all-to-all-done.recv_ref = bf16[16,15,16,128]{3,2,1,0:T(8,128)(2,1)S(1)} async-done(((bf16[16,15,16,128]{3,2,1,0:T(8,128)(2,1)}), bf16[16,15,16,128]{3,2,1,0:T(8,128)(2,1)S(1)}, u32[]{:S(2)}, u32[]{:S(2)}) %all-to-all-start) | async-done | bytes 983072 | tf_op jit(solution)/shard_map/all_to_all | solution.py:368
  33.8 0.6 shard_map.87.own_ref.down
  34.4 1.0 %collective-permute-start = (bf16[5,192,256]{2,1,0:T(8,128)(2,1)S(1)}, bf16[5,192,256]{2,1,0:T(8,128)(2,1)S(1)}, u32[]{:S(2)}, u32[]{:S(2)}) collective-permute-start(bf16[5,192,256]{2,1,0:T(8,128)(2,1)S(1)} %shard_map.87.own_ref.down), channel_id=1, source_target_pairs={{0,1},{1,0},{2,3},{3,2},{4,5},{5,4},{6,7},{7,6},{8,9},{9,8},{10,11... | collective-permute-start | bytes 1474568 | tf_op jit(solution)/shard_map/ppermute | solution.py:325
  35.4 0.0 collective-permute-start.1
  35.4 0.7 %fusion.3 = s32[5,14]{1,0:T(8,128)S(1)} fusion(s32[5,14]{1,0:T(8,128)} %param.10, s32[]{:T(128)S(6)} %select_n.53, s32[]{:T(128)S(6)} %axis_index.12), kind=kLoop, calls=%fused_computation.13 | loop fusion | flops 2170 | bytes 568 | tf_op jit(solution)/shard_map/add | solution.py:347
  36.1 0.2 select_reduce_fusion.1.block_ref
  36.3 0.9 %select_reduce_fusion = f32[256]{0:T(256)S(1)} fusion(f32[256]{0:T(256)} %param.13, s32[256]{0:T(256)} %param.12), kind=kLoop, calls=%fused_computation | loop fusion | flops 196352 | bytes 3072 | tf_op jit(solution)/shard_map/reduce_sum | solution.py:353
  37.2 0.6 shard_map.88.force_ref
  37.8 0.0 collective-permute-done.partner_ref.dnear
  37.8 6.0 %shard_map.89 = (f32[5,192,256]{2,1,0:T(8,128)S(1)}, bf16[5,192,960]{2,1,0:T(8,128)(2,1)S(1)}) custom-call(s32[5,15]{1,0:T(8,128)S(1)} %select_reduce_fusion.1.block_ref, bf16[5,14,192,192]{3,2,1,0:T(8,128)(2,1)} %phi_ref.1, bf16[5,192,256]{2,1,0:T(8,128)(2,1)S(1)} %shard_map.87.own_ref.down, ...), custom_call_target="tpu_custom_call" | custom-call | flops 880803840 | bytes 5160960 | tf_op jit(solution)/shard_map/pallas_call | solution.py:189
  43.8 5.1 %collective-permute-done.1.far_ref.dfar = bf16[5,192,256]{2,1,0:T(8,128)(2,1)S(1)} collective-permute-done((bf16[5,192,256]{2,1,0:T(8,128)(2,1)S(1)}, bf16[5,192,256]{2,1,0:T(8,128)(2,1)S(1)}, u32[]{:S(2)}, u32[]{:S(2)}) %collective-permute-start.1) | collective-permute-done | bytes 491552 | tf_op jit(solution)/shard_map/ppermute | solution.py:331
  48.9 1.5 %shard_map.90 = (bf16[5,192,256]{2,1,0:T(8,128)(2,1)}, bf16[5,192,256]{2,1,0:T(8,128)(2,1)S(1)}, bf16[5,192,512]{2,1,0:T(8,128)(2,1)S(1)}) custom-call(bf16[5,192,960]{2,1,0:T(8,128)(2,1)S(1)} %get-tuple-element.9.phi_ref, bf16[5,192,256]{2,1,0:T(8,128)(2,1)S(1)} %collective-permute-done.1.far_ref.dfar, f32[5,192,256]{2,1,0:T(8,128)S(1)} %get-tuple-element.10.base_ref, ...), custom_call_target="tpu_custom_call" | custom-call | flops 471859200 | bytes 1843200 | tf_op jit(solution)/shard_map/pallas_call | solution.py:221
  50.5 0.0 collective-permute-start.3
  50.5 0.0 collective-permute-start.2
  50.5 1.9 %collective-permute-done.3.rnear = bf16[5,192,256]{2,1,0:T(8,128)(2,1)S(1)} collective-permute-done((bf16[5,192,256]{2,1,0:T(8,128)(2,1)S(1)}, bf16[5,192,256]{2,1,0:T(8,128)(2,1)S(1)}, u32[]{:S(2)}, u32[]{:S(2)}) %collective-permute-start.3) | collective-permute-done | bytes 491552 | tf_op jit(solution)/shard_map/ppermute | solution.py:325
  52.3 4.7 %shard_map.91 = (bf16[5,14,192,192]{3,2,1,0:T(8,128)(2,1)}, f32[5,5,192,192]{3,2,1,0:T(8,128)S(1)}) custom-call(s32[5,15]{1,0:T(8,128)S(1)} %select_reduce_fusion.1.block_ref, bf16[5,192,512]{2,1,0:T(8,128)(2,1)S(1)} %get-tuple-element.12.left_ref, bf16[5,192,256]{2,1,0:T(8,128)(2,1)S(1)} %shard_map.87.own_ref.down, ...), custom_call_target="tpu_custom_call" | custom-call | flops 2359296000 | bytes 3686400 | tf_op jit(solution)/shard_map/pallas_call | solution.py:279
  57.0 7.0 %collective-permute-done.2.rfar = bf16[5,192,256]{2,1,0:T(8,128)(2,1)S(1)} collective-permute-done((bf16[5,192,256]{2,1,0:T(8,128)(2,1)S(1)}, bf16[5,192,256]{2,1,0:T(8,128)(2,1)S(1)}, u32[]{:S(2)}, u32[]{:S(2)}) %collective-permute-start.2) | collective-permute-done | bytes 491552 | tf_op jit(solution)/shard_map/ppermute | solution.py:331
  64.0 2.7 %shard_map.92 = bf16[5,14,192,192]{3,2,1,0:T(8,128)(2,1)} custom-call(s32[5,15]{1,0:T(8,128)S(1)} %select_reduce_fusion.1.block_ref, bf16[5,192,512]{2,1,0:T(8,128)(2,1)S(1)} %get-tuple-element.12.left_ref, bf16[5,192,256]{2,1,0:T(8,128)(2,1)S(1)} %collective-permute-done.2.rfar, ...), custom_call_target="tpu_custom_call", output_to_operand_aliasing={{}: (4, {})} | custom-call | flops 471859200 | bytes 5529600 | tf_op jit(solution)/shard_map/pallas_call | solution.py:308
Async XLA Ops:
  4.1 29.6 %all-to-all-start = ((bf16[16,15,16,128]{3,2,1,0:T(8,128)(2,1)}), bf16[16,15,16,128]{3,2,1,0:T(8,128)(2,1)S(1)}, u32[]{:S(2)}, u32[]{:S(2)}) async-start(bf16[16,15,16,128]{3,2,1,0:T(8,128)(2,1)} %shard_map.86), calls=%async_computation | async-start | bytes 1966080 | tf_op jit(solution)/shard_map/all_to_all | solution.py:368
  34.4 3.4 %collective-permute-start = (bf16[5,192,256]{2,1,0:T(8,128)(2,1)S(1)}, bf16[5,192,256]{2,1,0:T(8,128)(2,1)S(1)}, u32[]{:S(2)}, u32[]{:S(2)}) collective-permute-start(bf16[5,192,256]{2,1,0:T(8,128)(2,1)S(1)} %shard_map.87.own_ref.down), channel_id=1, source_target_pairs={{0,1},{1,0},{2,3},{3,2},{4,5},{5,4},{6,7},{7,6},{8,9},{9,8},{10,11... | collective-permute-start | bytes 1474568 | tf_op jit(solution)/shard_map/ppermute | solution.py:325
  35.4 13.5 %collective-permute-start.1 = (bf16[5,192,256]{2,1,0:T(8,128)(2,1)S(1)}, bf16[5,192,256]{2,1,0:T(8,128)(2,1)S(1)}, u32[]{:S(2)}, u32[]{:S(2)}) collective-permute-start(bf16[5,192,256]{2,1,0:T(8,128)(2,1)S(1)} %shard_map.87.own_ref.down), channel_id=1, source_target_pairs={{0,15},{1,2},{2,1},{3,4},{4,3},{5,6},{6,5},{7,8},{8,7},{9,10},{10,... | collective-permute-start | bytes 1474568 | tf_op jit(solution)/shard_map/ppermute | solution.py:331
  50.5 1.9 %collective-permute-start.3 = (bf16[5,192,256]{2,1,0:T(8,128)(2,1)S(1)}, bf16[5,192,256]{2,1,0:T(8,128)(2,1)S(1)}, u32[]{:S(2)}, u32[]{:S(2)}) collective-permute-start(bf16[5,192,256]{2,1,0:T(8,128)(2,1)S(1)} %get-tuple-element.13.rown), channel_id=1, source_target_pairs={{0,1},{1,0},{2,3},{3,2},{4,5},{5,4},{6,7},{7,6},{8,9},{9,8},{10,11... | collective-permute-start | bytes 1474568 | tf_op jit(solution)/shard_map/ppermute | solution.py:325
  50.5 13.5 %collective-permute-start.2 = (bf16[5,192,256]{2,1,0:T(8,128)(2,1)S(1)}, bf16[5,192,256]{2,1,0:T(8,128)(2,1)S(1)}, u32[]{:S(2)}, u32[]{:S(2)}) collective-permute-start(bf16[5,192,256]{2,1,0:T(8,128)(2,1)S(1)} %get-tuple-element.13.rown), channel_id=1, source_target_pairs={{0,15},{1,2},{2,1},{3,4},{4,3},{5,6},{6,5},{7,8},{8,7},{9,10},{10,... | collective-permute-start | bytes 1474568 | tf_op jit(solution)/shard_map/ppermute | solution.py:331

commit v4 on v3

v4 whole, which is shorter than its diff:
```python
import functools

import jax
import jax.numpy as jnp
from jax import lax
from jax.experimental import pallas as pl
from jax.experimental.pallas import tpu as pltpu
from jax.sharding import PartitionSpec as P


BF16 = jnp.bfloat16
F32 = jnp.float32
VMEM = pltpu.VMEM
SMEM = pltpu.SMEM
NT = (((1,), (1,)), ((), ()))
MIB = 1024 * 1024


def in_vmem(count):
    return [pl.BlockSpec(memory_space=VMEM)] * count


def in_smem():
    return pl.BlockSpec(memory_space=SMEM)


def params(mib, **kw):
    return pltpu.CompilerParams(vmem_limit_bytes=mib * MIB, **kw)


def cost(flops, nbytes):
    return pl.CostEstimate(flops=flops, bytes_accessed=nbytes, transcendentals=0)


def shape(dims, dtype=BF16):
    return jax.ShapeDtypeStruct(dims, dtype)


def pack_kernel(disp_hbm, force_hbm, out_hbm, disp_ref, force_ref, out_ref, sem, out_sem):
    parts, configs, lanes = disp_ref.shape
    steps = sem.shape[1]
    group = out_ref.shape[0] // steps
    chunk = lanes // steps
    per_pair = 2 * lanes // out_ref.shape[0]
    full = per_pair // 256
    base = parts * full
    low = lax.broadcasted_iota(jnp.int32, (configs, 128), 1) < 64

    def fetch(field, i):
        source, target = ((disp_hbm, disp_ref), (force_hbm, force_ref))[field]
        cols = pl.ds(i * chunk, chunk)
        return pltpu.make_async_copy(
            source.at[:, :, cols], target.at[:, :, cols], sem.at[field, i]
        )

    def send(i):
        dests = pl.ds(i * group, group)
        return pltpu.make_async_copy(out_ref.at[dests], out_hbm.at[dests], out_sem.at[i])

    def tile(ref, a, pair, t):
        return ref[a, :, pl.ds(per_pair * pair + 128 * t, 128)]

    def paired(ref0, a0, ref1, a1, pair, e):
        x, y = tile(ref0, a0, pair, full).astype(F32), tile(ref1, a1, pair, full).astype(F32)
        if e == 0:
            y = pltpu.roll(y, 64, 1)
        else:
            x = pltpu.roll(x, 64, 1)
        return jnp.where(low, x, y).astype(BF16)

    for i in range(steps):
        for field in range(2):
            fetch(field, i).start()
    for i in range(steps):
        for field in range(2):
            fetch(field, i).wait()
        for dest in range(i * group, (i + 1) * group):
            pair, e = dest // 2, dest % 2
            first = e * (full + 1)
            for a in range(parts):
                for t in range(full):
                    out_ref[dest, a * full + t] = tile(disp_ref, a, pair, first + t)
                    out_ref[dest, base + 3 + a * full + t] = tile(force_ref, a, pair, first + t)
            out_ref[dest, base] = paired(disp_ref, 0, disp_ref, 1, pair, e)
            out_ref[dest, base + 1] = paired(disp_ref, 2, force_ref, 2, pair, e)
            out_ref[dest, base + 2] = paired(force_ref, 0, force_ref, 1, pair, e)
        send(i).start()
    for i in range(steps):
        send(i).wait()


def pack(displacements, forces, width):
    parts, configs, atoms = displacements.shape
    per = atoms // width
    steps = 4 if width % 8 == 0 else 1
    tiles = 2 * parts * (per // 128) + 3
    hbm = pl.BlockSpec(memory_space=pltpu.HBM)
    return pl.pallas_call(
        pack_kernel,
        in_specs=[hbm, hbm],
        out_specs=hbm,
        out_shape=shape((width, tiles, configs, 128)),
        scratch_shapes=[VMEM(displacements.shape, BF16)] * 2
        + [VMEM((width, tiles, configs, 128), BF16)]
        + [pltpu.SemaphoreType.DMA((2, steps)), pltpu.SemaphoreType.DMA((steps,))],
        compiler_params=params(8),
        cost_estimate=cost(0, 8 * displacements.size),
    )(*(pltpu.with_memory_space_constraint(x, pltpu.HBM) for x in (displacements, forces)))


def one_hots(index_ref, full):
    index = index_ref[...]
    rows = index.shape[0]
    lane = lax.broadcasted_iota(jnp.int32, (rows, 128), 1)

    def hot(cond):
        return jnp.where(cond, 1.0, 0.0).astype(BF16)

    wholes = [hot(index - 128 * t == lane) for t in range(full)]
    rest = index - 128 * full
    lower = hot(rest == lane)
    upper = hot((rest >= 0) & (rest + 64 == lane))
    return wholes, lower, upper


def picked(wholes, half_hot, tiles, half):
    total = lax.dot_general(half_hot, half, NT, preferred_element_type=F32)
    for hot, tile in zip(wholes, tiles):
        total = total + lax.dot_general(hot, tile, NT, preferred_element_type=F32)
    return total


def flat(ref, t):
    block = ref[:, t]
    return block.reshape(block.shape[0] * block.shape[1], 128)


def component(recv_ref, hots, field, a):
    wholes, lower, upper = hots
    full = len(wholes)
    base = 3 * full
    half = base + 1 if a == 2 else base + 2 * field
    first = a * full + field * (base + 3)
    half_hot = upper if (a == 1 if field == 0 else a > 0) else lower
    tiles = [flat(recv_ref, first + t) for t in range(full)]
    return picked(wholes, half_hot, tiles, flat(recv_ref, half))


def gather_kernel(field, index_ref, recv_ref, out_ref):
    clusters, dof, _ = out_ref.shape
    atoms = dof // 3
    hots = one_hots(index_ref, (recv_ref.shape[1] - 3) // 6)
    for a in range(3):
        got = component(recv_ref, hots, field, a).astype(BF16)
        for c in range(clusters):
            out_ref[c, a * atoms : (a + 1) * atoms] = got[c * atoms : (c + 1) * atoms]


def gather(index, recv, field, clusters, atoms):
    configs = recv.shape[0] * recv.shape[2]
    return pl.pallas_call(
        functools.partial(gather_kernel, field),
        in_specs=in_vmem(2),
        out_specs=in_vmem(1)[0],
        out_shape=shape((clusters, 3 * atoms, configs)),
        compiler_params=params(8),
        cost_estimate=cost(recv.size * index.size, 3 * recv.size),
    )(index, recv)


def order_kernel(block_ref, phi_ref, near_ref, far_ref):
    c = pl.program_id(0)
    blocks, dof = phi_ref.shape[1:3]
    near = near_ref.shape[2] // dof

    def block(n):
        k = block_ref[c, n]
        got = phi_ref[0, jnp.minimum(k, blocks - 1)]
        return jnp.where(k < blocks, got, jnp.zeros_like(got))

    near_ref[0] = jnp.concatenate([block(n) for n in range(near)], axis=1)
    far_ref[0] = jnp.concatenate([block(near + n) for n in range(near // 2)], axis=1)


def ordered(block_of, phi):
    clusters, blocks, dof, _ = phi.shape
    layer = block_of.shape[1] // 3
    widths = (2 * layer * dof, layer * dof)
    return pl.pallas_call(
        order_kernel,
        grid_spec=pltpu.PrefetchScalarGridSpec(
            num_scalar_prefetch=1,
            grid=(clusters,),
            in_specs=[pl.BlockSpec((1, blocks, dof, dof), lambda c, block: (c, 0, 0, 0))],
            out_specs=[pl.BlockSpec((1, dof, w), lambda c, block: (c, 0, 0)) for w in widths],
        ),
        out_shape=[shape((clusters, dof, w)) for w in widths],
        compiler_params=params(40),
        cost_estimate=cost(0, 4 * phi.size),
    )(block_of, phi)


def near_harmonic_kernel(phi_ref, own_ref, partner_ref, force_ref, wt_ref, out_ref, wdisp_ref):
    c = pl.program_id(0)
    depth = phi_ref.shape[2] // 2
    configs = own_ref.shape[2]
    total = force_ref[0].astype(F32)
    for i, ref in enumerate((own_ref, partner_ref)):
        left = phi_ref[0, :, depth * i : depth * (i + 1)]
        total = total + jnp.dot(
            left, ref[...].reshape(depth, configs), preferred_element_type=F32
        )
    out_ref[0] = total
    wdisp_ref[0] = (own_ref[c].astype(F32) * (0.5 * wt_ref[...])).astype(BF16)


def near_harmonic(phi_near, own, partner, force, wt):
    clusters, dof, width = phi_near.shape
    configs = own.shape[2]
    one = pl.BlockSpec((1, dof, configs), lambda c: (c, 0, 0))
    return pl.pallas_call(
        near_harmonic_kernel,
        grid=(clusters,),
        in_specs=[pl.BlockSpec((1, dof, width), lambda c: (c, 0, 0))]
        + in_vmem(2)
        + [one, pl.BlockSpec((1, configs), lambda c: (0, 0))],
        out_specs=[one, one],
        out_shape=[shape(own.shape, F32), shape(own.shape)],
        compiler_params=params(16),
        cost_estimate=cost(2 * phi_near.size * configs, 2 * phi_near.size),
    )(phi_near, own, partner, force, wt)


def residual_kernel(phi_ref, far_ref, base_ref, wt_ref, res_ref, wres_ref):
    clusters, _, configs = res_ref.shape
    far = far_ref[...].reshape(phi_ref.shape[2], configs)
    wt = 0.5 * wt_ref[...]
    for c in range(clusters):
        total = base_ref[c] + jnp.dot(phi_ref[c], far, preferred_element_type=F32)
        res = total.astype(BF16)
        res_ref[c] = res
        wres_ref[c] = (res.astype(F32) * wt).astype(BF16)


def residual_of(phi_far, far, base, wt):
    return pl.pallas_call(
        residual_kernel,
        in_specs=in_vmem(4),
        out_specs=in_vmem(2),
        out_shape=[shape(far.shape)] * 2,
        compiler_params=params(8),
        cost_estimate=cost(2 * phi_far.size * far.shape[2], 2 * phi_far.size),
    )(phi_far, far, base, wt)


def put_blocks(block_ref, held, out_ref, sem, first):
    clusters, blocks = out_ref.shape[:2]

    def placed(i, c, act):
        k = block_ref[c, first + i]
        copy = pltpu.make_async_copy(
            held.at[i, c], out_ref.at[c, jnp.minimum(k, blocks - 1)], sem.at[i, c]
        )
        pl.when(k < blocks)(getattr(copy, act))

    def start(i):
        for c in range(clusters):
            placed(i, c, "start")

    def finish():
        for i in range(held.shape[0]):
            for c in range(clusters):
                placed(i, c, "wait")

    return start, finish


def near_gradient_kernel(
    block_ref, wres_ref, wdisp_ref, down, dnear, dfar, rown, rnear, out_ref, whole_ref, far_ref,
    held, sem, whole_sem
):
    clusters, dof, configs = wres_ref.shape
    layer = down.shape[0]
    keep = pltpu.make_async_copy(rown, whole_ref, whole_sem)
    keep.start()
    start, finish = put_blocks(block_ref, held, out_ref, sem, 0)
    wres = wres_ref[...].reshape(clusters * dof, configs)
    wdisp = wdisp_ref[...].reshape(clusters * dof, configs)
    left = jnp.concatenate([wres, wdisp], axis=1)
    for i in range(2 * layer):
        disp, res = (down, rown) if i < layer else (dnear, rnear)
        right = jnp.concatenate([disp[i % layer], res[i % layer]], axis=1)
        got = lax.dot_general(left, right, NT, preferred_element_type=F32)
        held[i] = got.astype(BF16).reshape(held.shape[1:])
        start(i)
    for i in range(layer):
        got = lax.dot_general(wres, dfar[i], NT, preferred_element_type=F32)
        far_ref[i] = got.reshape(far_ref.shape[1:])
    finish()
    keep.wait()


def far_gradient_kernel(block_ref, wdisp_ref, rfar, far_ref, prior_ref, out_ref, held, sem):
    clusters, dof, configs = wdisp_ref.shape
    start, finish = put_blocks(block_ref, held, out_ref, sem, 2 * far_ref.shape[0])
    left = wdisp_ref[...].reshape(clusters * dof, configs)
    for i in range(rfar.shape[0]):
        got = lax.dot_general(left, rfar[i], NT, preferred_element_type=F32)
        held[i] = (far_ref[i] + got.reshape(held.shape[1:])).astype(BF16)
        start(i)
    finish()


def block_copies(count, clusters, dof):
    return [
        VMEM((count, clusters, dof, dof), BF16),
        pltpu.SemaphoreType.DMA((count, clusters)),
    ]


def near_gradient(block_of, wres, wdisp, fields, out):
    clusters, _, dof, _ = out.shape
    layer = fields[0].shape[0]
    hbm = pl.BlockSpec(memory_space=pltpu.HBM)
    return pl.pallas_call(
        near_gradient_kernel,
        in_specs=[in_smem()] + in_vmem(7),
        out_specs=[hbm, hbm] + in_vmem(1),
        out_shape=[out, shape(wres.shape), shape((layer, clusters, dof, dof), F32)],
        scratch_shapes=block_copies(2 * layer, clusters, dof) + [pltpu.SemaphoreType.DMA(())],
        compiler_params=params(16),
        cost_estimate=cost(10 * layer * dof * wres.size, 4 * layer * clusters * dof * dof),
    )(block_of, wres, wdisp, *fields)


def far_gradient(block_of, wdisp, rfar, far, prior):
    clusters, _, dof, _ = prior.shape
    layer = rfar.shape[0]
    hbm = pl.BlockSpec(memory_space=pltpu.HBM)
    return pl.pallas_call(
        far_gradient_kernel,
        in_specs=[in_smem()] + in_vmem(3) + [hbm],
        out_specs=hbm,
        out_shape=shape(prior.shape),
        scratch_shapes=block_copies(layer, clusters, dof),
        input_output_aliases={4: 0},
        compiler_params=params(8),
        cost_estimate=cost(2 * layer * dof * wdisp.size, 6 * layer * clusters * dof * dof),
    )(block_of, wdisp, rfar, far, prior)


def swap_near(block):
    count = lax.axis_size("cx")
    return lax.ppermute(block, "cx", [(i, i ^ 1) for i in range(count)])


def swap_far(block):
    count = lax.axis_size("cx")
    pairs = [(i, (i + 1) % count if i % 2 else (i - 1) % count) for i in range(count)]
    return lax.ppermute(block, "cx", pairs)


def arrange(field, atom_map):
    taken = jnp.take(field, atom_map.reshape(-1), axis=2)
    taken = taken.reshape(field.shape[0], 3, atom_map.shape[0], atom_map.shape[1])
    return jnp.transpose(taken, (2, 1, 3, 0)).reshape(
        atom_map.shape[0], 3 * atom_map.shape[1], field.shape[0]
    )


def tables(neighbours, config_order, weights, layer, position, width):
    blocks = neighbours.shape[1]
    offset = (neighbours // layer - position + 1 + width) % width
    partner = jnp.where(position % 2 == 0, 2, 0)
    group = jnp.where(offset == 1, 0, jnp.where(offset == partner, 1, 2))
    slot = group * layer + neighbours % layer
    named = slot[:, None, :] == jnp.arange(3 * layer, dtype=jnp.int32)[None, :, None]
    block_of = jnp.min(
        jnp.where(named, jnp.arange(blocks, dtype=jnp.int32)[None, None, :], blocks), axis=2
    )
    match = config_order[:, None] == jnp.arange(config_order.shape[0], dtype=jnp.int32)[None, :]
    wt = jnp.sum(jnp.where(match, weights[None, :], 0.0), axis=1)[None, :]
    return block_of, wt


def shards(displacements, forces, phi, neighbours, cluster_atoms, config_order, weights):
    width = lax.axis_size("cx")
    position = lax.axis_index("cx")
    layer, atoms = cluster_atoms.shape
    per = displacements.shape[2] // width
    block_of, wt = tables(neighbours, config_order, weights, layer, position, width)
    atom_local = cluster_atoms - position * per
    if displacements.shape[0] % 16 == 0 and per % 128 == 64 and width % 2 == 0:
        send = pack(
            jnp.transpose(displacements, (1, 0, 2)), jnp.transpose(forces, (1, 0, 2)), width
        )
        recv = lax.all_to_all(send, "cx", split_axis=0, concat_axis=0, tiled=True)
        index = ((atom_local - 64 * (position % 2) + per) % per).reshape(-1, 1)
        disp = gather(index, recv, 0, layer, atoms)
        force = gather(index, recv, 1, layer, atoms)
    else:
        disp, force = (
            arrange(lax.all_to_all(x, "cx", split_axis=2, concat_axis=0, tiled=True), atom_local)
            for x in (displacements, forces)
        )
    phi_near, phi_far = ordered(block_of, phi)
    disp_far = swap_far(disp)
    disp_near = swap_near(disp)
    base, wdisp = near_harmonic(phi_near, disp, disp_near, force, wt)
    res, wres = residual_of(phi_far, disp_far, base, wt)
    res_far = swap_far(res)
    res_near = swap_near(res)
    gradient, residual, far = near_gradient(
        block_of, wres, wdisp, (disp, disp_near, disp_far, res, res_near), shape(phi.shape)
    )
    return residual, far_gradient(block_of, wdisp, res_far, far, gradient)


def solution(mesh):
    both = ("groups", "cx")
    in_specs = (
        P(both, None, None),
        P(both, None, None),
        P(both, None, None, None),
        P("cx", None),
        P("cx", None),
        P("groups"),
        P("groups"),
    )
    out_specs = (P(both, None, None), P(both, None, None, None))
    return jax.shard_map(shards, mesh=mesh, in_specs=in_specs, out_specs=out_specs, check_vma=False)
```

time: 67 us -> 65 us (0.970)
  the two profiles are of different devices: /device:TPU:17 before, /device:TPU:1 now
where the time goes in v4:
time: 65 us; the launch traced here: 63.8 us
  waiting for transfers between devices  31 us (48%)
  Pallas kernels  15.9 us (24%)
  starting transfers between devices  11.3 us (17%)
  local copies, waits for them, and re-layouts  3.13 us (5%)
  other arithmetic  1.77 us (3%)
  between operations  0.77 us (1%)
    all_to_all x1, waiting for transfers between devices, shards(): recv = lax.all_to_all(send, 'cx', split_axis=0, concat_axis=0, tiled=True)  21.2 us
    ppermute x2, waiting for transfers between devices, swap_far(): return lax.ppermute(block, 'cx', pairs)  9.73 us
    all_to_all x1, starting transfers between devices, shards(): recv = lax.all_to_all(send, 'cx', split_axis=0, concat_axis=0, tiled=True)  7.35 us
    pallas_call x1, Pallas kernels, near_gradient(): pl.pallas_call(near_gradient_kernel, in_specs=[in_smem()] + in_vmem(7), o...  5.02 us
    ppermute x2, starting transfers between devices, swap_far(): return lax.ppermute(block, 'cx', pairs)  3.59 us
    unnamed x6, local copies, waits for them, and re-layouts  2.98 us
    pallas_call x1, Pallas kernels, far_gradient(): pl.pallas_call(far_gradient_kernel, in_specs=[in_smem()] + in_vmem(3) + [...  2.62 us
    pallas_call x1, Pallas kernels, pack(): pl.pallas_call(pack_kernel, in_specs=[hbm, hbm], out_specs=hbm, out_shape...  2.18 us
  transfers between devices with their start and end apart: 5, of which 3 were waited for; matrix products, arithmetic and copies ran while one was open for 3% of the time, Pallas kernels for 15%

profile of v4, /device:TPU:1, one launch (start us, length us, event | category | flops | bytes accessed | tf_op | source)
XLA Modules:
  0.0 63.8 jit_solution(10214161679869129094)
XLA Ops:
  0.6 0.0 copy-start.1
  0.6 0.0 copy-start.2
  0.7 2.2 %shard_map.87 = bf16[16,15,16,128]{3,2,1,0:T(8,128)(2,1)} custom-call(bf16[3,16,5120]{2,1,0:T(8,128)(2,1)} %bitcast.5, bf16[3,16,5120]{2,1,0:T(8,128)(2,1)} %bitcast.6), custom_call_target="tpu_custom_call" | custom-call | bytes 1966080 | tf_op jit(solution)/shard_map/pallas_call | solution.py:98
  2.8 7.4 %all-to-all-start = ((bf16[16,15,16,128]{3,2,1,0:T(8,128)(2,1)}), bf16[16,15,16,128]{3,2,1,0:T(8,128)(2,1)S(1)}, u32[]{:S(2)}, u32[]{:S(2)}) async-start(bf16[16,15,16,128]{3,2,1,0:T(8,128)(2,1)} %shard_map.87), calls=%async_computation | async-start | bytes 1966080 | tf_op jit(solution)/shard_map/all_to_all | solution.py:397
  10.2 0.7 %add_select_fusion = s32[5,64]{1,0:T(8,128)S(1)} fusion(s32[5,64]{1,0:T(8,128)} %param.11, s32[]{:T(128)S(6)} %mul_shard_map.3, s32[]{:T(128)S(6)} %mul.8), kind=kLoop, calls=%fused_computation.4 | loop fusion | flops 2880 | bytes 2568 | tf_op jit(solution)/shard_map/jit(remainder)/select_n | solution.py:398
  10.9 0.1 reshape.11.index_ref
  11.1 21.2 %all-to-all-done.recv_ref = bf16[16,15,16,128]{3,2,1,0:T(8,128)(2,1)S(1)} async-done(((bf16[16,15,16,128]{3,2,1,0:T(8,128)(2,1)}), bf16[16,15,16,128]{3,2,1,0:T(8,128)(2,1)S(1)}, u32[]{:S(2)}, u32[]{:S(2)}) %all-to-all-start) | async-done | bytes 983072 | tf_op jit(solution)/shard_map/all_to_all | solution.py:397
  32.2 0.6 shard_map.88.own_ref.down
  32.8 0.1 collective-permute-start.1
  32.9 2.0 %collective-permute-start = (bf16[5,192,256]{2,1,0:T(8,128)(2,1)S(1)}, bf16[5,192,256]{2,1,0:T(8,128)(2,1)S(1)}, u32[]{:S(2)}, u32[]{:S(2)}) collective-permute-start(bf16[5,192,256]{2,1,0:T(8,128)(2,1)S(1)} %shard_map.88.own_ref.down), channel_id=1, source_target_pairs={{0,15},{1,2},{2,1},{3,4},{4,3},{5,6},{6,5},{7,8},{8,7},{9,10},{10,... | collective-permute-start | bytes 1474568 | tf_op jit(solution)/shard_map/ppermute | solution.py:360
  34.9 0.7 %fusion.3 = s32[5,14]{1,0:T(8,128)S(1)} fusion(s32[5,14]{1,0:T(8,128)} %param.10, s32[]{:T(128)S(6)} %select_n.53, s32[]{:T(128)S(6)} %axis_index.12), kind=kLoop, calls=%fused_computation.13 | loop fusion | flops 2170 | bytes 568 | tf_op jit(solution)/shard_map/add | solution.py:376
  35.6 0.2 select_reduce_fusion.1.block_ref
  35.8 0.0 copy-start
  35.8 3.0 %copy-done = bf16[5,14,192,192]{3,2,1,0:T(8,128)(2,1)S(1)} copy-done((bf16[5,14,192,192]{3,2,1,0:T(8,128)(2,1)S(1)}, bf16[5,14,192,192]{3,2,1,0:T(8,128)(2,1)}, u32[]{:S(2)}) %copy-start) | copy-done | bytes 5160984
  38.8 2.2 %shard_map.86 = (bf16[5,192,1920]{2,1,0:T(8,128)(2,1)S(1)}, bf16[5,192,960]{2,1,0:T(8,128)(2,1)S(1)}) custom-call(s32[5,15]{1,0:T(8,128)S(1)} %select_reduce_fusion.1.block_ref, bf16[5,14,192,192]{3,2,1,0:T(8,128)(2,1)S(1)} %copy-done), custom_call_target="tpu_custom_call" | custom-call | bytes 10321920 | tf_op jit(solution)/shard_map/pallas_call | solution.py:189
  40.9 0.0 copy-done.1
  41.0 0.0 copy-done.2
  41.0 0.2 select_reduce_fusion
  41.1 0.6 shard_map.89.force_ref
  41.7 0.0 collective-permute-done.1.partner_ref.dnear
  41.8 2.0 %shard_map.90 = (f32[5,192,256]{2,1,0:T(8,128)S(1)}, bf16[5,192,256]{2,1,0:T(8,128)(2,1)S(1)}) custom-call(bf16[5,192,1920]{2,1,0:T(8,128)(2,1)S(1)} %get-tuple-element.12.phi_ref, bf16[5,192,256]{2,1,0:T(8,128)(2,1)S(1)} %shard_map.88.own_ref.down, bf16[5,192,256]{2,1,0:T(8,128)(2,1)S(1)} %collective-permute-done.1.partner_ref.dnear, ...), custom_call_target="tpu_custom_call" | custom-call | flops 943718400 | bytes 3686400 | tf_op jit(solution)/shard_map/pallas_call | solution.py:221
  43.8 2.9 %collective-permute-done.far_ref.dfar = bf16[5,192,256]{2,1,0:T(8,128)(2,1)S(1)} collective-permute-done((bf16[5,192,256]{2,1,0:T(8,128)(2,1)S(1)}, bf16[5,192,256]{2,1,0:T(8,128)(2,1)S(1)}, u32[]{:S(2)}, u32[]{:S(2)}) %collective-permute-start) | collective-permute-done | bytes 491552 | tf_op jit(solution)/shard_map/ppermute | solution.py:360
  46.7 0.7 %shard_map.91 = (bf16[5,192,256]{2,1,0:T(8,128)(2,1)S(1)}, bf16[5,192,256]{2,1,0:T(8,128)(2,1)S(1)}) custom-call(bf16[5,192,960]{2,1,0:T(8,128)(2,1)S(1)} %get-tuple-element.11.phi_ref, bf16[5,192,256]{2,1,0:T(8,128)(2,1)S(1)} %collective-permute-done.far_ref.dfar, f32[5,192,256]{2,1,0:T(8,128)S(1)} %get-tuple-element.13.base_ref, f32[1,256]{1,0:T(1,128)S(1)} %bitcast.4), custom_call_target="tpu_custom_call" | custom-call | flops 471859200 | bytes 1843200 | tf_op jit(solution)/shard_map/pallas_call | solution.py:246
  47.4 0.3 collective-permute-start.2
  47.7 1.6 %collective-permute-start.3 = (bf16[5,192,256]{2,1,0:T(8,128)(2,1)S(1)}, bf16[5,192,256]{2,1,0:T(8,128)(2,1)S(1)}, u32[]{:S(2)}, u32[]{:S(2)}) collective-permute-start(bf16[5,192,256]{2,1,0:T(8,128)(2,1)S(1)} %get-tuple-element.16.rown), channel_id=1, source_target_pairs={{0,15},{1,2},{2,1},{3,4},{4,3},{5,6},{6,5},{7,8},{8,7},{9,10},{10,... | collective-permute-start | bytes 1474568 | tf_op jit(solution)/shard_map/ppermute | solution.py:360
  49.3 0.0 collective-permute-done.2.rnear
  49.3 5.0 %shard_map.92 = (bf16[5,14,192,192]{3,2,1,0:T(8,128)(2,1)}, bf16[5,192,256]{2,1,0:T(8,128)(2,1)}, f32[5,5,192,192]{3,2,1,0:T(8,128)S(1)}) custom-call(s32[5,15]{1,0:T(8,128)S(1)} %select_reduce_fusion.1.block_ref, bf16[5,192,256]{2,1,0:T(8,128)(2,1)S(1)} %get-tuple-element.14.wres_ref, bf16[5,192,256]{2,1,0:T(8,128)(2,1)S(1)} %get-tuple-element.15.wdisp_ref, ...), custom_call_target="tpu_custom_call" | custom-call | flops 2359296000 | bytes 3686400 | tf_op jit(solution)/shard_map/pallas_call | solution.py:325
  54.3 6.8 %collective-permute-done.3.rfar = bf16[5,192,256]{2,1,0:T(8,128)(2,1)S(1)} collective-permute-done((bf16[5,192,256]{2,1,0:T(8,128)(2,1)S(1)}, bf16[5,192,256]{2,1,0:T(8,128)(2,1)S(1)}, u32[]{:S(2)}, u32[]{:S(2)}) %collective-permute-start.3) | collective-permute-done | bytes 491552 | tf_op jit(solution)/shard_map/ppermute | solution.py:360
  61.2 2.6 %shard_map.93 = bf16[5,14,192,192]{3,2,1,0:T(8,128)(2,1)} custom-call(s32[5,15]{1,0:T(8,128)S(1)} %select_reduce_fusion.1.block_ref, bf16[5,192,256]{2,1,0:T(8,128)(2,1)S(1)} %get-tuple-element.15.wdisp_ref, bf16[5,192,256]{2,1,0:T(8,128)(2,1)S(1)} %collective-permute-done.3.rfar, ...), custom_call_target="tpu_custom_call", output_to_operand_aliasing={{}: (4, {})} | custom-call | flops 471859200 | bytes 5529600 | tf_op jit(solution)/shard_map/pallas_call | solution.py:340
Async XLA Ops:
  0.6 40.3 %copy-start.1 = (f32[256]{0:T(256)S(1)}, f32[256]{0:T(256)}, u32[]{:S(2)}) copy-start(f32[256]{0:T(256)} %param.13) | copy-start | bytes 3076
  0.6 40.3 %copy-start.2 = (s32[256]{0:T(256)S(1)}, s32[256]{0:T(256)}, u32[]{:S(2)}) copy-start(s32[256]{0:T(256)} %param.12) | copy-start | bytes 3076
  2.8 29.4 %all-to-all-start = ((bf16[16,15,16,128]{3,2,1,0:T(8,128)(2,1)}), bf16[16,15,16,128]{3,2,1,0:T(8,128)(2,1)S(1)}, u32[]{:S(2)}, u32[]{:S(2)}) async-start(bf16[16,15,16,128]{3,2,1,0:T(8,128)(2,1)} %shard_map.87), calls=%async_computation | async-start | bytes 1966080 | tf_op jit(solution)/shard_map/all_to_all | solution.py:397
  32.8 8.9 %collective-permute-start.1 = (bf16[5,192,256]{2,1,0:T(8,128)(2,1)S(1)}, bf16[5,192,256]{2,1,0:T(8,128)(2,1)S(1)}, u32[]{:S(2)}, u32[]{:S(2)}) collective-permute-start(bf16[5,192,256]{2,1,0:T(8,128)(2,1)S(1)} %shard_map.88.own_ref.down), channel_id=1, source_target_pairs={{0,1},{1,0},{2,3},{3,2},{4,5},{5,4},{6,7},{7,6},{8,9},{9,8},{10,11... | collective-permute-start | bytes 1474568 | tf_op jit(solution)/shard_map/ppermute | solution.py:354
  32.9 13.8 %collective-permute-start = (bf16[5,192,256]{2,1,0:T(8,128)(2,1)S(1)}, bf16[5,192,256]{2,1,0:T(8,128)(2,1)S(1)}, u32[]{:S(2)}, u32[]{:S(2)}) collective-permute-start(bf16[5,192,256]{2,1,0:T(8,128)(2,1)S(1)} %shard_map.88.own_ref.down), channel_id=1, source_target_pairs={{0,15},{1,2},{2,1},{3,4},{4,3},{5,6},{6,5},{7,8},{8,7},{9,10},{10,... | collective-permute-start | bytes 1474568 | tf_op jit(solution)/shard_map/ppermute | solution.py:360
  35.8 3.0 %copy-start = (bf16[5,14,192,192]{3,2,1,0:T(8,128)(2,1)S(1)}, bf16[5,14,192,192]{3,2,1,0:T(8,128)(2,1)}, u32[]{:S(2)}) copy-start(bf16[5,14,192,192]{3,2,1,0:T(8,128)(2,1)} %phi_ref.1) | copy-start | bytes 15482884
  47.4 1.9 %collective-permute-start.2 = (bf16[5,192,256]{2,1,0:T(8,128)(2,1)S(1)}, bf16[5,192,256]{2,1,0:T(8,128)(2,1)S(1)}, u32[]{:S(2)}, u32[]{:S(2)}) collective-permute-start(bf16[5,192,256]{2,1,0:T(8,128)(2,1)S(1)} %get-tuple-element.16.rown), channel_id=1, source_target_pairs={{0,1},{1,0},{2,3},{3,2},{4,5},{5,4},{6,7},{7,6},{8,9},{9,8},{10,11... | collective-permute-start | bytes 1474568 | tf_op jit(solution)/shard_map/ppermute | solution.py:354
  47.7 13.5 %collective-permute-start.3 = (bf16[5,192,256]{2,1,0:T(8,128)(2,1)S(1)}, bf16[5,192,256]{2,1,0:T(8,128)(2,1)S(1)}, u32[]{:S(2)}, u32[]{:S(2)}) collective-permute-start(bf16[5,192,256]{2,1,0:T(8,128)(2,1)S(1)} %get-tuple-element.16.rown), channel_id=1, source_target_pairs={{0,15},{1,2},{2,1},{3,4},{4,3},{5,6},{6,5},{7,8},{8,7},{9,10},{10,... | collective-permute-start | bytes 1474568 | tf_op jit(solution)/shard_map/ppermute | solution.py:360

commit v5 on v4

--- a/solution.py
+++ b/solution.py
@@ -146,89 +146,227 @@
     return picked(wholes, half_hot, tiles, flat(recv_ref, half))
 
 
-def gather_kernel(field, index_ref, recv_ref, out_ref):
+def put(out_ref, index_ref, recv_ref, field, dtype):
     clusters, dof, _ = out_ref.shape
     atoms = dof // 3
-    hots = one_hots(index_ref, (recv_ref.shape[1] - 3) // 6)
+    hots = one_hots(index_ref, recv_ref.shape[1] // (6 if recv_ref.shape[1] % 3 == 0 else 3))
     for a in range(3):
-        got = component(recv_ref, hots, field, a).astype(BF16)
+        got = component(recv_ref, hots, field, a).astype(dtype)
         for c in range(clusters):
             out_ref[c, a * atoms : (a + 1) * atoms] = got[c * atoms : (c + 1) * atoms]
 
 
-def gather(index, recv, field, clusters, atoms):
-    configs = recv.shape[0] * recv.shape[2]
-    return pl.pallas_call(
-        functools.partial(gather_kernel, field),
-        in_specs=in_vmem(2),
-        out_specs=in_vmem(1)[0],
-        out_shape=shape((clusters, 3 * atoms, configs)),
+def gather_and_pass_kernel(route_ref, index_ref, recv_ref, out_ref, pass_ref):
+    for i in range(pass_ref.shape[0]):
+        pass_ref[i] = recv_ref[route_ref[3, i], : pass_ref.shape[1]]
+    put(out_ref, index_ref, recv_ref, 0, BF16)
+
+
+def disp_tiles(recv):
+    return 3 * ((recv.shape[1] - 3) // 6) + 2
+
+
+def gather_and_pass(route, index, recv, clusters, atoms):
+    width, _, configs, _ = recv.shape
+    return pl.pallas_call(
+        gather_and_pass_kernel,
+        in_specs=[in_smem()] + in_vmem(2),
+        out_specs=in_vmem(2),
+        out_shape=[
+            shape((clusters, 3 * atoms, width * configs)),
+            shape((route.shape[1], disp_tiles(recv), configs, 128)),
+        ],
         compiler_params=params(8),
         cost_estimate=cost(recv.size * index.size, 3 * recv.size),
-    )(index, recv)
-
-
-def order_kernel(block_ref, phi_ref, near_ref, far_ref):
-    c = pl.program_id(0)
-    blocks, dof = phi_ref.shape[1:3]
-    near = near_ref.shape[2] // dof
-
-    def block(n):
-        k = block_ref[c, n]
-        got = phi_ref[0, jnp.minimum(k, blocks - 1)]
-        return jnp.where(k < blocks, got, jnp.zeros_like(got))
-
-    near_ref[0] = jnp.concatenate([block(n) for n in range(near)], axis=1)
-    far_ref[0] = jnp.concatenate([block(near + n) for n in range(near // 2)], axis=1)
+    )(route, index, recv)
+
+
+def pick_kernel(route_ref, send_ref, *rest):
+    outs, sem = rest[:-1], rest[-1]
+    copies = [
+        pltpu.make_async_copy(
+            send_ref.at[route_ref[0, j], pl.ds(0, out.shape[0])], out, sem.at[j]
+        )
+        for j, out in enumerate(outs)
+    ]
+    for copy in copies:
+        copy.start()
+    for copy in copies:
+        copy.wait()
+
+
+def pick(route, send):
+    reach = route.shape[1]
+    _, _, configs, _ = send.shape
+    return pl.pallas_call(
+        pick_kernel,
+        in_specs=[in_smem(), pl.BlockSpec(memory_space=pltpu.HBM)],
+        out_specs=in_vmem(reach),
+        out_shape=[shape((disp_tiles(send), configs, 128))] * reach,
+        scratch_shapes=[pltpu.SemaphoreType.DMA((reach,))],
+        compiler_params=params(60),
+        cost_estimate=cost(0, send.size),
+    )(route, pltpu.with_memory_space_constraint(send, pltpu.HBM))
+
+
+def masked(block_ref, block, c, n, blocks):
+    return jnp.where(block_ref[c, n] < blocks, block, jnp.zeros_like(block))
+
+
+def order_kernel(block_ref, phi_ref, out_ref, held, sem):
+    clusters, blocks = phi_ref.shape[:2]
+    layer = held.shape[1]
+
+    def fetch(c, n):
+        k = jnp.minimum(block_ref[c, 2 * layer + n], blocks - 1)
+        return pltpu.make_async_copy(phi_ref.at[c, k], held.at[c, n], sem.at[c, n])
+
+    for c in range(clusters):
+        for n in range(layer):
+            fetch(c, n).start()
+    for c in range(clusters):
+        for n in range(layer):
+            fetch(c, n).wait()
+        row = [masked(block_ref, held[c, n], c, 2 * layer + n, blocks) for n in range(layer)]
+        out_ref[c] = jnp.concatenate(row, axis=1)
 
 
 def ordered(block_of, phi):
-    clusters, blocks, dof, _ = phi.shape
+    clusters, _, dof, _ = phi.shape
     layer = block_of.shape[1] // 3
-    widths = (2 * layer * dof, layer * dof)
     return pl.pallas_call(
         order_kernel,
-        grid_spec=pltpu.PrefetchScalarGridSpec(
-            num_scalar_prefetch=1,
-            grid=(clusters,),
-            in_specs=[pl.BlockSpec((1, blocks, dof, dof), lambda c, block: (c, 0, 0, 0))],
-            out_specs=[pl.BlockSpec((1, dof, w), lambda c, block: (c, 0, 0)) for w in widths],
-        ),
-        out_shape=[shape((clusters, dof, w)) for w in widths],
-        compiler_params=params(40),
-        cost_estimate=cost(0, 4 * phi.size),
-    )(block_of, phi)
-
-
-def near_harmonic_kernel(phi_ref, own_ref, partner_ref, force_ref, wt_ref, out_ref, wdisp_ref):
-    c = pl.program_id(0)
-    depth = phi_ref.shape[2] // 2
-    configs = own_ref.shape[2]
-    total = force_ref[0].astype(F32)
-    for i, ref in enumerate((own_ref, partner_ref)):
-        left = phi_ref[0, :, depth * i : depth * (i + 1)]
-        total = total + jnp.dot(
-            left, ref[...].reshape(depth, configs), preferred_element_type=F32
-        )
-    out_ref[0] = total
-    wdisp_ref[0] = (own_ref[c].astype(F32) * (0.5 * wt_ref[...])).astype(BF16)
-
-
-def near_harmonic(phi_near, own, partner, force, wt):
-    clusters, dof, width = phi_near.shape
-    configs = own.shape[2]
-    one = pl.BlockSpec((1, dof, configs), lambda c: (c, 0, 0))
-    return pl.pallas_call(
-        near_harmonic_kernel,
-        grid=(clusters,),
-        in_specs=[pl.BlockSpec((1, dof, width), lambda c: (c, 0, 0))]
-        + in_vmem(2)
-        + [one, pl.BlockSpec((1, configs), lambda c: (0, 0))],
-        out_specs=[one, one],
-        out_shape=[shape(own.shape, F32), shape(own.shape)],
-        compiler_params=params(16),
-        cost_estimate=cost(2 * phi_near.size * configs, 2 * phi_near.size),
-    )(phi_near, own, partner, force, wt)
+        in_specs=[in_smem(), pl.BlockSpec(memory_space=pltpu.HBM)],
+        out_specs=in_vmem(1)[0],
+        out_shape=shape((clusters, dof, layer * dof)),
+        scratch_shapes=[
+            VMEM((clusters, layer, dof, dof), BF16),
+            pltpu.SemaphoreType.DMA((clusters, layer)),
+        ],
+        compiler_params=params(60),
+        cost_estimate=cost(0, 2 * phi.size),
+    )(block_of, pltpu.with_memory_space_constraint(phi, pltpu.HBM))
+
+
+def stacked(block_ref, held, n, blocks):
+    clusters = held.shape[0]
+    return jnp.concatenate(
+        [masked(block_ref, held[c], c, n, blocks) for c in range(clusters)], axis=0
+    )
+
+
+def fetcher(block_ref, phi_ref, sem):
+    def fetch(n, c, place):
+        k = jnp.minimum(block_ref[c, n], phi_ref.shape[1] - 1)
+        return pltpu.make_async_copy(phi_ref.at[c, k], place.at[c], sem.at[n, c])
+
+    return fetch
+
+
+def own_harmonic(block_ref, blocks, own_ref, held, out_ref, ready):
+    for n in range(own_ref.shape[0]):
+        ready(n)
+        left = stacked(block_ref, held.at[n], n, blocks)
+        got = jnp.dot(left, own_ref[n], preferred_element_type=F32)
+        out_ref[...] = out_ref[...] + got.reshape(out_ref.shape)
+
+
+def own_kernel(block_ref, phi_ref, own_ref, wt_ref, *rest, dense):
+    if dense:
+        route_ref, index_ref, index_far_ref, recv_ref, *rest = rest
+        reach = route_ref.shape[1]
+        pieces, rest = rest[:reach], rest[reach:]
+        out_ref, wdisp_ref, partner_ref, direct_ref, held, sem, frame, frame_sem = rest
+        copies = [
+            pltpu.make_async_copy(
+                piece, frame.at[lax.rem(route_ref[1, j], reach)], frame_sem.at[j]
+            )
+            for j, piece in enumerate(pieces)
+        ]
+    else:
+        force_ref, out_ref, wdisp_ref, partner_ref, held, sem = rest
+        copies = []
+    layer = own_ref.shape[0]
+    clusters, blocks = phi_ref.shape[:2]
+    fetch = fetcher(block_ref, phi_ref, sem)
+    for n in range(2 * layer):
+        for c in range(clusters):
+            place = held.at[n] if n < layer else partner_ref.at[n - layer]
+            fetch(n, c, place).start()
+    for copy in copies:
+        copy.start()
+    wt = 0.5 * wt_ref[...]
+    for c in range(clusters):
+        wdisp_ref[c] = (own_ref[c].astype(F32) * wt).astype(BF16)
+    if dense:
+        put(out_ref, index_ref, recv_ref, 1, F32)
+    else:
+        out_ref[...] = force_ref[...].astype(F32)
+
+    def ready(n):
+        for c in range(clusters):
+            fetch(n, c, held.at[n] if n < layer else partner_ref.at[n - layer]).wait()
+
+    own_harmonic(block_ref, blocks, own_ref, held, out_ref, ready)
+    for copy in copies:
+        copy.wait()
+    if dense:
+        put(direct_ref, index_far_ref, frame, 0, BF16)
+    for n in range(layer, 2 * layer):
+        ready(n)
+
+
+def own_part(block_of, phi, own, wt, dense, extra):
+    clusters, _, dof, _ = phi.shape
+    layer, _, configs = own.shape
+    hbm = pl.BlockSpec(memory_space=pltpu.HBM)
+    in_specs = [in_smem(), hbm] + in_vmem(2)
+    out_shape = [shape(own.shape, F32), shape(own.shape), shape((layer, clusters, dof, dof))]
+    scratch = [
+        VMEM((layer, clusters, dof, dof), BF16),
+        pltpu.SemaphoreType.DMA((2 * layer, clusters)),
+    ]
+    if dense:
+        pieces = extra[4:]
+        tiles, few, _ = pieces[0].shape
+        in_specs += [in_smem()] + in_vmem(3) + [hbm] * len(pieces)
+        out_shape.append(shape((clusters, dof, len(pieces) * few)))
+        scratch += [
+            VMEM((len(pieces), tiles, few, 128), BF16),
+            pltpu.SemaphoreType.DMA((len(pieces),)),
+        ]
+        pieces = [pltpu.with_memory_space_constraint(p, pltpu.HBM) for p in pieces]
+        extra = (*extra[:4], *pieces)
+    else:
+        in_specs += in_vmem(1)
+    return pl.pallas_call(
+        functools.partial(own_kernel, dense=dense),
+        in_specs=in_specs,
+        out_specs=in_vmem(len(out_shape)),
+        out_shape=out_shape,
+        scratch_shapes=scratch,
+        compiler_params=params(12),
+        cost_estimate=cost(phi.size * configs, 2 * phi.size),
+    )(block_of, pltpu.with_memory_space_constraint(phi, pltpu.HBM), own, wt, *extra)
+
+
+def partner_kernel(blocks, block_ref, phi_ref, partner_ref, base_ref, out_ref):
+    layer = partner_ref.shape[0]
+    for n in range(layer):
+        left = stacked(block_ref, phi_ref.at[n], layer + n, blocks)
+        got = jnp.dot(left, partner_ref[n], preferred_element_type=F32).reshape(out_ref.shape)
+        out_ref[...] = (base_ref if n == 0 else out_ref)[...] + got
+
+
+def partner_part(blocks, block_of, phi_partner, partner, base):
+    return pl.pallas_call(
+        functools.partial(partner_kernel, blocks),
+        in_specs=[in_smem()] + in_vmem(3),
+        out_specs=in_vmem(1)[0],
+        out_shape=shape(base.shape, F32),
+        compiler_params=params(8),
+        cost_estimate=cost(2 * phi_partner.size * base.shape[2], 2 * phi_partner.size),
+    )(block_of, phi_partner, partner, base)
 
 
 def residual_kernel(phi_ref, far_ref, base_ref, wt_ref, res_ref, wres_ref):
@@ -251,6 +389,38 @@
         compiler_params=params(8),
         cost_estimate=cost(2 * phi_far.size * far.shape[2], 2 * phi_far.size),
     )(phi_far, far, base, wt)
+
+
+def merged_residual_kernel(
+    route_ref, index_ref, recv_ref, direct_ref, phi_ref, base_ref, wt_ref, res_ref, wres_ref,
+    far_ref
+):
+    clusters, dof, configs = res_ref.shape
+    atoms = dof // 3
+    half = configs // 2
+    first = route_ref[1, 0] < route_ref.shape[1]
+    hots = one_hots(index_ref, (recv_ref.shape[1] - 2) // 3)
+    for a in range(3):
+        rest = component(recv_ref, hots, 0, a).astype(BF16)
+        for c in range(clusters):
+            rows = pl.ds(a * atoms, atoms)
+            x, y = direct_ref[c, rows], rest[c * atoms : (c + 1) * atoms]
+            far_ref[c, rows, :half] = jnp.where(first, x, y)
+            far_ref[c, rows, half:] = jnp.where(first, y, x)
+    residual_kernel(phi_ref, far_ref, base_ref, wt_ref, res_ref, wres_ref)
+
+
+def merged_residual(route, index, recv, near_half, phi_far, base, wt):
+    return pl.pallas_call(
+        merged_residual_kernel,
+        in_specs=[in_smem()] + in_vmem(6),
+        out_specs=in_vmem(3),
+        out_shape=[shape(base.shape)] * 3,
+        compiler_params=params(8),
+        cost_estimate=cost(
+            2 * phi_far.size * base.shape[2] + recv.size * index.size, 2 * phi_far.size
+        ),
+    )(route, index, recv, near_half, phi_far, base, wt)
 
 
 def put_blocks(block_ref, held, out_ref, sem, first):
@@ -360,6 +530,20 @@
     return lax.ppermute(block, "cx", pairs)
 
 
+def far_of(i, count):
+    return (i + 2 * (i % 2) - 1) % count
+
+
+def routes(position, width, reach):
+    q = jnp.arange(reach, dtype=jnp.int32)[None, :]
+    row = jnp.arange(4, dtype=jnp.int32)[:, None]
+    block = position // reach * reach
+    far_block = far_of(position, width) // reach * reach
+    peer = position ^ q
+    rest = (jnp.where(row == 2, block, far_block) + reach + q) % width
+    return jnp.where(row == 0, far_of(peer, width), jnp.where(row == 1, peer, rest))
+
+
 def arrange(field, atom_map):
     taken = jnp.take(field, atom_map.reshape(-1), axis=2)
     taken = taken.reshape(field.shape[0], 3, atom_map.shape[0], atom_map.shape[1])
@@ -390,24 +574,41 @@
     per = displacements.shape[2] // width
     block_of, wt = tables(neighbours, config_order, weights, layer, position, width)
     atom_local = cluster_atoms - position * per
-    if displacements.shape[0] % 16 == 0 and per % 128 == 64 and width % 2 == 0:
+    reach = width // 2
+    dense = displacements.shape[0] % 16 == 0 and per % 128 == 64
+    dense = dense and reach & (reach - 1) == 0 and displacements.shape[0] * reach % 128 == 0
+    phi_far = ordered(block_of, phi)
+    if dense:
         send = pack(
             jnp.transpose(displacements, (1, 0, 2)), jnp.transpose(forces, (1, 0, 2)), width
         )
         recv = lax.all_to_all(send, "cx", split_axis=0, concat_axis=0, tiled=True)
-        index = ((atom_local - 64 * (position % 2) + per) % per).reshape(-1, 1)
-        disp = gather(index, recv, 0, layer, atoms)
-        force = gather(index, recv, 1, layer, atoms)
+        index = (atom_local - 64 * (position % 2) + per) % per
+        route = routes(position, width, reach)
+        index_far = swap_far(index).reshape(-1, 1)
+        index = index.reshape(-1, 1)
+        pieces = list(pick(route, send))
+        for j in range(1, reach):
+            pieces[j] = lax.ppermute(pieces[j], "cx", [(i, i ^ j) for i in range(width)])
+        disp, passed = gather_and_pass(route, index, recv, layer, atoms)
+        recv_far = swap_far(passed)
+        extra = (route, index, index_far, recv, *pieces)
     else:
         disp, force = (
             arrange(lax.all_to_all(x, "cx", split_axis=2, concat_axis=0, tiled=True), atom_local)
             for x in (displacements, forces)
         )
-    phi_near, phi_far = ordered(block_of, phi)
-    disp_far = swap_far(disp)
+        disp_far = swap_far(disp)
+        extra = (force,)
     disp_near = swap_near(disp)
-    base, wdisp = near_harmonic(phi_near, disp, disp_near, force, wt)
-    res, wres = residual_of(phi_far, disp_far, base, wt)
+    base, wdisp, phi_partner, *near_half = own_part(block_of, phi, disp, wt, dense, extra)
+    base = partner_part(phi.shape[1], block_of, phi_partner, disp_near, base)
+    if dense:
+        res, wres, disp_far = merged_residual(
+            route, index_far, recv_far, near_half[0], phi_far, base, wt
+        )
+    else:
+        res, wres = residual_of(phi_far, disp_far, base, wt)
     res_far = swap_far(res)
     res_near = swap_near(res)
     gradient, residual, far = near_gradient(

time: 65 us -> 75 us (1.15)
  starting transfers between devices: 11.3 us -> 23 us
  waiting for transfers between devices: 31 us -> 19.6 us
  Pallas kernels: 15.9 us -> 25.8 us
  other arithmetic: 1.77 us -> 3.74 us
  local copies, waits for them, and re-layouts: 3.13 us -> 1.54 us
    ppermute x0 -> x7, starting transfers between devices: none -> 10.8 us  [shards(): lax.ppermute(pieces[j], 'cx', [(i, i ^ j) for i in range(width)])]
    pallas_call x5 -> x6, Pallas kernels: 6.07 us -> 15.9 us  [the longest x1 4.9 us: own_part(): pl.pallas_call(functools.partial(own_kernel, dense=dense), in_specs=in_sp...]
    all_to_all x1, waiting for transfers between devices: 21.2 us -> 11.9 us  [shards(): recv = lax.all_to_all(send, 'cx', split_axis=0, concat_axis=0, tiled=True)]
    ppermute x2 -> x3, waiting for transfers between devices: 9.73 us -> 7.03 us  [swap_far(): return lax.ppermute(block, 'cx', pairs)]
    unnamed x6 -> x22, local copies, waits for them, and re-layouts: 2.98 us -> 1.24 us
    ppermute x2 -> x3, starting transfers between devices: 3.59 us -> 4.21 us  [swap_far(): return lax.ppermute(block, 'cx', pairs)]
  transfers between devices with their start and end apart: 5 -> 13, of which waited for: 3 -> 3; matrix products, arithmetic and copies ran while one was open for 3% -> 5% of each run, Pallas kernels for 15% -> 26%
where the time goes in v5:
time: 75 us; the launch traced here: 74.5 us
  Pallas kernels  25.8 us (34%)
  starting transfers between devices  23 us (31%)
  waiting for transfers between devices  19.6 us (26%)
  other arithmetic  3.74 us (5%)
  local copies, waits for them, and re-layouts  1.54 us (2%)
  between operations  0.87 us (1%)
    all_to_all x1, waiting for transfers between devices, shards(): recv = lax.all_to_all(send, 'cx', split_axis=0, concat_axis=0, tiled=True)  11.9 us
    ppermute x7, starting transfers between devices, shards(): lax.ppermute(pieces[j], 'cx', [(i, i ^ j) for i in range(width)])  10.8 us
    all_to_all x1, starting transfers between devices, shards(): recv = lax.all_to_all(send, 'cx', split_axis=0, concat_axis=0, tiled=True)  7.35 us
    ppermute x3, waiting for transfers between devices, swap_far(): return lax.ppermute(block, 'cx', pairs)  7.03 us
    pallas_call x1, Pallas kernels, near_gradient(): pl.pallas_call(near_gradient_kernel, in_specs=[in_smem()] + in_vmem(7), o...  5 us
    pallas_call x1, Pallas kernels, own_part(): pl.pallas_call(functools.partial(own_kernel, dense=dense), in_specs=in_sp...  4.9 us
    ppermute x3, starting transfers between devices, swap_far(): return lax.ppermute(block, 'cx', pairs)  4.21 us
    pallas_call x1, Pallas kernels, ordered(): pl.pallas_call(order_kernel, in_specs=[in_smem(), pl.BlockSpec(memory_spa...  4.2 us
  transfers between devices with their start and end apart: 13, of which 3 were waited for; matrix products, arithmetic and copies ran while one was open for 5% of the time, Pallas kernels for 26%

profile of v5, /device:TPU:1, one launch (start us, length us, event | category | flops | bytes accessed | tf_op | source)
XLA Modules:
  0.0 74.5 jit_solution(3153452262389495605)
XLA Ops:
  0.6 2.2 %shard_map.86.send_ref = bf16[16,15,16,128]{3,2,1,0:T(8,128)(2,1)} custom-call(bf16[3,16,5120]{2,1,0:T(8,128)(2,1)} %bitcast.5, bf16[3,16,5120]{2,1,0:T(8,128)(2,1)} %bitcast.6), custom_call_target="tpu_custom_call" | custom-call | bytes 1966080 | tf_op jit(solution)/shard_map/pallas_call | solution.py:98
  2.8 7.4 %all-to-all-start = ((bf16[16,15,16,128]{3,2,1,0:T(8,128)(2,1)}), bf16[16,15,16,128]{3,2,1,0:T(8,128)(2,1)S(1)}, u32[]{:S(2)}, u32[]{:S(2)}) async-start(bf16[16,15,16,128]{3,2,1,0:T(8,128)(2,1)} %shard_map.86.send_ref), calls=%async_computation | async-start | bytes 1966080 | tf_op jit(solution)/shard_map/all_to_all | solution.py:585
  10.2 0.7 add_select_fusion
  10.9 1.7 %collective-permute-start = (s32[5,64]{1,0:T(8,128)S(1)}, s32[5,64]{1,0:T(8,128)S(1)}, u32[]{:S(2)}, u32[]{:S(2)}) collective-permute-start(s32[5,64]{1,0:T(8,128)S(1)} %add_select_fusion), channel_id=1, source_target_pairs={{0,15},{1,2},{2,1},{3,4},{4,3},{5,6},{6,5},{7,8},{8,7},{9,10},{10,... | collective-permute-start | bytes 3848 | tf_op jit(solution)/shard_map/ppermute | solution.py:530
  12.6 0.6 fusion.7.route_ref.rest_0_
  13.2 2.4 %shard_map.88 = (bf16[8,16,128]{2,1,0:T(8,128)(2,1)}, bf16[8,16,128]{2,1,0:T(8,128)(2,1)}, bf16[8,16,128]{2,1,0:T(8,128)(2,1)}, bf16[8,16,128]{2,1,0:T(8,128)(2,...) custom-call(s32[4,8]{1,0:T(4,128)} %fusion.7.route_ref.rest_0_, ...), custom_call_target="tpu_custom_call" | custom-call | bytes 491520 | tf_op jit(solution)/shard_map/pallas_call | solution.py:201
  15.6 2.9 %collective-permute-start.2 = (bf16[8,16,128]{2,1,0:T(8,128)(2,1)}, bf16[8,16,128]{2,1,0:T(8,128)(2,1)S(1)}, u32[]{:S(2)}, u32[]{:S(2)}) collective-permute-start(bf16[8,16,128]{2,1,0:T(8,128)(2,1)} %get-tuple-element.25), channel_id=1, source_target_pairs={{0,1},{1,0},{2,3},{3,2},{4,5},{5,4},{6,7},{7,6},{8,9},{9,8},{10,11... | collective-permute-start | bytes 98312 | tf_op jit(solution)/shard_map/ppermute | solution.py:592
  18.5 0.0 collective-permute-start.3
  18.5 1.7 %collective-permute-start.4 = (bf16[8,16,128]{2,1,0:T(8,128)(2,1)}, bf16[8,16,128]{2,1,0:T(8,128)(2,1)S(1)}, u32[]{:S(2)}, u32[]{:S(2)}) collective-permute-start(bf16[8,16,128]{2,1,0:T(8,128)(2,1)} %get-tuple-element.27), channel_id=1, source_target_pairs={{0,3},{1,2},{2,1},{3,0},{4,7},{5,6},{6,5},{7,4},{8,11},{9,10},{10,... | collective-permute-start | bytes 98312 | tf_op jit(solution)/shard_map/ppermute | solution.py:592
  20.2 0.1 reshape.81.index_ref.rest_1_
  20.4 11.9 %all-to-all-done.recv_ref.rest_3_ = bf16[16,15,16,128]{3,2,1,0:T(8,128)(2,1)S(1)} async-done(((bf16[16,15,16,128]{3,2,1,0:T(8,128)(2,1)}), bf16[16,15,16,128]{3,2,1,0:T(8,128)(2,1)S(1)}, u32[]{:S(2)}, u32[]{:S(2)}) %all-to-all-start) | async-done | bytes 983072 | tf_op jit(solution)/shard_map/all_to_all | solution.py:585
  32.3 0.7 copy-done.2
  32.9 1.1 %shard_map.87 = (bf16[5,192,256]{2,1,0:T(8,128)(2,1)S(1)}, bf16[8,8,16,128]{3,2,1,0:T(8,128)(2,1)S(1)}) custom-call(s32[4,8]{1,0:T(4,128)S(1)} %copy-done.2, s32[320,1]{1,0:T(8,128)S(1)} %reshape.81.index_ref.rest_1_, bf16[16,15,16,128]{3,2,1,0:T(8,128)(2,1)S(1)} %all-to-all-done.recv_ref.rest_3_), custom_call_target="tpu_custom_call" | custom-call | flops 157286400 | bytes 1474560 | tf_op jit(solution)/shard_map/pallas_call | solution.py:171
  34.1 0.1 collective-permute-start.9
  34.1 0.7 fusion.3
  34.9 0.0 collective-permute-done
  34.9 3.0 %collective-permute-start.5 = (bf16[8,16,128]{2,1,0:T(8,128)(2,1)}, bf16[8,16,128]{2,1,0:T(8,128)(2,1)S(1)}, u32[]{:S(2)}, u32[]{:S(2)}) collective-permute-start(bf16[8,16,128]{2,1,0:T(8,128)(2,1)} %get-tuple-element.28), channel_id=1, source_target_pairs={{0,4},{1,5},{2,6},{3,7},{4,0},{5,1},{6,2},{7,3},{8,12},{9,13},{10,... | collective-permute-start | bytes 98312 | tf_op jit(solution)/shard_map/ppermute | solution.py:592
  37.9 0.0 collective-permute-done.2.rest_5_
  37.9 1.7 %collective-permute-start.1 = (bf16[8,8,16,128]{3,2,1,0:T(8,128)(2,1)S(1)}, bf16[8,8,16,128]{3,2,1,0:T(8,128)(2,1)S(1)}, u32[]{:S(2)}, u32[]{:S(2)}) collective-permute-start(bf16[8,8,16,128]{3,2,1,0:T(8,128)(2,1)S(1)} %get-tuple-element.22), channel_id=1, source_target_pairs={{0,15},{1,2},{2,1},{3,4},{4,3},{5,6},{6,5},{7,8},{8,7},{9,10},{10,... | collective-permute-start | bytes 786440 | tf_op jit(solution)/shard_map/ppermute | solution.py:530
  39.6 0.9 %select_reduce_fusion = f32[256]{0:T(256)S(1)} fusion(f32[256]{0:T(256)} %param.13, s32[256]{0:T(256)} %param.12), kind=kLoop, calls=%fused_computation | loop fusion | flops 196352 | bytes 3072 | tf_op jit(solution)/shard_map/reduce_sum | solution.py:566
  40.4 0.0 collective-permute-done.3.rest_6_
  40.4 0.0 copy-start.5
  40.4 1.0 %collective-permute-start.6 = (bf16[8,16,128]{2,1,0:T(8,128)(2,1)}, bf16[8,16,128]{2,1,0:T(8,128)(2,1)S(1)}, u32[]{:S(2)}, u32[]{:S(2)}) collective-permute-start(bf16[8,16,128]{2,1,0:T(8,128)(2,1)} %get-tuple-element.29), channel_id=1, source_target_pairs={{0,5},{1,4},{2,7},{3,6},{4,1},{5,0},{6,3},{7,2},{8,13},{9,12},{10,... | collective-permute-start | bytes 98312 | tf_op jit(solution)/shard_map/ppermute | solution.py:592
  41.4 0.0 collective-permute-done.4.rest_7_
  41.4 0.3 collective-permute-start.7
  41.8 0.0 collective-permute-done.5.rest_8_
  41.8 1.9 %collective-permute-start.8 = (bf16[8,16,128]{2,1,0:T(8,128)(2,1)}, bf16[8,16,128]{2,1,0:T(8,128)(2,1)S(1)}, u32[]{:S(2)}, u32[]{:S(2)}) collective-permute-start(bf16[8,16,128]{2,1,0:T(8,128)(2,1)} %get-tuple-element.31), channel_id=1, source_target_pairs={{0,7},{1,6},{2,5},{3,4},{4,3},{5,2},{6,1},{7,0},{8,15},{9,14},{10,... | collective-permute-start | bytes 98312 | tf_op jit(solution)/shard_map/ppermute | solution.py:592
  43.7 0.8 %select_reduce_fusion.1.block_ref = s32[5,15]{1,0:T(8,128)} fusion(s32[5,14]{1,0:T(8,128)S(1)} %fusion.3), kind=kLoop, calls=%fused_computation.2 | loop fusion | flops 3075 | bytes 580 | tf_op jit(solution)/shard_map/reduce_min | solution.py:562
  44.4 4.2 %shard_map.90.phi_ref = bf16[5,192,960]{2,1,0:T(8,128)(2,1)} custom-call(s32[5,15]{1,0:T(8,128)} %select_reduce_fusion.1.block_ref, bf16[5,14,192,192]{3,2,1,0:T(8,128)(2,1)} %phi_ref.3), custom_call_target="tpu_custom_call" | custom-call | bytes 5160960 | tf_op jit(solution)/shard_map/pallas_call | solution.py:237
  48.7 0.1 reshape.80.rest_2_.index_ref
  48.8 0.0 collective-permute-done.6.rest_9_
  48.8 0.0 collective-permute-done.7.rest_10_
  48.8 0.0 copy-start.9
  48.8 0.0 collective-permute-done.8.rest_11_
  48.9 0.5 copy-done.8
  49.4 0.0 copy-done.9
  49.5 0.0 copy-done.10
  49.5 4.9 %shard_map.89 = (f32[5,192,256]{2,1,0:T(8,128)S(1)}, bf16[5,192,256]{2,1,0:T(8,128)(2,1)S(1)}, bf16[5,5,192,192]{3,2,1,0:T(8,128)(2,1)S(1)}, bf16[5,192,128]{2,1,0:T(8,128)(2,1)S(1)}) custom-call(s32[5,15]{1,0:T(8,128)S(1)} %copy-done.1, bf16[5,14,192,192]{3,2,1,0:T(8,128)(2,1)} %phi_ref.3, bf16[5,192,256]{2,1,0:T(8,128)(2,1)S(1)} %get-tuple-element.23.own_ref.down, ...), custom_call_target="tpu_custom_call" | custom-call | flops 660602880 | bytes 5160960 | tf_op jit(solution)/shard_map/pallas_call | solution.py:342
  54.4 0.0 collective-permute-done.9.partner_ref.dnear
  54.4 1.5 %shard_map.91.base_ref = f32[5,192,256]{2,1,0:T(8,128)S(1)} custom-call(s32[5,15]{1,0:T(8,128)S(1)} %copy-done.1, bf16[5,5,192,192]{3,2,1,0:T(8,128)(2,1)S(1)} %get-tuple-element.33.phi_ref, bf16[5,192,256]{2,1,0:T(8,128)(2,1)S(1)} %collective-permute-done.9.partner_ref.dnear, f32[5,192,256]{2,1,0:T(8,128)S(1)} %get-tuple-element.34.base_ref), custom_call_target="tpu_custom_call" | custom-call | flops 471859200 | bytes 1843200 | tf_op jit(solution)/shard_map/pallas_call | solution.py:362
  55.9 0.0 collective-permute-done.1.recv_ref
  55.9 1.8 %shard_map.92 = (bf16[5,192,256]{2,1,0:T(8,128)(2,1)S(1)}, bf16[5,192,256]{2,1,0:T(8,128)(2,1)S(1)}, bf16[5,192,256]{2,1,0:T(8,128)(2,1)S(1)}) custom-call(s32[4,8]{1,0:T(4,128)S(1)} %copy-done.3, s32[320,1]{1,0:T(8,128)S(1)} %reshape.80.rest_2_.index_ref, bf16[8,8,16,128]{3,2,1,0:T(8,128)(2,1)S(1)} %collective-permute-done.1.recv_ref, ...), custom_call_target="tpu_custom_call" | custom-call | flops 513802240 | bytes 1843200 | tf_op jit(solution)/shard_map/pallas_call | solution.py:414
  57.7 0.6 collective-permute-start.10
  58.3 0.8 %collective-permute-start.11 = (bf16[5,192,256]{2,1,0:T(8,128)(2,1)S(1)}, bf16[5,192,256]{2,1,0:T(8,128)(2,1)S(1)}, u32[]{:S(2)}, u32[]{:S(2)}) collective-permute-start(bf16[5,192,256]{2,1,0:T(8,128)(2,1)S(1)} %get-tuple-element.38.rown), channel_id=1, source_target_pairs={{0,15},{1,2},{2,1},{3,4},{4,3},{5,6},{6,5},{7,8},{8,7},{9,10},{10,... | collective-permute-start | bytes 1474568 | tf_op jit(solution)/shard_map/ppermute | solution.py:530
  59.2 0.6 collective-permute-done.10.rnear
  59.8 5.0 %shard_map.93 = (bf16[5,14,192,192]{3,2,1,0:T(8,128)(2,1)}, bf16[5,192,256]{2,1,0:T(8,128)(2,1)}, f32[5,5,192,192]{3,2,1,0:T(8,128)S(1)}) custom-call(s32[5,15]{1,0:T(8,128)S(1)} %copy-done.1, bf16[5,192,256]{2,1,0:T(8,128)(2,1)S(1)} %get-tuple-element.35.wres_ref, bf16[5,192,256]{2,1,0:T(8,128)(2,1)S(1)} %get-tuple-element.36.wdisp_ref, ...), custom_call_target="tpu_custom_call" | custom-call | flops 2359296000 | bytes 3686400 | tf_op jit(solution)/shard_map/pallas_call | solution.py:495
  64.8 7.0 %collective-permute-done.11.rfar = bf16[5,192,256]{2,1,0:T(8,128)(2,1)S(1)} collective-permute-done((bf16[5,192,256]{2,1,0:T(8,128)(2,1)S(1)}, bf16[5,192,256]{2,1,0:T(8,128)(2,1)S(1)}, u32[]{:S(2)}, u32[]{:S(2)}) %collective-permute-start.11) | collective-permute-done | bytes 491552 | tf_op jit(solution)/shard_map/ppermute | solution.py:530
  71.8 2.6 %shard_map.94 = bf16[5,14,192,192]{3,2,1,0:T(8,128)(2,1)} custom-call(s32[5,15]{1,0:T(8,128)S(1)} %copy-done.1, bf16[5,192,256]{2,1,0:T(8,128)(2,1)S(1)} %get-tuple-element.36.wdisp_ref, bf16[5,192,256]{2,1,0:T(8,128)(2,1)S(1)} %collective-permute-done.11.rfar, f32[5,5,192,192]{3,2,1,0:T(8,128)S(1)} %get-tuple-element.40.far_ref, ...), custom_call_target="tpu_custom_call", output_to_operand_aliasing={{}: (4, {})} | custom-call | flops 471859200 | bytes 5529600 | tf_op jit(solution)/shard_map/pallas_call | solution.py:510
  (19 shorter events, 0.1 us)
Async XLA Ops:
  2.8 29.4 %all-to-all-start = ((bf16[16,15,16,128]{3,2,1,0:T(8,128)(2,1)}), bf16[16,15,16,128]{3,2,1,0:T(8,128)(2,1)S(1)}, u32[]{:S(2)}, u32[]{:S(2)}) async-start(bf16[16,15,16,128]{3,2,1,0:T(8,128)(2,1)} %shard_map.86.send_ref), calls=%async_computation | async-start | bytes 1966080 | tf_op jit(solution)/shard_map/all_to_all | solution.py:585
  10.9 24.0 %collective-permute-start = (s32[5,64]{1,0:T(8,128)S(1)}, s32[5,64]{1,0:T(8,128)S(1)}, u32[]{:S(2)}, u32[]{:S(2)}) collective-permute-start(s32[5,64]{1,0:T(8,128)S(1)} %add_select_fusion), channel_id=1, source_target_pairs={{0,15},{1,2},{2,1},{3,4},{4,3},{5,6},{6,5},{7,8},{8,7},{9,10},{10,... | collective-permute-start | bytes 3848 | tf_op jit(solution)/shard_map/ppermute | solution.py:530
  13.2 36.2 %copy-start.3 = (s32[4,8]{1,0:T(4,128)S(1)}, s32[4,8]{1,0:T(4,128)}, u32[]{:S(2)}) copy-start(s32[4,8]{1,0:T(4,128)} %fusion.7.route_ref.rest_0_) | copy-start | bytes 388
  15.6 22.2 %collective-permute-start.2 = (bf16[8,16,128]{2,1,0:T(8,128)(2,1)}, bf16[8,16,128]{2,1,0:T(8,128)(2,1)S(1)}, u32[]{:S(2)}, u32[]{:S(2)}) collective-permute-start(bf16[8,16,128]{2,1,0:T(8,128)(2,1)} %get-tuple-element.25), channel_id=1, source_target_pairs={{0,1},{1,0},{2,3},{3,2},{4,5},{5,4},{6,7},{7,6},{8,9},{9,8},{10,11... | collective-permute-start | bytes 98312 | tf_op jit(solution)/shard_map/ppermute | solution.py:592
  18.5 21.9 %collective-permute-start.3 = (bf16[8,16,128]{2,1,0:T(8,128)(2,1)}, bf16[8,16,128]{2,1,0:T(8,128)(2,1)S(1)}, u32[]{:S(2)}, u32[]{:S(2)}) collective-permute-start(bf16[8,16,128]{2,1,0:T(8,128)(2,1)} %get-tuple-element.26), channel_id=1, source_target_pairs={{0,2},{1,3},{2,0},{3,1},{4,6},{5,7},{6,4},{7,5},{8,10},{9,11},{10,... | collective-permute-start | bytes 98312 | tf_op jit(solution)/shard_map/ppermute | solution.py:592
  18.5 22.9 %collective-permute-start.4 = (bf16[8,16,128]{2,1,0:T(8,128)(2,1)}, bf16[8,16,128]{2,1,0:T(8,128)(2,1)S(1)}, u32[]{:S(2)}, u32[]{:S(2)}) collective-permute-start(bf16[8,16,128]{2,1,0:T(8,128)(2,1)} %get-tuple-element.27), channel_id=1, source_target_pairs={{0,3},{1,2},{2,1},{3,0},{4,7},{5,6},{6,5},{7,4},{8,11},{9,10},{10,... | collective-permute-start | bytes 98312 | tf_op jit(solution)/shard_map/ppermute | solution.py:592
  32.2 0.7 copy-start.2
  34.1 20.3 %collective-permute-start.9 = (bf16[5,192,256]{2,1,0:T(8,128)(2,1)S(1)}, bf16[5,192,256]{2,1,0:T(8,128)(2,1)S(1)}, u32[]{:S(2)}, u32[]{:S(2)}) collective-permute-start(bf16[5,192,256]{2,1,0:T(8,128)(2,1)S(1)} %get-tuple-element.23.own_ref.down), channel_id=1, source_target_pairs={{0,1},{1,0},{2,3},{3,2},{4,5},{5,4},{6,7},{7,6},{8,9},{9,8},{10,11... | collective-permute-start | bytes 1474568 | tf_op jit(solution)/shard_map/ppermute | solution.py:524
  34.9 6.9 %collective-permute-start.5 = (bf16[8,16,128]{2,1,0:T(8,128)(2,1)}, bf16[8,16,128]{2,1,0:T(8,128)(2,1)S(1)}, u32[]{:S(2)}, u32[]{:S(2)}) collective-permute-start(bf16[8,16,128]{2,1,0:T(8,128)(2,1)} %get-tuple-element.28), channel_id=1, source_target_pairs={{0,4},{1,5},{2,6},{3,7},{4,0},{5,1},{6,2},{7,3},{8,12},{9,13},{10,... | collective-permute-start | bytes 98312 | tf_op jit(solution)/shard_map/ppermute | solution.py:592
  37.9 11.0 %copy-start.4 = (bf16[8,16,128]{2,1,0:T(8,128)(2,1)}, bf16[8,16,128]{2,1,0:T(8,128)(2,1)S(1)}, u32[]{:S(2)}) copy-start(bf16[8,16,128]{2,1,0:T(8,128)(2,1)S(1)} %collective-permute-done.2.rest_5_) | copy-start | bytes 98308
  37.9 18.1 %collective-permute-start.1 = (bf16[8,8,16,128]{3,2,1,0:T(8,128)(2,1)S(1)}, bf16[8,8,16,128]{3,2,1,0:T(8,128)(2,1)S(1)}, u32[]{:S(2)}, u32[]{:S(2)}) collective-permute-start(bf16[8,8,16,128]{3,2,1,0:T(8,128)(2,1)S(1)} %get-tuple-element.22), channel_id=1, source_target_pairs={{0,15},{1,2},{2,1},{3,4},{4,3},{5,6},{6,5},{7,8},{8,7},{9,10},{10,... | collective-permute-start | bytes 786440 | tf_op jit(solution)/shard_map/ppermute | solution.py:530
  40.4 8.4 %copy-start.5 = (bf16[8,16,128]{2,1,0:T(8,128)(2,1)}, bf16[8,16,128]{2,1,0:T(8,128)(2,1)S(1)}, u32[]{:S(2)}) copy-start(bf16[8,16,128]{2,1,0:T(8,128)(2,1)S(1)} %collective-permute-done.3.rest_6_) | copy-start | bytes 98308
  40.4 8.4 %collective-permute-start.6 = (bf16[8,16,128]{2,1,0:T(8,128)(2,1)}, bf16[8,16,128]{2,1,0:T(8,128)(2,1)S(1)}, u32[]{:S(2)}, u32[]{:S(2)}) collective-permute-start(bf16[8,16,128]{2,1,0:T(8,128)(2,1)} %get-tuple-element.29), channel_id=1, source_target_pairs={{0,5},{1,4},{2,7},{3,6},{4,1},{5,0},{6,3},{7,2},{8,13},{9,12},{10,... | collective-permute-start | bytes 98312 | tf_op jit(solution)/shard_map/ppermute | solution.py:592
  41.4 7.5 %copy-start.6 = (bf16[8,16,128]{2,1,0:T(8,128)(2,1)}, bf16[8,16,128]{2,1,0:T(8,128)(2,1)S(1)}, u32[]{:S(2)}) copy-start(bf16[8,16,128]{2,1,0:T(8,128)(2,1)S(1)} %collective-permute-done.4.rest_7_) | copy-start | bytes 98308
  41.4 7.4 %collective-permute-start.7 = (bf16[8,16,128]{2,1,0:T(8,128)(2,1)}, bf16[8,16,128]{2,1,0:T(8,128)(2,1)S(1)}, u32[]{:S(2)}, u32[]{:S(2)}) collective-permute-start(bf16[8,16,128]{2,1,0:T(8,128)(2,1)} %get-tuple-element.30), channel_id=1, source_target_pairs={{0,6},{1,7},{2,4},{3,5},{4,2},{5,3},{6,0},{7,1},{8,14},{9,15},{10,... | collective-permute-start | bytes 98312 | tf_op jit(solution)/shard_map/ppermute | solution.py:592
  41.8 7.1 %copy-start.7 = (bf16[8,16,128]{2,1,0:T(8,128)(2,1)}, bf16[8,16,128]{2,1,0:T(8,128)(2,1)S(1)}, u32[]{:S(2)}) copy-start(bf16[8,16,128]{2,1,0:T(8,128)(2,1)S(1)} %collective-permute-done.5.rest_8_) | copy-start | bytes 98308
  41.8 7.1 %collective-permute-start.8 = (bf16[8,16,128]{2,1,0:T(8,128)(2,1)}, bf16[8,16,128]{2,1,0:T(8,128)(2,1)S(1)}, u32[]{:S(2)}, u32[]{:S(2)}) collective-permute-start(bf16[8,16,128]{2,1,0:T(8,128)(2,1)} %get-tuple-element.31), channel_id=1, source_target_pairs={{0,7},{1,6},{2,5},{3,4},{4,3},{5,2},{6,1},{7,0},{8,15},{9,14},{10,... | collective-permute-start | bytes 98312 | tf_op jit(solution)/shard_map/ppermute | solution.py:592
  44.4 5.0 %copy-start.1 = (s32[5,15]{1,0:T(8,128)S(1)}, s32[5,15]{1,0:T(8,128)}, u32[]{:S(2)}) copy-start(s32[5,15]{1,0:T(8,128)} %select_reduce_fusion.1.block_ref) | copy-start | bytes 904
  48.8 0.6 copy-start.8
  48.8 0.6 copy-start.9
  48.9 0.6 copy-start.10
  49.5 6.5 %copy-start = (bf16[5,192,960]{2,1,0:T(8,128)(2,1)S(1)}, bf16[5,192,960]{2,1,0:T(8,128)(2,1)}, u32[]{:S(2)}) copy-start(bf16[5,192,960]{2,1,0:T(8,128)(2,1)} %shard_map.90.phi_ref) | copy-start | bytes 5529604
  57.7 2.1 %collective-permute-start.10 = (bf16[5,192,256]{2,1,0:T(8,128)(2,1)S(1)}, bf16[5,192,256]{2,1,0:T(8,128)(2,1)S(1)}, u32[]{:S(2)}, u32[]{:S(2)}) collective-permute-start(bf16[5,192,256]{2,1,0:T(8,128)(2,1)S(1)} %get-tuple-element.38.rown), channel_id=1, source_target_pairs={{0,1},{1,0},{2,3},{3,2},{4,5},{5,4},{6,7},{7,6},{8,9},{9,8},{10,11... | collective-permute-start | bytes 1474568 | tf_op jit(solution)/shard_map/ppermute | solution.py:524
  58.3 13.5 %collective-permute-start.11 = (bf16[5,192,256]{2,1,0:T(8,128)(2,1)S(1)}, bf16[5,192,256]{2,1,0:T(8,128)(2,1)S(1)}, u32[]{:S(2)}, u32[]{:S(2)}) collective-permute-start(bf16[5,192,256]{2,1,0:T(8,128)(2,1)S(1)} %get-tuple-element.38.rown), channel_id=1, source_target_pairs={{0,15},{1,2},{2,1},{3,4},{4,3},{5,6},{6,5},{7,8},{8,7},{9,10},{10,... | collective-permute-start | bytes 1474568 | tf_op jit(solution)/shard_map/ppermute | solution.py:530

commit v6 on v5

--- a/solution.py
+++ b/solution.py
@@ -116,18 +116,17 @@
     def hot(cond):
         return jnp.where(cond, 1.0, 0.0).astype(BF16)
 
-    wholes = [hot(index - 128 * t == lane) for t in range(full)]
+    wholes = [jnp.concatenate([hot(index - 128 * t == lane) for t in range(full)], axis=1)]
     rest = index - 128 * full
     lower = hot(rest == lane)
     upper = hot((rest >= 0) & (rest + 64 == lane))
     return wholes, lower, upper
 
 
-def picked(wholes, half_hot, tiles, half):
-    total = lax.dot_general(half_hot, half, NT, preferred_element_type=F32)
-    for hot, tile in zip(wholes, tiles):
-        total = total + lax.dot_general(hot, tile, NT, preferred_element_type=F32)
-    return total
+def picked(whole_hot, half_hot, tiles, half):
+    hot = jnp.concatenate([whole_hot, half_hot], axis=1)
+    tile = jnp.concatenate([*tiles, half], axis=1)
+    return lax.dot_general(hot, tile, NT, preferred_element_type=F32)
 
 
 def flat(ref, t):
@@ -136,8 +135,8 @@
 
 
 def component(recv_ref, hots, field, a):
-    wholes, lower, upper = hots
-    full = len(wholes)
+    (wholes,), lower, upper = hots
+    full = wholes.shape[1] // 128
     base = 3 * full
     half = base + 1 if a == 2 else base + 2 * field
     first = a * full + field * (base + 3)
@@ -156,9 +155,12 @@
             out_ref[c, a * atoms : (a + 1) * atoms] = got[c * atoms : (c + 1) * atoms]
 
 
-def gather_and_pass_kernel(route_ref, index_ref, recv_ref, out_ref, pass_ref):
-    for i in range(pass_ref.shape[0]):
-        pass_ref[i] = recv_ref[route_ref[3, i], : pass_ref.shape[1]]
+def gather_and_pass_kernel(flag_ref, index_ref, recv_ref, out_ref, pass_ref):
+    reach, tiles, configs, _ = pass_ref.shape
+    upper = jnp.broadcast_to(flag_ref[0:1] > 0, (configs, 128))
+    for i in range(reach):
+        for t in range(tiles):
+            pass_ref[i, t] = jnp.where(upper, recv_ref[reach + i, t], recv_ref[i, t])
     put(out_ref, index_ref, recv_ref, 0, BF16)
 
 
@@ -166,19 +168,19 @@
     return 3 * ((recv.shape[1] - 3) // 6) + 2
 
 
-def gather_and_pass(route, index, recv, clusters, atoms):
+def gather_and_pass(flags, index, recv, clusters, atoms):
     width, _, configs, _ = recv.shape
     return pl.pallas_call(
         gather_and_pass_kernel,
-        in_specs=[in_smem()] + in_vmem(2),
+        in_specs=in_vmem(3),
         out_specs=in_vmem(2),
         out_shape=[
             shape((clusters, 3 * atoms, width * configs)),
-            shape((route.shape[1], disp_tiles(recv), configs, 128)),
+            shape((width // 2, disp_tiles(recv), configs, 128)),
         ],
         compiler_params=params(8),
         cost_estimate=cost(recv.size * index.size, 3 * recv.size),
-    )(route, index, recv)
+    )(flags, index, recv)
 
 
 def pick_kernel(route_ref, send_ref, *rest):
@@ -248,51 +250,33 @@
     )(block_of, pltpu.with_memory_space_constraint(phi, pltpu.HBM))
 
 
-def stacked(block_ref, held, n, blocks):
-    clusters = held.shape[0]
-    return jnp.concatenate(
-        [masked(block_ref, held[c], c, n, blocks) for c in range(clusters)], axis=0
-    )
-
-
-def fetcher(block_ref, phi_ref, sem):
-    def fetch(n, c, place):
-        k = jnp.minimum(block_ref[c, n], phi_ref.shape[1] - 1)
-        return pltpu.make_async_copy(phi_ref.at[c, k], place.at[c], sem.at[n, c])
-
-    return fetch
-
-
-def own_harmonic(block_ref, blocks, own_ref, held, out_ref, ready):
-    for n in range(own_ref.shape[0]):
-        ready(n)
-        left = stacked(block_ref, held.at[n], n, blocks)
-        got = jnp.dot(left, own_ref[n], preferred_element_type=F32)
-        out_ref[...] = out_ref[...] + got.reshape(out_ref.shape)
-
-
-def own_kernel(block_ref, phi_ref, own_ref, wt_ref, *rest, dense):
+def near_harmonic_kernel(
+    block_ref, phi_ref, own_ref, partner_ref, wt_ref, *rest, dense
+):
     if dense:
-        route_ref, index_ref, index_far_ref, recv_ref, *rest = rest
+        route_ref, index_ref, recv_ref, *rest = rest
         reach = route_ref.shape[1]
-        pieces, rest = rest[:reach], rest[reach:]
-        out_ref, wdisp_ref, partner_ref, direct_ref, held, sem, frame, frame_sem = rest
+        pieces = rest[:reach]
+        out_ref, wdisp_ref, frame_ref, held, block_sem, sem = rest[reach:]
         copies = [
             pltpu.make_async_copy(
-                piece, frame.at[lax.rem(route_ref[1, j], reach)], frame_sem.at[j]
+                piece, frame_ref.at[lax.rem(route_ref[1, j], reach)], sem.at[j]
             )
             for j, piece in enumerate(pieces)
         ]
     else:
-        force_ref, out_ref, wdisp_ref, partner_ref, held, sem = rest
+        force_ref, out_ref, wdisp_ref, held, block_sem = rest
         copies = []
     layer = own_ref.shape[0]
     clusters, blocks = phi_ref.shape[:2]
-    fetch = fetcher(block_ref, phi_ref, sem)
+
+    def fetch(n, c):
+        k = jnp.minimum(block_ref[c, n], blocks - 1)
+        return pltpu.make_async_copy(phi_ref.at[c, k], held.at[n, c], block_sem.at[n, c])
+
     for n in range(2 * layer):
         for c in range(clusters):
-            place = held.at[n] if n < layer else partner_ref.at[n - layer]
-            fetch(n, c, place).start()
+            fetch(n, c).start()
     for copy in copies:
         copy.start()
     wt = 0.5 * wt_ref[...]
@@ -302,71 +286,46 @@
         put(out_ref, index_ref, recv_ref, 1, F32)
     else:
         out_ref[...] = force_ref[...].astype(F32)
-
-    def ready(n):
+    for n in range(2 * layer):
         for c in range(clusters):
-            fetch(n, c, held.at[n] if n < layer else partner_ref.at[n - layer]).wait()
-
-    own_harmonic(block_ref, blocks, own_ref, held, out_ref, ready)
+            fetch(n, c).wait()
+        left = jnp.concatenate(
+            [masked(block_ref, held[n, c], c, n, blocks) for c in range(clusters)], axis=0
+        )
+        disp = own_ref[n] if n < layer else partner_ref[n - layer]
+        got = jnp.dot(left, disp, preferred_element_type=F32)
+        out_ref[...] = out_ref[...] + got.reshape(out_ref.shape)
     for copy in copies:
         copy.wait()
-    if dense:
-        put(direct_ref, index_far_ref, frame, 0, BF16)
-    for n in range(layer, 2 * layer):
-        ready(n)
-
-
-def own_part(block_of, phi, own, wt, dense, extra):
+
+
+def near_harmonic(block_of, phi, own, partner, wt, dense, extra):
     clusters, _, dof, _ = phi.shape
-    layer, _, configs = own.shape
-    hbm = pl.BlockSpec(memory_space=pltpu.HBM)
-    in_specs = [in_smem(), hbm] + in_vmem(2)
-    out_shape = [shape(own.shape, F32), shape(own.shape), shape((layer, clusters, dof, dof))]
+    configs = own.shape[2]
+    layer = own.shape[0]
+    in_specs = [in_smem(), pl.BlockSpec(memory_space=pltpu.HBM)] + in_vmem(3)
+    out_shape = [shape(own.shape, F32), shape(own.shape)]
     scratch = [
-        VMEM((layer, clusters, dof, dof), BF16),
+        VMEM((2 * layer, clusters, dof, dof), BF16),
         pltpu.SemaphoreType.DMA((2 * layer, clusters)),
     ]
     if dense:
-        pieces = extra[4:]
-        tiles, few, _ = pieces[0].shape
-        in_specs += [in_smem()] + in_vmem(3) + [hbm] * len(pieces)
-        out_shape.append(shape((clusters, dof, len(pieces) * few)))
-        scratch += [
-            VMEM((len(pieces), tiles, few, 128), BF16),
-            pltpu.SemaphoreType.DMA((len(pieces),)),
-        ]
-        pieces = [pltpu.with_memory_space_constraint(p, pltpu.HBM) for p in pieces]
-        extra = (*extra[:4], *pieces)
+        pieces = extra[3:]
+        in_specs += [in_smem()] + in_vmem(2)
+        in_specs += [pl.BlockSpec(memory_space=pl.ANY)] * len(pieces)
+        out_shape.append(shape((len(pieces), *pieces[0].shape)))
+        scratch.append(pltpu.SemaphoreType.DMA((len(pieces),)))
     else:
         in_specs += in_vmem(1)
     return pl.pallas_call(
-        functools.partial(own_kernel, dense=dense),
+        functools.partial(near_harmonic_kernel, dense=dense),
         in_specs=in_specs,
         out_specs=in_vmem(len(out_shape)),
         out_shape=out_shape,
         scratch_shapes=scratch,
-        compiler_params=params(12),
-        cost_estimate=cost(phi.size * configs, 2 * phi.size),
-    )(block_of, pltpu.with_memory_space_constraint(phi, pltpu.HBM), own, wt, *extra)
-
-
-def partner_kernel(blocks, block_ref, phi_ref, partner_ref, base_ref, out_ref):
-    layer = partner_ref.shape[0]
-    for n in range(layer):
-        left = stacked(block_ref, phi_ref.at[n], layer + n, blocks)
-        got = jnp.dot(left, partner_ref[n], preferred_element_type=F32).reshape(out_ref.shape)
-        out_ref[...] = (base_ref if n == 0 else out_ref)[...] + got
-
-
-def partner_part(blocks, block_of, phi_partner, partner, base):
-    return pl.pallas_call(
-        functools.partial(partner_kernel, blocks),
-        in_specs=[in_smem()] + in_vmem(3),
-        out_specs=in_vmem(1)[0],
-        out_shape=shape(base.shape, F32),
-        compiler_params=params(8),
-        cost_estimate=cost(2 * phi_partner.size * base.shape[2], 2 * phi_partner.size),
-    )(block_of, phi_partner, partner, base)
+        compiler_params=params(16),
+        cost_estimate=cost(2 * phi.size * configs, 2 * phi.size),
+    )(block_of, pltpu.with_memory_space_constraint(phi, pltpu.HBM), own, partner, wt, *extra)
 
 
 def residual_kernel(phi_ref, far_ref, base_ref, wt_ref, res_ref, wres_ref):
@@ -392,35 +351,33 @@
 
 
 def merged_residual_kernel(
-    route_ref, index_ref, recv_ref, direct_ref, phi_ref, base_ref, wt_ref, res_ref, wres_ref,
-    far_ref
+    flag_ref, index_ref, recv_ref, frame_ref, phi_ref, base_ref, wt_ref, res_ref, wres_ref,
+    far_ref, both
 ):
-    clusters, dof, configs = res_ref.shape
-    atoms = dof // 3
-    half = configs // 2
-    first = route_ref[1, 0] < route_ref.shape[1]
-    hots = one_hots(index_ref, (recv_ref.shape[1] - 2) // 3)
-    for a in range(3):
-        rest = component(recv_ref, hots, 0, a).astype(BF16)
-        for c in range(clusters):
-            rows = pl.ds(a * atoms, atoms)
-            x, y = direct_ref[c, rows], rest[c * atoms : (c + 1) * atoms]
-            far_ref[c, rows, :half] = jnp.where(first, x, y)
-            far_ref[c, rows, half:] = jnp.where(first, y, x)
+    reach, tiles, configs, _ = recv_ref.shape
+    first = jnp.broadcast_to(flag_ref[1:2] > 0, (configs, 128))
+    for i in range(reach):
+        for t in range(tiles):
+            x, y = frame_ref[i, t], recv_ref[i, t]
+            both[i, t] = jnp.where(first, x, y)
+            both[reach + i, t] = jnp.where(first, y, x)
+    put(far_ref, index_ref, both, 0, BF16)
     residual_kernel(phi_ref, far_ref, base_ref, wt_ref, res_ref, wres_ref)
 
 
-def merged_residual(route, index, recv, near_half, phi_far, base, wt):
+def merged_residual(flags, index, recv, frame, phi_far, base, wt):
+    reach, tiles, configs, _ = recv.shape
     return pl.pallas_call(
         merged_residual_kernel,
-        in_specs=[in_smem()] + in_vmem(6),
+        in_specs=in_vmem(7),
         out_specs=in_vmem(3),
         out_shape=[shape(base.shape)] * 3,
+        scratch_shapes=[VMEM((2 * reach, tiles, configs, 128), BF16)],
         compiler_params=params(8),
         cost_estimate=cost(
-            2 * phi_far.size * base.shape[2] + recv.size * index.size, 2 * phi_far.size
+            2 * phi_far.size * base.shape[2] + 2 * recv.size * index.size, 2 * phi_far.size
         ),
-    )(route, index, recv, near_half, phi_far, base, wt)
+    )(flags, index, recv, frame, phi_far, base, wt)
 
 
 def put_blocks(block_ref, held, out_ref, sem, first):
@@ -470,13 +427,19 @@
     keep.wait()
 
 
-def far_gradient_kernel(block_ref, wdisp_ref, rfar, far_ref, prior_ref, out_ref, held, sem):
+def far_gradient_kernel(
+    table_ref, wdisp_ref, rfar, far_ref, prior_ref, out_ref, held, sem, block_ref, table_sem
+):
     clusters, dof, configs = wdisp_ref.shape
+    table = pltpu.make_async_copy(table_ref, block_ref, table_sem)
+    table.start()
     start, finish = put_blocks(block_ref, held, out_ref, sem, 2 * far_ref.shape[0])
     left = wdisp_ref[...].reshape(clusters * dof, configs)
     for i in range(rfar.shape[0]):
         got = lax.dot_general(left, rfar[i], NT, preferred_element_type=F32)
         held[i] = (far_ref[i] + got.reshape(held.shape[1:])).astype(BF16)
+        if i == 0:
+            table.wait()
         start(i)
     finish()
 
@@ -509,10 +472,11 @@
     hbm = pl.BlockSpec(memory_space=pltpu.HBM)
     return pl.pallas_call(
         far_gradient_kernel,
-        in_specs=[in_smem()] + in_vmem(3) + [hbm],
+        in_specs=in_vmem(4) + [hbm],
         out_specs=hbm,
         out_shape=shape(prior.shape),
-        scratch_shapes=block_copies(layer, clusters, dof),
+        scratch_shapes=block_copies(layer, clusters, dof)
+        + [SMEM(block_of.shape, jnp.int32), pltpu.SemaphoreType.DMA(())],
         input_output_aliases={4: 0},
         compiler_params=params(8),
         cost_estimate=cost(2 * layer * dof * wdisp.size, 6 * layer * clusters * dof * dof),
@@ -542,6 +506,12 @@
     peer = position ^ q
     rest = (jnp.where(row == 2, block, far_block) + reach + q) % width
     return jnp.where(row == 0, far_of(peer, width), jnp.where(row == 1, peer, rest))
+
+
+def halves(position, width, reach):
+    row = jnp.arange(2, dtype=jnp.int32)[:, None]
+    who = jnp.where(row == 0, far_of(position, width), position)
+    return jnp.broadcast_to((who < reach).astype(jnp.int32), (2, 128))
 
 
 def arrange(field, atom_map):
@@ -585,14 +555,15 @@
         recv = lax.all_to_all(send, "cx", split_axis=0, concat_axis=0, tiled=True)
         index = (atom_local - 64 * (position % 2) + per) % per
         route = routes(position, width, reach)
+        flags = halves(position, width, reach)
         index_far = swap_far(index).reshape(-1, 1)
         index = index.reshape(-1, 1)
         pieces = list(pick(route, send))
         for j in range(1, reach):
             pieces[j] = lax.ppermute(pieces[j], "cx", [(i, i ^ j) for i in range(width)])
-        disp, passed = gather_and_pass(route, index, recv, layer, atoms)
+        disp, passed = gather_and_pass(flags, index, recv, layer, atoms)
         recv_far = swap_far(passed)
-        extra = (route, index, index_far, recv, *pieces)
+        extra = (route, index, recv, *pieces)
     else:
         disp, force = (
             arrange(lax.all_to_all(x, "cx", split_axis=2, concat_axis=0, tiled=True), atom_local)
@@ -601,11 +572,10 @@
         disp_far = swap_far(disp)
         extra = (force,)
     disp_near = swap_near(disp)
-    base, wdisp, phi_partner, *near_half = own_part(block_of, phi, disp, wt, dense, extra)
-    base = partner_part(phi.shape[1], block_of, phi_partner, disp_near, base)
+    base, wdisp, *frame = near_harmonic(block_of, phi, disp, disp_near, wt, dense, extra)
     if dense:
         res, wres, disp_far = merged_residual(
-            route, index_far, recv_far, near_half[0], phi_far, base, wt
+            flags, index_far, recv_far, frame[0], phi_far, base, wt
         )
     else:
         res, wres = residual_of(phi_far, disp_far, base, wt)

time: 75 us -> 85.4 us (1.14)
  waiting for transfers between devices: 19.6 us -> 26.3 us
  local copies, waits for them, and re-layouts: 1.54 us -> 7.42 us
  starting transfers between devices: 23 us -> 20.7 us
    all_to_all x1, waiting for transfers between devices: 11.9 us -> 19.4 us  [shards(): recv = lax.all_to_all(send, 'cx', split_axis=0, concat_axis=0, tiled=True)]
    unnamed x22 -> x26, local copies, waits for them, and re-layouts: 1.24 us -> 6.24 us
    ppermute x7, starting transfers between devices: 10.8 us -> 9.02 us  [shards(): lax.ppermute(pieces[j], 'cx', [(i, i ^ j) for i in range(width)])]
    pallas_call x5 -> x4, Pallas kernels: 12 us -> 11.1 us  [the longest x1 5.89 us: near_harmonic(): pl.pallas_call(functools.partial(near_harmonic_kernel, dense=dense), in_s...]
  transfers between devices with their start and end apart: 13 -> 13, of which waited for: 3 -> 3; matrix products, arithmetic and copies ran while one was open for 5% -> 6% of each run, Pallas kernels for 26% -> 23%
where the time goes in v6:
time: 85.4 us; the launch traced here: 84.6 us
  waiting for transfers between devices  26.3 us (31%)
  Pallas kernels  25.5 us (30%)
  starting transfers between devices  20.7 us (24%)
  local copies, waits for them, and re-layouts  7.42 us (9%)
  other arithmetic  3.76 us (4%)
  between operations  0.89 us (1%)
    all_to_all x1, waiting for transfers between devices, shards(): recv = lax.all_to_all(send, 'cx', split_axis=0, concat_axis=0, tiled=True)  19.4 us
    ppermute x7, starting transfers between devices, shards(): lax.ppermute(pieces[j], 'cx', [(i, i ^ j) for i in range(width)])  9.02 us
    all_to_all x1, starting transfers between devices, shards(): recv = lax.all_to_all(send, 'cx', split_axis=0, concat_axis=0, tiled=True)  7.35 us
    unnamed x26, local copies, waits for them, and re-layouts  6.24 us
    ppermute x3, waiting for transfers between devices, swap_far(): return lax.ppermute(block, 'cx', pairs)  6.23 us
    pallas_call x1, Pallas kernels, near_harmonic(): pl.pallas_call(functools.partial(near_harmonic_kernel, dense=dense), in_s...  5.89 us
    pallas_call x1, Pallas kernels, near_gradient(): pl.pallas_call(near_gradient_kernel, in_specs=[in_smem()] + in_vmem(7), o...  5.61 us
    pallas_call x1, Pallas kernels, ordered(): pl.pallas_call(order_kernel, in_specs=[in_smem(), pl.BlockSpec(memory_spa...  4.2 us
  transfers between devices with their start and end apart: 13, of which 3 were waited for; matrix products, arithmetic and copies ran while one was open for 6% of the time, Pallas kernels for 23%

profile of v6, /device:TPU:1, one launch (start us, length us, event | category | flops | bytes accessed | tf_op | source)
XLA Modules:
  0.0 84.6 jit_solution(13873023022265709958)
XLA Ops:
  0.6 2.2 %shard_map.86.send_ref = bf16[16,15,16,128]{3,2,1,0:T(8,128)(2,1)} custom-call(bf16[3,16,5120]{2,1,0:T(8,128)(2,1)} %bitcast.5, bf16[3,16,5120]{2,1,0:T(8,128)(2,1)} %bitcast.6), custom_call_target="tpu_custom_call" | custom-call | bytes 1966080 | tf_op jit(solution)/shard_map/pallas_call | solution.py:98
  2.8 7.4 %all-to-all-start = ((bf16[16,15,16,128]{3,2,1,0:T(8,128)(2,1)}), bf16[16,15,16,128]{3,2,1,0:T(8,128)(2,1)S(1)}, u32[]{:S(2)}, u32[]{:S(2)}) async-start(bf16[16,15,16,128]{3,2,1,0:T(8,128)(2,1)} %shard_map.86.send_ref), calls=%async_computation | async-start | bytes 1966080 | tf_op jit(solution)/shard_map/all_to_all | solution.py:555
  10.2 0.7 add_select_fusion
  10.9 1.7 %collective-permute-start = (s32[5,64]{1,0:T(8,128)S(1)}, s32[5,64]{1,0:T(8,128)S(1)}, u32[]{:S(2)}, u32[]{:S(2)}) collective-permute-start(s32[5,64]{1,0:T(8,128)S(1)} %add_select_fusion), channel_id=1, source_target_pairs={{0,15},{1,2},{2,1},{3,4},{4,3},{5,6},{6,5},{7,8},{8,7},{9,10},{10,... | collective-permute-start | bytes 3848 | tf_op jit(solution)/shard_map/ppermute | solution.py:494
  12.6 0.1 reshape.92.index_ref.rest_1_
  12.8 19.4 %all-to-all-done.recv_ref.rest_2_ = bf16[16,15,16,128]{3,2,1,0:T(8,128)(2,1)S(1)} async-done(((bf16[16,15,16,128]{3,2,1,0:T(8,128)(2,1)}), bf16[16,15,16,128]{3,2,1,0:T(8,128)(2,1)S(1)}, u32[]{:S(2)}, u32[]{:S(2)}) %all-to-all-start) | async-done | bytes 983072 | tf_op jit(solution)/shard_map/all_to_all | solution.py:555
  32.2 0.1 broadcast_in_dim.96.flag_ref
  32.3 1.4 %shard_map.87 = (bf16[5,192,256]{2,1,0:T(8,128)(2,1)}, bf16[8,8,16,128]{3,2,1,0:T(8,128)(2,1)}) custom-call(s32[2,128]{1,0:T(2,128)S(1)} %broadcast_in_dim.96.flag_ref, s32[320,1]{1,0:T(8,128)S(1)} %reshape.92.index_ref.rest_1_, bf16[16,15,16,128]{3,2,1,0:T(8,128)(2,1)S(1)} %all-to-all-done.recv_ref.rest_2_), custom_call_target="tpu_custom_call" | custom-call | flops 157286400 | bytes 1474560 | tf_op jit(solution)/shard_map/pallas_call | solution.py:173
  33.7 0.7 fusion.7.route_ref.rest_0_
  34.4 2.4 %shard_map.88 = (bf16[8,16,128]{2,1,0:T(8,128)(2,1)}, bf16[8,16,128]{2,1,0:T(8,128)(2,1)}, bf16[8,16,128]{2,1,0:T(8,128)(2,1)}, bf16[8,16,128]{2,1,0:T(8,128)(2,...) custom-call(s32[4,8]{1,0:T(4,128)} %fusion.7.route_ref.rest_0_, ...), custom_call_target="tpu_custom_call" | custom-call | bytes 491520 | tf_op jit(solution)/shard_map/pallas_call | solution.py:203
  36.8 0.6 collective-permute-start.3
  37.4 1.6 %collective-permute-start.4 = (bf16[8,16,128]{2,1,0:T(8,128)(2,1)}, bf16[8,16,128]{2,1,0:T(8,128)(2,1)S(1)}, u32[]{:S(2)}, u32[]{:S(2)}) collective-permute-start(bf16[8,16,128]{2,1,0:T(8,128)(2,1)} %get-tuple-element.25), channel_id=1, source_target_pairs={{0,2},{1,3},{2,0},{3,1},{4,6},{5,7},{6,4},{7,5},{8,10},{9,11},{10,... | collective-permute-start | bytes 98312 | tf_op jit(solution)/shard_map/ppermute | solution.py:563
  39.0 0.1 collective-permute-start.5
  39.1 0.7 fusion.3
  39.8 0.0 collective-permute-done
  39.8 3.0 %collective-permute-start.6 = (bf16[8,16,128]{2,1,0:T(8,128)(2,1)}, bf16[8,16,128]{2,1,0:T(8,128)(2,1)S(1)}, u32[]{:S(2)}, u32[]{:S(2)}) collective-permute-start(bf16[8,16,128]{2,1,0:T(8,128)(2,1)} %get-tuple-element.27), channel_id=1, source_target_pairs={{0,4},{1,5},{2,6},{3,7},{4,0},{5,1},{6,2},{7,3},{8,12},{9,13},{10,... | collective-permute-start | bytes 98312 | tf_op jit(solution)/shard_map/ppermute | solution.py:563
  42.8 0.0 collective-permute-done.3.rest_4_
  42.8 0.6 copy-done.3
  43.4 1.3 %collective-permute-start.1 = (bf16[8,8,16,128]{3,2,1,0:T(8,128)(2,1)}, bf16[8,8,16,128]{3,2,1,0:T(8,128)(2,1)S(1)}, u32[]{:S(2)}, u32[]{:S(2)}) collective-permute-start(bf16[8,8,16,128]{3,2,1,0:T(8,128)(2,1)} %get-tuple-element.21), channel_id=1, source_target_pairs={{0,15},{1,2},{2,1},{3,4},{4,3},{5,6},{6,5},{7,8},{8,7},{9,10},{10,... | collective-permute-start | bytes 786440 | tf_op jit(solution)/shard_map/ppermute | solution.py:494
  44.8 0.9 %select_reduce_fusion = f32[256]{0:T(256)S(1)} fusion(f32[256]{0:T(256)} %param.13, s32[256]{0:T(256)} %param.12), kind=kLoop, calls=%fused_computation | loop fusion | flops 196352 | bytes 3072 | tf_op jit(solution)/shard_map/reduce_sum | solution.py:536
  45.6 0.0 collective-permute-done.4.rest_5_
  45.7 0.6 copy-done.5
  46.3 1.2 %collective-permute-start.7 = (bf16[8,16,128]{2,1,0:T(8,128)(2,1)}, bf16[8,16,128]{2,1,0:T(8,128)(2,1)}, u32[]{:S(2)}, u32[]{:S(2)}) collective-permute-start(bf16[8,16,128]{2,1,0:T(8,128)(2,1)} %get-tuple-element.28), channel_id=1, source_target_pairs={{0,5},{1,4},{2,7},{3,6},{4,1},{5,0},{6,3},{7,2},{8,13},{9,12},{10,... | collective-permute-start | bytes 98312 | tf_op jit(solution)/shard_map/ppermute | solution.py:563
  47.4 0.6 copy-done.7
  48.1 0.4 collective-permute-start.8
  48.5 0.0 collective-permute-done.6.rest_7_
  48.5 0.6 copy-done.9
  49.1 2.2 %collective-permute-start.9 = (bf16[8,16,128]{2,1,0:T(8,128)(2,1)}, bf16[8,16,128]{2,1,0:T(8,128)(2,1)}, u32[]{:S(2)}, u32[]{:S(2)}) collective-permute-start(bf16[8,16,128]{2,1,0:T(8,128)(2,1)} %get-tuple-element.30), channel_id=1, source_target_pairs={{0,7},{1,6},{2,5},{3,4},{4,3},{5,2},{6,1},{7,0},{8,15},{9,14},{10,... | collective-permute-start | bytes 98312 | tf_op jit(solution)/shard_map/ppermute | solution.py:563
  51.3 0.8 select_reduce_fusion.1.block_ref.table_ref
  52.0 4.2 %shard_map.90.phi_ref = bf16[5,192,960]{2,1,0:T(8,128)(2,1)} custom-call(s32[5,15]{1,0:T(8,128)} %select_reduce_fusion.1.block_ref.table_ref, bf16[5,14,192,192]{3,2,1,0:T(8,128)(2,1)} %phi_ref.3), custom_call_target="tpu_custom_call" | custom-call | bytes 5160960 | tf_op jit(solution)/shard_map/pallas_call | solution.py:239
  56.2 0.0 copy-start
  56.2 1.0 %reshape.91.index_ref = s32[320,1]{1,0:T(8,128)S(1)} reshape(s32[5,64]{1,0:T(8,128)} %copy-done.12) | data formatting | bytes 2560 | tf_op jit(solution)/shard_map/reshape | solution.py:559
  57.2 0.0 collective-permute-done.7.rest_8_
  57.2 0.0 collective-permute-done.9.rest_10_
  57.3 0.0 collective-permute-done.2.partner_ref.dnear
  57.3 0.7 copy-done.2
  58.0 0.8 copy-done.4
  58.8 0.8 copy-done.6
  59.6 0.8 copy-done.8
  60.3 0.8 copy-done.10
  61.1 5.9 %shard_map.89 = (f32[5,192,256]{2,1,0:T(8,128)S(1)}, bf16[5,192,256]{2,1,0:T(8,128)(2,1)S(1)}, bf16[8,8,16,128]{3,2,1,0:T(8,128)(2,1)S(1)}) custom-call(s32[5,15]{1,0:T(8,128)S(1)} %copy-done.1, bf16[5,14,192,192]{3,2,1,0:T(8,128)(2,1)} %phi_ref.3, bf16[5,192,256]{2,1,0:T(8,128)(2,1)} %get-tuple-element.22.own_ref.down, ...), custom_call_target="tpu_custom_call" | custom-call | flops 1321205760 | bytes 5160960 | tf_op jit(solution)/shard_map/pallas_call | solution.py:320
  67.0 1.3 %shard_map.91 = (bf16[5,192,256]{2,1,0:T(8,128)(2,1)S(1)}, bf16[5,192,256]{2,1,0:T(8,128)(2,1)S(1)}, bf16[5,192,256]{2,1,0:T(8,128)(2,1)S(1)}) custom-call(s32[2,128]{1,0:T(2,128)S(1)} %broadcast_in_dim.96.flag_ref, s32[320,1]{1,0:T(8,128)S(1)} %reshape.91.index_ref, bf16[8,8,16,128]{3,2,1,0:T(8,128)(2,1)S(1)} %collective-permute-done.1.recv_ref, ...), custom_call_target="tpu_custom_call" | custom-call | flops 555745280 | bytes 1843200 | tf_op jit(solution)/shard_map/pallas_call | solution.py:370
  68.3 0.3 collective-permute-start.10
  68.6 1.0 %collective-permute-start.11 = (bf16[5,192,256]{2,1,0:T(8,128)(2,1)S(1)}, bf16[5,192,256]{2,1,0:T(8,128)(2,1)S(1)}, u32[]{:S(2)}, u32[]{:S(2)}) collective-permute-start(bf16[5,192,256]{2,1,0:T(8,128)(2,1)S(1)} %get-tuple-element.36.rown), channel_id=1, source_target_pairs={{0,15},{1,2},{2,1},{3,4},{4,3},{5,6},{6,5},{7,8},{8,7},{9,10},{10,... | collective-permute-start | bytes 1474568 | tf_op jit(solution)/shard_map/ppermute | solution.py:494
  69.6 0.6 collective-permute-done.10.rnear
  70.2 5.6 %shard_map.92 = (bf16[5,14,192,192]{3,2,1,0:T(8,128)(2,1)}, bf16[5,192,256]{2,1,0:T(8,128)(2,1)}, f32[5,5,192,192]{3,2,1,0:T(8,128)S(1)}) custom-call(s32[5,15]{1,0:T(8,128)S(1)} %copy-done.1, bf16[5,192,256]{2,1,0:T(8,128)(2,1)S(1)} %get-tuple-element.33.wres_ref, bf16[5,192,256]{2,1,0:T(8,128)(2,1)S(1)} %get-tuple-element.34.wdisp_ref, ...), custom_call_target="tpu_custom_call" | custom-call | flops 2359296000 | bytes 3686400 | tf_op jit(solution)/shard_map/pallas_call | solution.py:458
  75.9 6.2 %collective-permute-done.11.rfar = bf16[5,192,256]{2,1,0:T(8,128)(2,1)S(1)} collective-permute-done((bf16[5,192,256]{2,1,0:T(8,128)(2,1)S(1)}, bf16[5,192,256]{2,1,0:T(8,128)(2,1)S(1)}, u32[]{:S(2)}, u32[]{:S(2)}) %collective-permute-start.11) | collective-permute-done | bytes 491552 | tf_op jit(solution)/shard_map/ppermute | solution.py:494
  82.1 2.5 %shard_map.93 = bf16[5,14,192,192]{3,2,1,0:T(8,128)(2,1)} custom-call(s32[5,15]{1,0:T(8,128)S(1)} %copy-done.1, bf16[5,192,256]{2,1,0:T(8,128)(2,1)S(1)} %get-tuple-element.34.wdisp_ref, bf16[5,192,256]{2,1,0:T(8,128)(2,1)S(1)} %collective-permute-done.11.rfar, f32[5,5,192,192]{3,2,1,0:T(8,128)S(1)} %get-tuple-element.38.far_ref, ...), custom_call_target="tpu_custom_call", output_to_operand_aliasing={{}: (4, {})} | custom-call | flops 471859200 | bytes 5529600 | tf_op jit(solution)/shard_map/pallas_call | solution.py:473
  (24 shorter events, 0.1 us)
Async XLA Ops:
  2.8 29.4 %all-to-all-start = ((bf16[16,15,16,128]{3,2,1,0:T(8,128)(2,1)}), bf16[16,15,16,128]{3,2,1,0:T(8,128)(2,1)S(1)}, u32[]{:S(2)}, u32[]{:S(2)}) async-start(bf16[16,15,16,128]{3,2,1,0:T(8,128)(2,1)} %shard_map.86.send_ref), calls=%async_computation | async-start | bytes 1966080 | tf_op jit(solution)/shard_map/all_to_all | solution.py:555
  10.9 28.9 %collective-permute-start = (s32[5,64]{1,0:T(8,128)S(1)}, s32[5,64]{1,0:T(8,128)S(1)}, u32[]{:S(2)}, u32[]{:S(2)}) collective-permute-start(s32[5,64]{1,0:T(8,128)S(1)} %add_select_fusion), channel_id=1, source_target_pairs={{0,15},{1,2},{2,1},{3,4},{4,3},{5,6},{6,5},{7,8},{8,7},{9,10},{10,... | collective-permute-start | bytes 3848 | tf_op jit(solution)/shard_map/ppermute | solution.py:494
  33.7 23.6 %collective-permute-start.2 = (bf16[5,192,256]{2,1,0:T(8,128)(2,1)}, bf16[5,192,256]{2,1,0:T(8,128)(2,1)}, u32[]{:S(2)}, u32[]{:S(2)}) collective-permute-start(bf16[5,192,256]{2,1,0:T(8,128)(2,1)} %get-tuple-element.22.own_ref.down), channel_id=1, source_target_pairs={{0,1},{1,0},{2,3},{3,2},{4,5},{5,4},{6,7},{7,6},{8,9},{9,8},{10,11... | collective-permute-start | bytes 1474568 | tf_op jit(solution)/shard_map/ppermute | solution.py:488
  34.4 22.9 %copy-start.11 = (s32[4,8]{1,0:T(4,128)S(1)}, s32[4,8]{1,0:T(4,128)}, u32[]{:S(2)}) copy-start(s32[4,8]{1,0:T(4,128)} %fusion.7.route_ref.rest_0_) | copy-start | bytes 388
  36.8 6.0 %collective-permute-start.3 = (bf16[8,16,128]{2,1,0:T(8,128)(2,1)}, bf16[8,16,128]{2,1,0:T(8,128)(2,1)S(1)}, u32[]{:S(2)}, u32[]{:S(2)}) collective-permute-start(bf16[8,16,128]{2,1,0:T(8,128)(2,1)} %get-tuple-element.24), channel_id=1, source_target_pairs={{0,1},{1,0},{2,3},{3,2},{4,5},{5,4},{6,7},{7,6},{8,9},{9,8},{10,11... | collective-permute-start | bytes 98312 | tf_op jit(solution)/shard_map/ppermute | solution.py:563
  37.4 8.3 %collective-permute-start.4 = (bf16[8,16,128]{2,1,0:T(8,128)(2,1)}, bf16[8,16,128]{2,1,0:T(8,128)(2,1)S(1)}, u32[]{:S(2)}, u32[]{:S(2)}) collective-permute-start(bf16[8,16,128]{2,1,0:T(8,128)(2,1)} %get-tuple-element.25), channel_id=1, source_target_pairs={{0,2},{1,3},{2,0},{3,1},{4,6},{5,7},{6,4},{7,5},{8,10},{9,11},{10,... | collective-permute-start | bytes 98312 | tf_op jit(solution)/shard_map/ppermute | solution.py:563
  39.0 8.5 %collective-permute-start.5 = (bf16[8,16,128]{2,1,0:T(8,128)(2,1)}, bf16[8,16,128]{2,1,0:T(8,128)(2,1)S(1)}, u32[]{:S(2)}, u32[]{:S(2)}) collective-permute-start(bf16[8,16,128]{2,1,0:T(8,128)(2,1)} %get-tuple-element.26), channel_id=1, source_target_pairs={{0,3},{1,2},{2,1},{3,0},{4,7},{5,6},{6,5},{7,4},{8,11},{9,10},{10,... | collective-permute-start | bytes 98312 | tf_op jit(solution)/shard_map/ppermute | solution.py:563
  39.8 3.0 %copy-start.12 = (s32[5,64]{1,0:T(8,128)}, s32[5,64]{1,0:T(8,128)S(1)}, u32[]{:S(2)}) copy-start(s32[5,64]{1,0:T(8,128)S(1)} %collective-permute-done) | copy-start | bytes 3844
  39.8 8.6 %collective-permute-start.6 = (bf16[8,16,128]{2,1,0:T(8,128)(2,1)}, bf16[8,16,128]{2,1,0:T(8,128)(2,1)S(1)}, u32[]{:S(2)}, u32[]{:S(2)}) collective-permute-start(bf16[8,16,128]{2,1,0:T(8,128)(2,1)} %get-tuple-element.27), channel_id=1, source_target_pairs={{0,4},{1,5},{2,6},{3,7},{4,0},{5,1},{6,2},{7,3},{8,12},{9,13},{10,... | collective-permute-start | bytes 98312 | tf_op jit(solution)/shard_map/ppermute | solution.py:563
  42.8 0.6 copy-start.3
  43.4 23.6 %collective-permute-start.1 = (bf16[8,8,16,128]{3,2,1,0:T(8,128)(2,1)}, bf16[8,8,16,128]{3,2,1,0:T(8,128)(2,1)S(1)}, u32[]{:S(2)}, u32[]{:S(2)}) collective-permute-start(bf16[8,8,16,128]{3,2,1,0:T(8,128)(2,1)} %get-tuple-element.21), channel_id=1, source_target_pairs={{0,15},{1,2},{2,1},{3,4},{4,3},{5,6},{6,5},{7,8},{8,7},{9,10},{10,... | collective-permute-start | bytes 786440 | tf_op jit(solution)/shard_map/ppermute | solution.py:494
  45.6 0.6 copy-start.5
  46.3 11.0 %collective-permute-start.7 = (bf16[8,16,128]{2,1,0:T(8,128)(2,1)}, bf16[8,16,128]{2,1,0:T(8,128)(2,1)}, u32[]{:S(2)}, u32[]{:S(2)}) collective-permute-start(bf16[8,16,128]{2,1,0:T(8,128)(2,1)} %get-tuple-element.28), channel_id=1, source_target_pairs={{0,5},{1,4},{2,7},{3,6},{4,1},{5,0},{6,3},{7,2},{8,13},{9,12},{10,... | collective-permute-start | bytes 98312 | tf_op jit(solution)/shard_map/ppermute | solution.py:563
  47.4 0.6 copy-start.7
  48.1 9.2 %collective-permute-start.8 = (bf16[8,16,128]{2,1,0:T(8,128)(2,1)}, bf16[8,16,128]{2,1,0:T(8,128)(2,1)}, u32[]{:S(2)}, u32[]{:S(2)}) collective-permute-start(bf16[8,16,128]{2,1,0:T(8,128)(2,1)} %get-tuple-element.29), channel_id=1, source_target_pairs={{0,6},{1,7},{2,4},{3,5},{4,2},{5,3},{6,0},{7,1},{8,14},{9,15},{10,... | collective-permute-start | bytes 98312 | tf_op jit(solution)/shard_map/ppermute | solution.py:563
  48.5 0.6 copy-start.9
  49.1 8.2 %collective-permute-start.9 = (bf16[8,16,128]{2,1,0:T(8,128)(2,1)}, bf16[8,16,128]{2,1,0:T(8,128)(2,1)}, u32[]{:S(2)}, u32[]{:S(2)}) collective-permute-start(bf16[8,16,128]{2,1,0:T(8,128)(2,1)} %get-tuple-element.30), channel_id=1, source_target_pairs={{0,7},{1,6},{2,5},{3,4},{4,3},{5,2},{6,1},{7,0},{8,15},{9,14},{10,... | collective-permute-start | bytes 98312 | tf_op jit(solution)/shard_map/ppermute | solution.py:563
  52.0 5.2 %copy-start.1 = (s32[5,15]{1,0:T(8,128)S(1)}, s32[5,15]{1,0:T(8,128)}, u32[]{:S(2)}) copy-start(s32[5,15]{1,0:T(8,128)} %select_reduce_fusion.1.block_ref.table_ref) | copy-start | bytes 904
  56.2 10.8 %copy-start = (bf16[5,192,960]{2,1,0:T(8,128)(2,1)S(1)}, bf16[5,192,960]{2,1,0:T(8,128)(2,1)}, u32[]{:S(2)}) copy-start(bf16[5,192,960]{2,1,0:T(8,128)(2,1)} %shard_map.90.phi_ref) | copy-start | bytes 5529604
  57.3 0.8 copy-start.2
  58.0 0.8 copy-start.4
  58.8 0.8 copy-start.6
  59.6 0.8 copy-start.8
  60.3 0.8 copy-start.10
  68.3 1.9 %collective-permute-start.10 = (bf16[5,192,256]{2,1,0:T(8,128)(2,1)S(1)}, bf16[5,192,256]{2,1,0:T(8,128)(2,1)S(1)}, u32[]{:S(2)}, u32[]{:S(2)}) collective-permute-start(bf16[5,192,256]{2,1,0:T(8,128)(2,1)S(1)} %get-tuple-element.36.rown), channel_id=1, source_target_pairs={{0,1},{1,0},{2,3},{3,2},{4,5},{5,4},{6,7},{7,6},{8,9},{9,8},{10,11... | collective-permute-start | bytes 1474568 | tf_op jit(solution)/shard_map/ppermute | solution.py:488
  68.6 13.5 %collective-permute-start.11 = (bf16[5,192,256]{2,1,0:T(8,128)(2,1)S(1)}, bf16[5,192,256]{2,1,0:T(8,128)(2,1)S(1)}, u32[]{:S(2)}, u32[]{:S(2)}) collective-permute-start(bf16[5,192,256]{2,1,0:T(8,128)(2,1)S(1)} %get-tuple-element.36.rown), channel_id=1, source_target_pairs={{0,15},{1,2},{2,1},{3,4},{4,3},{5,6},{6,5},{7,8},{8,7},{9,10},{10,... | collective-permute-start | bytes 1474568 | tf_op jit(solution)/shard_map/ppermute | solution.py:494
